TPU v7x, 32 devices: a whole 2x2x4 slice. The times are simulated.
32 devices in a mesh: gx: 4 (over y, x), gy: 4 (over z), gz: 2 (over core).
Axes of the slice: x: 2, y: 2, z: 4, core: 2. Of those that a mesh axis runs over, the one named last changes fastest.
Arguments:
- features: bfloat16 [4, 4, 4, 128, 128], P('gx', 'gy', 'gz'), may hold values from -6 to 6
- positions: int32 [3, 4, 4, 4, 128], P(None, 'gx', 'gy', 'gz'), may hold values from 0 to 63
- wavevectors: int32 [3, 1024], replicated, may hold values from -6 to 6
- radial_mix: bfloat16 [768, 128], replicated, may hold values from -0.0546875 to 0.0546875
- charge_weight: bfloat16 [128, 128], replicated, may hold values from -0.5 to 0.5
- filters: float32 [1024, 128], replicated, may hold values from 0.01 to 0.1
- mix_weight: float32 [128, 128], replicated, may hold values from -0.5 to 0.5
- norm_gain: float32 [128], replicated, may hold values from 0.1 to 1.9
- up_weight: bfloat16 [128, 256], replicated, may hold values from -0.5 to 0.5
- down_weight: bfloat16 [256, 128], replicated, may hold values from -0.375 to 0.375
Outputs:
- updated: bfloat16 [4, 4, 4, 128, 128], P('gx', 'gy', 'gz')
All inputs are finite; a program needn't handle non-finite values.
Results may differ from a plain program's by a relative error of at most 0.006.
Values may be sent and summed in bfloat16 or wider, within the bound.
No kernel may reach another device: no remote copies, remote signals or barrier semaphores. Data moves between devices by JAX's collectives and lax.ppermute only.
A program may use at most 64 MiB of HBM per device.

v0:
```python
import math

import jax
import jax.numpy as jnp
from jax import lax
from jax.sharding import PartitionSpec as P

NRBF = 6
GRID = 64


SHARP = 18.0
TWO_PI = 2.0 * math.pi
EPS = 1e-06
CONTRACT_FIRST = (((0,), (0,)), ((), ()))


def extended(array, sides, width):
    for axis, dim in sides:
        size, length = (lax.axis_size(axis), array.shape[dim])
        up = [(i, (i + 1) % size) for i in range(size)]
        down = [(j, i) for i, j in up]
        last = lax.slice_in_dim(array, length - width, length, axis=dim)
        first = lax.slice_in_dim(array, 0, width, axis=dim)
        before = lax.ppermute(last, axis, up)
        after = lax.ppermute(first, axis, down)
        array = jnp.concatenate([before, array, after], axis=dim)
    return array


def radial_basis(center, nearby_pos):
    tile_size = center.shape[1]
    offsets = (
        jnp.stack(
            [lax.broadcasted_iota(jnp.int32, (3, 3, 3, 1), component) for component in range(3)]
        )
        - 1
    )
    coords = (nearby_pos + offsets * GRID).reshape(3, 27 * tile_size)
    displace = coords[:, None, :] - center[:, :, None]
    square = jnp.sum(displace * displace, axis=0)
    scaled_dist = jnp.sqrt(square.astype(jnp.float32)) / GRID
    inside = (square > 0) & (square < GRID * GRID)
    envelope = jnp.where(inside, (1.0 - scaled_dist * scaled_dist) ** 2, 0.0)
    centres = (jnp.arange(NRBF, dtype=jnp.float32) + 0.5) / NRBF
    radial = (
        jnp.exp(-SHARP * (scaled_dist[:, None, :] - centres[None, :, None]) ** 2)
        * envelope[:, None, :]
    )
    return radial.astype(jnp.bfloat16)


def phase_tables(wavevectors, coords, lengths):
    fraction = jnp.zeros((wavevectors.shape[1], coords.shape[1]), jnp.float32)
    for component in range(3):
        product = jnp.mod(
            wavevectors[component][:, None] * coords[component][None, :], lengths[component]
        )
        fraction = fraction + product.astype(jnp.float32) / lengths[component]
    phase_angle = TWO_PI * fraction
    return (jnp.cos(phase_angle).astype(jnp.bfloat16), jnp.sin(phase_angle).astype(jnp.bfloat16))


def filter_mix(filters, factor, mix_weight):
    return jnp.dot(filters * factor, mix_weight, precision=lax.Precision.HIGHEST).astype(
        jnp.bfloat16
    )


def on_device(
    features,
    positions,
    wavevectors,
    radial_mix,
    charge_weight,
    filters,
    mix_weight,
    norm_gain,
    up_weight,
    down_weight,
):
    count_x, count_y, count_z, tile_size, feat_width = features.shape
    beside_all = extended(features, (("gx", 0), ("gy", 1), ("gz", 2)), 1)
    around_pos = extended(positions, (("gx", 1), ("gy", 2), ("gz", 3)), 1)
    anchor = jnp.zeros((), jnp.int32)

    def one_tile(flat_index):
        tile_x = flat_index // (count_y * count_z)
        tile_y = flat_index // count_z % count_y
        tile_z = flat_index % count_z
        neighbour = lax.dynamic_slice(
            beside_all, (tile_x, tile_y, tile_z, anchor, anchor), (3, 3, 3, tile_size, feat_width)
        )
        nearby_pos = lax.dynamic_slice(
            around_pos, (anchor, tile_x, tile_y, tile_z, anchor), (3, 3, 3, 3, tile_size)
        )
        center = lax.dynamic_slice(
            positions, (anchor, tile_x, tile_y, tile_z, anchor), (3, 1, 1, 1, tile_size)
        ).reshape(3, tile_size)
        radial = radial_basis(center, nearby_pos)
        pooled = jnp.einsum(
            "irj,jd->ird",
            radial,
            neighbour.reshape(27 * tile_size, feat_width),
            preferred_element_type=jnp.float32,
        )
        pooled = pooled.astype(jnp.bfloat16).reshape(tile_size, -1)
        return jnp.dot(pooled, radial_mix, preferred_element_type=jnp.float32)

    message = lax.map(one_tile, jnp.arange(count_x * count_y * count_z, dtype=jnp.int32))
    message = message.reshape(count_x * count_y * count_z * tile_size, feat_width)
    atom_count = count_x * count_y * count_z * tile_size
    counts = (count_x, count_y, count_z)
    axis_sizes = (lax.axis_size("gx"), lax.axis_size("gy"), lax.axis_size("gz"))
    axis_index = (lax.axis_index("gx"), lax.axis_index("gy"), lax.axis_index("gz"))
    lengths = tuple((counts[component] * axis_sizes[component] * GRID for component in range(3)))
    coords = jnp.stack(
        [
            (
                axis_index[component] * counts[component]
                + lax.broadcasted_iota(jnp.int32, (count_x, count_y, count_z, tile_size), component)
            )
            * GRID
            + positions[component]
            for component in range(3)
        ]
    ).reshape(3, atom_count)
    cos_table, sin_table = phase_tables(wavevectors, coords, lengths)
    charges = jnp.dot(
        features.reshape(atom_count, feat_width), charge_weight, preferred_element_type=jnp.float32
    ).astype(jnp.bfloat16)
    partial_cos = jnp.dot(cos_table, charges, preferred_element_type=jnp.float32)
    partial_sin = jnp.dot(sin_table, charges, preferred_element_type=jnp.float32)
    scale = 1.0 / math.sqrt(atom_count * axis_sizes[0] * axis_sizes[1] * axis_sizes[2])
    summed_cos, summed_sin = lax.psum((partial_cos, partial_sin), ("gx", "gy", "gz"))
    filtered_cos = filter_mix(filters, summed_cos * scale, mix_weight)
    filtered_sin = filter_mix(filters, summed_sin * scale, mix_weight)
    longrange = lax.dot_general(
        cos_table, filtered_cos, CONTRACT_FIRST, preferred_element_type=jnp.float32
    )
    longrange = longrange + lax.dot_general(
        sin_table, filtered_sin, CONTRACT_FIRST, preferred_element_type=jnp.float32
    )
    flat_sum = features.reshape(atom_count, feat_width).astype(jnp.float32) + message + longrange
    normed = (
        flat_sum
        * lax.rsqrt(jnp.mean(flat_sum * flat_sum, axis=-1, keepdims=True) + EPS)
        * norm_gain
    )
    hidden = jax.nn.silu(
        jnp.dot(normed.astype(jnp.bfloat16), up_weight, preferred_element_type=jnp.float32)
    ).astype(jnp.bfloat16)
    updated = flat_sum + jnp.dot(hidden, down_weight, preferred_element_type=jnp.float32)
    return updated.reshape(features.shape).astype(jnp.bfloat16)


def solution(mesh):
    in_specs = (
        P("gx", "gy", "gz", None, None),
        P(None, "gx", "gy", "gz", None),
        P(),
        P(),
        P(),
        P(),
        P(),
        P(),
        P(),
        P(),
    )
    out_specs = P("gx", "gy", "gz", None, None)
    return jax.shard_map(
        on_device, mesh=mesh, in_specs=in_specs, out_specs=out_specs, check_vma=False
    )
```

profile of v0, /device:TPU:0, one launch (start us, length us, event | category | flops | bytes accessed | tf_op | source)
XLA Modules:
  0.0 202.5 jit_solution(5004561161883564987)
XLA Ops:
  6.5 3.0 %collective-permute-start = (s32[3,1,1,2,128]{4,3,2,1,0:T(2,128)}, s32[3,1,1,2,128]{4,3,2,1,0:T(2,128)S(1)}, u32[]{:S(2)}, u32[]{:S(2)}) collective-permute-start(s32[3,1,1,2,128]{4,3,2,1,0:T(2,128)} %param.13), channel_id=1, source_target_pairs={{0,8},{8,16},{16,24},{24,0},{1,9},{9,17},{17,25},{25,1},{2,10},{10... | collective-permute-start | bytes 9224 | tf_op jit(solution)/shard_map/ppermute | solution.py:25
  9.5 1.0 collective-permute-start.1
  10.5 1.1 collective-permute-start.6
  11.5 1.9 collective-permute-start.7
  13.4 0.8 fusion.51
  14.2 1.0 convolution_convert_fusion.2
  15.2 0.8 add_bitcast_fusion.2
  16.0 6.4 %fusion.22 = f32[1024,128]{1,0:T(8,128)} fusion(bf16[256,128]{1,0:T(8,128)(2,1)S(1)} %convolution_convert_fusion.2, s32[256]{0:T(256)S(1)} %get-tuple-element.130, s32[1024]{0:T(1024)S(1)} %bitcast.63, s32[256]{0:T(256)S(1)} %get-tuple-element.131, s32[1024]{0:T(1024)S(1)} %bitcast.67, s32[256]{0:T(256)S(1)} %get-tuple-element.129, s32[1024]{0:T(1024)S(1)} %bitcast.59), kind=kOutput, calls=%fused_computation.57 | convolution fusion | flops 78381056 | bytes 605184 | tf_op jit(solution)/shard_map/dot_general | solution.py:132
  22.5 4.1 %collective-permute-start.3 = (s32[3,3,1,2,128]{4,3,2,1,0:T(2,128)S(1)}, s32[3,3,1,2,128]{4,3,2,1,0:T(2,128)S(1)}, u32[]{:S(2)}, u32[]{:S(2)}) collective-permute-start(s32[3,3,1,2,128]{4,3,2,1,0:T(2,128)S(1)} %constant_dynamic-update-slice_fusion), channel_id=1, source_target_pairs={{2,0},{4,2},{6,4},{0,6},{3,1},{5,3},{7,5},{1,7},{10,8},{12,10},{14... | collective-permute-start | bytes 27656 | tf_op jit(solution)/shard_map/ppermute | solution.py:26
  26.6 6.4 %fusion.20 = f32[1024,128]{1,0:T(8,128)} fusion(bf16[256,128]{1,0:T(8,128)(2,1)S(1)} %convolution_convert_fusion.2, s32[256]{0:T(256)S(1)} %get-tuple-element.130, s32[1024]{0:T(1024)S(1)} %bitcast.64, s32[256]{0:T(256)S(1)} %get-tuple-element.131, s32[1024]{0:T(1024)S(1)} %bitcast.68, s32[256]{0:T(256)S(1)} %get-tuple-element.129, s32[1024]{0:T(1024)S(1)} %bitcast.60), kind=kOutput, calls=%fused_computation.55 | convolution fusion | flops 78381056 | bytes 605184 | tf_op jit(solution)/shard_map/dot_general | solution.py:133
  33.2 3.9 %collective-permute-start.9 = (bf16[3,1,2,128,128]{4,3,2,1,0:T(8,128)(2,1)S(1)}, bf16[3,1,2,128,128]{4,3,2,1,0:T(8,128)(2,1)S(1)}, u32[]{:S(2)}, u32[]{:S(2)}) collective-permute-start(bf16[3,1,2,128,128]{4,3,2,1,0:T(8,128)(2,1)S(1)} %constant_dynamic-update-slice_fusion.3), channel_id=1, source_target_pairs={{2,0},{4,2},{6,4},{0,6},{3,1},{5,3},{7,5},{1,7},{10,8},{12,10},{14... | collective-permute-start | bytes 589832 | tf_op jit(solution)/shard_map/ppermute | solution.py:26
  37.2 0.5 collective-permute-start.4
  37.7 0.7 collective-permute-done.5
  38.6 3.9 %collective-permute-done.9 = bf16[3,1,2,128,128]{4,3,2,1,0:T(8,128)(2,1)S(1)} collective-permute-done((bf16[3,1,2,128,128]{4,3,2,1,0:T(8,128)(2,1)S(1)}, bf16[3,1,2,128,128]{4,3,2,1,0:T(8,128)(2,1)S(1)}, u32[]{:S(2)}, u32[]{:S(2)}) %collective-permute-start.9) | collective-permute-done | bytes 196640 | tf_op jit(solution)/shard_map/ppermute | solution.py:26
  42.5 3.1 %collective-permute-done.8 = bf16[3,1,2,128,128]{4,3,2,1,0:T(8,128)(2,1)S(1)} collective-permute-done((bf16[3,1,2,128,128]{4,3,2,1,0:T(8,128)(2,1)S(1)}, bf16[3,1,2,128,128]{4,3,2,1,0:T(8,128)(2,1)S(1)}, u32[]{:S(2)}, u32[]{:S(2)}) %collective-permute-start.8) | collective-permute-done | bytes 196640 | tf_op jit(solution)/shard_map/ppermute | solution.py:25
  45.8 0.5 collective-permute-start.10
  46.3 119.1 %all-reduce.3.cloned.1.call-done = (f32[1024,128]{1,0:T(8,128)}, f32[1024,128]{1,0:T(8,128)}) async-done(((f32[1024,128]{1,0:T(8,128)}, f32[1024,128]{1,0:T(8,128)}), (f32[1024,128]{1,0:T(8,128)}, f32[1024,128]{1,0:T(8,128)})) %all-reduce.3.cloned.1.call-update) | async-done | bytes 1048592 | tf_op jit(solution)/shard_map/psum | solution.py:135
  165.5 1.6 convolution_convert_fusion.1
  167.1 5.1 %fusion.21 = f32[256,128]{1,0:T(8,128)S(1)} fusion(bf16[1024,128]{1,0:T(8,128)(2,1)S(1)} %convolution_convert_fusion.1, s32[256]{0:T(256)S(1)} %get-tuple-element.130, s32[1024]{0:T(1024)S(1)} %bitcast.65, s32[256]{0:T(256)S(1)} %get-tuple-element.131, s32[1024]{0:T(1024)S(1)} %bitcast.69, s32[256]{0:T(256)S(1)} %get-tuple-element.129, s32[1024]{0:T(1024)S(1)} %bitcast.61), kind=kOutput, calls=%fused_computation.56 | convolution fusion | flops 78381056 | bytes 408576 | tf_op jit(solution)/shard_map/dot_general | solution.py:138
  172.3 1.3 convolution_convert_fusion
  173.7 15.5 %while.12 = (s32[]{:T(128)}, f32[2,128,128]{2,1,0:T(8,128)S(1)}, s32[2]{0:T(128)S(1)}, s32[3,3,3,4,128]{4,3,2,1,0:T(4,128)S(1)}, s32[3,1,1,2,128]{4,3,2,1,0:T(2,...) while((s32[]{:T(128)}, f32[2,128,128]{2,1,0:T(8,128)S(1)}, ...), condition=%wide.region_2.3_spmd, body=%wide.region_0.2_spmd.sunk | while | flops 725543424 | bytes 14143097 | solution.py:110
  173.9 0.6 dynamic_slice.38
  176.8 0.7 multiply_reduce_fusion.3
  177.5 0.9 sqrt_multiply_fusion.2
  178.4 2.9 %fusion.75 = bf16[128,6,128]{0,2,1:T(8,128)(2,1)S(1)} fusion(bf16[3456,128,1]{1,0,2:T(8,128)(2,1)S(1)} %bitcast.55, f32[128,3456]{1,0:T(8,128)S(1)} %get-tuple-element.179, f32[6]{0:T(128)S(1)} %add_multiply_fusion.3, f32[128,3456]{1,0:T(8,128)S(1)} %get-tuple-element.180), kind=kOutput, calls=%fused_computation.5.clone.1 | convolution fusion | flops 692846592 | bytes 4620312 | tf_op jit(solution)/shard_map/while/body/eval_jaxpr/irj,jd->ird/dot_general | solution.py:101
  181.3 0.3 fusion.76
  181.6 0.6 dynamic_slice.38
  184.5 0.7 multiply_reduce_fusion.3
  185.1 0.9 sqrt_multiply_fusion.2
  186.1 2.9 %fusion.75 = bf16[128,6,128]{0,2,1:T(8,128)(2,1)S(1)} fusion(bf16[3456,128,1]{1,0,2:T(8,128)(2,1)S(1)} %bitcast.55, f32[128,3456]{1,0:T(8,128)S(1)} %get-tuple-element.179, f32[6]{0:T(128)S(1)} %add_multiply_fusion.3, f32[128,3456]{1,0:T(8,128)S(1)} %get-tuple-element.180), kind=kOutput, calls=%fused_computation.5.clone.1 | convolution fusion | flops 692846592 | bytes 4620312 | tf_op jit(solution)/shard_map/while/body/eval_jaxpr/irj,jd->ird/dot_general | solution.py:101
  189.3 5.3 %multiply_reduce_fusion.1 = (f32[256]{0:T(256)S(1)}, f32[256,128]{1,0:T(8,128)S(1)}) fusion(f32[256,128]{1,0:T(8,128)S(1)} %bitcast_add_fusion, f32[256,128]{1,0:T(8,128)S(1)} %fusion.21, bf16[1024,128]{1,0:T(8,128)(2,1)S(1)} %copy-done.5, s32[256]{0:T(256)S(1)} %get-tuple-element.130, s32[1024]{0:T(1024)S(1)} %bitcast.66, s32[256]{0:T(256)S(1)} %get-tuple-element.131, ...), kind=kOutput, calls=%fused_computation.64 | convolution fusion | flops 78511872 | bytes 671744 | tf_op jit(solution)/shard_map/dot_general | solution.py:141
  194.6 1.0 fusion.6
  (73 shorter events, 1.6 us)
Async XLA Ops:
  6.5 158.9 %copy-start = (f32[128,128]{1,0:T(8,128)S(1)}, f32[128,128]{1,0:T(8,128)}, u32[]{:S(2)}) copy-start(f32[128,128]{1,0:T(8,128)} %param.18) | copy-start | bytes 196612
  6.5 158.9 %all-reduce.3.cloned.1.call-start = ((), (), s32[]{:S(2)}) async-start(), calls=%async_computation | async-start | bytes 2097152 | tf_op jit(solution)/shard_map/psum | solution.py:135
  6.5 15.9 %collective-permute-start = (s32[3,1,1,2,128]{4,3,2,1,0:T(2,128)}, s32[3,1,1,2,128]{4,3,2,1,0:T(2,128)S(1)}, u32[]{:S(2)}, u32[]{:S(2)}) collective-permute-start(s32[3,1,1,2,128]{4,3,2,1,0:T(2,128)} %param.13), channel_id=1, source_target_pairs={{0,8},{8,16},{16,24},{24,0},{1,9},{9,17},{17,25},{25,1},{2,10},{10... | collective-permute-start | bytes 9224 | tf_op jit(solution)/shard_map/ppermute | solution.py:25
  9.5 12.9 %collective-permute-start.1 = (s32[3,1,1,2,128]{4,3,2,1,0:T(2,128)}, s32[3,1,1,2,128]{4,3,2,1,0:T(2,128)S(1)}, u32[]{:S(2)}, u32[]{:S(2)}) collective-permute-start(s32[3,1,1,2,128]{4,3,2,1,0:T(2,128)} %param.13), channel_id=1, source_target_pairs={{8,0},{16,8},{24,16},{0,24},{9,1},{17,9},{25,17},{1,25},{10,2},{18... | collective-permute-start | bytes 9224 | tf_op jit(solution)/shard_map/ppermute | solution.py:26
  10.5 22.6 %collective-permute-start.6 = (bf16[1,1,2,128,128]{4,3,2,1,0:T(8,128)(2,1)}, bf16[1,1,2,128,128]{4,3,2,1,0:T(8,128)(2,1)S(1)}, u32[]{:S(2)}, u32[]{:S(2)}) collective-permute-start(bf16[1,1,2,128,128]{4,3,2,1,0:T(8,128)(2,1)} %param.12), channel_id=1, source_target_pairs={{0,8},{8,16},{16,24},{24,0},{1,9},{9,17},{17,25},{25,1},{2,10},{10... | collective-permute-start | bytes 196616 | tf_op jit(solution)/shard_map/ppermute | solution.py:25
  11.5 21.6 %collective-permute-start.7 = (bf16[1,1,2,128,128]{4,3,2,1,0:T(8,128)(2,1)}, bf16[1,1,2,128,128]{4,3,2,1,0:T(8,128)(2,1)S(1)}, u32[]{:S(2)}, u32[]{:S(2)}) collective-permute-start(bf16[1,1,2,128,128]{4,3,2,1,0:T(8,128)(2,1)} %param.12), channel_id=1, source_target_pairs={{8,0},{16,8},{24,16},{0,24},{9,1},{17,9},{25,17},{1,25},{10,2},{18... | collective-permute-start | bytes 196616 | tf_op jit(solution)/shard_map/ppermute | solution.py:26
  16.0 6.4 %copy-start.6 = (s32[3,1,1,2,128]{4,3,2,1,0:T(2,128)S(1)}, s32[3,1,1,2,128]{4,3,2,1,0:T(2,128)}, u32[]{:S(2)}) copy-start(s32[3,1,1,2,128]{4,3,2,1,0:T(2,128)} %param.13) | copy-start | bytes 9220
  22.5 10.7 %copy-start.3 = (bf16[1,1,2,128,128]{4,3,2,1,0:T(8,128)(2,1)S(1)}, bf16[1,1,2,128,128]{4,3,2,1,0:T(8,128)(2,1)}, u32[]{:S(2)}) copy-start(bf16[1,1,2,128,128]{4,3,2,1,0:T(8,128)(2,1)} %param.12) | copy-start | bytes 196612
  22.5 10.6 %collective-permute-start.3 = (s32[3,3,1,2,128]{4,3,2,1,0:T(2,128)S(1)}, s32[3,3,1,2,128]{4,3,2,1,0:T(2,128)S(1)}, u32[]{:S(2)}, u32[]{:S(2)}) collective-permute-start(s32[3,3,1,2,128]{4,3,2,1,0:T(2,128)S(1)} %constant_dynamic-update-slice_fusion), channel_id=1, source_target_pairs={{2,0},{4,2},{6,4},{0,6},{3,1},{5,3},{7,5},{1,7},{10,8},{12,10},{14... | collective-permute-start | bytes 27656 | tf_op jit(solution)/shard_map/ppermute | solution.py:26
  26.6 6.5 %collective-permute-start.2 = (s32[3,3,1,2,128]{4,3,2,1,0:T(2,128)S(1)}, s32[3,3,1,2,128]{4,3,2,1,0:T(2,128)S(1)}, u32[]{:S(2)}, u32[]{:S(2)}) collective-permute-start(s32[3,3,1,2,128]{4,3,2,1,0:T(2,128)S(1)} %constant_dynamic-update-slice_fusion), channel_id=1, source_target_pairs={{0,2},{2,4},{4,6},{6,0},{1,3},{3,5},{5,7},{7,1},{8,10},{10,12},{12... | collective-permute-start | bytes 27656 | tf_op jit(solution)/shard_map/ppermute | solution.py:25
  33.0 132.4 %copy-start.2 = (f32[1024,128]{1,0:T(8,128)S(1)}, f32[1024,128]{1,0:T(8,128)}, u32[]{:S(2)}) copy-start(f32[1024,128]{1,0:T(8,128)} %param.17) | copy-start | bytes 1572868
  33.2 9.3 %collective-permute-start.9 = (bf16[3,1,2,128,128]{4,3,2,1,0:T(8,128)(2,1)S(1)}, bf16[3,1,2,128,128]{4,3,2,1,0:T(8,128)(2,1)S(1)}, u32[]{:S(2)}, u32[]{:S(2)}) collective-permute-start(bf16[3,1,2,128,128]{4,3,2,1,0:T(8,128)(2,1)S(1)} %constant_dynamic-update-slice_fusion.3), channel_id=1, source_target_pairs={{2,0},{4,2},{6,4},{0,6},{3,1},{5,3},{7,5},{1,7},{10,8},{12,10},{14... | collective-permute-start | bytes 589832 | tf_op jit(solution)/shard_map/ppermute | solution.py:26
  37.1 8.6 %collective-permute-start.8 = (bf16[3,1,2,128,128]{4,3,2,1,0:T(8,128)(2,1)S(1)}, bf16[3,1,2,128,128]{4,3,2,1,0:T(8,128)(2,1)S(1)}, u32[]{:S(2)}, u32[]{:S(2)}) collective-permute-start(bf16[3,1,2,128,128]{4,3,2,1,0:T(8,128)(2,1)S(1)} %constant_dynamic-update-slice_fusion.3), channel_id=1, source_target_pairs={{0,2},{2,4},{4,6},{6,0},{1,3},{3,5},{5,7},{7,1},{8,10},{10,12},{12... | collective-permute-start | bytes 589832 | tf_op jit(solution)/shard_map/ppermute | solution.py:25
  37.1 1.2 collective-permute-start.5
  37.2 1.3 collective-permute-start.4
  45.8 127.8 %collective-permute-start.11 = (bf16[3,3,1,128,128]{4,3,2,1,0:T(8,128)(2,1)S(1)}, bf16[3,3,1,128,128]{4,3,2,1,0:T(8,128)(2,1)S(1)}, u32[]{:S(2)}, u32[]{:S(2)}) collective-permute-start(bf16[3,3,1,128,128]{4,3,2,1,0:T(8,128)(2,1)S(1)} %get-tuple-element.123), channel_id=1, source_target_pairs={{1,0},{0,1},{3,2},{2,3},{5,4},{4,5},{7,6},{6,7},{9,8},{8,9},{11,10... | collective-permute-start | bytes 884744 | tf_op jit(solution)/shard_map/ppermute | solution.py:26
  45.8 127.7 %collective-permute-start.10 = (bf16[3,3,1,128,128]{4,3,2,1,0:T(8,128)(2,1)S(1)}, bf16[3,3,1,128,128]{4,3,2,1,0:T(8,128)(2,1)S(1)}, u32[]{:S(2)}, u32[]{:S(2)}) collective-permute-start(bf16[3,3,1,128,128]{4,3,2,1,0:T(8,128)(2,1)S(1)} %get-tuple-element.122), channel_id=1, source_target_pairs={{0,1},{1,0},{2,3},{3,2},{4,5},{5,4},{6,7},{7,6},{8,9},{9,8},{10,11... | collective-permute-start | bytes 884744 | tf_op jit(solution)/shard_map/ppermute | solution.py:25
  167.1 5.2 %copy-start.4 = (f32[1024,128]{1,0:T(8,128)S(1)}, f32[1024,128]{1,0:T(8,128)}, u32[]{:S(2)}) copy-start(f32[1024,128]{1,0:T(8,128)} %get-tuple-element.119) | copy-start | bytes 1572868
  172.2 1.5 copy-start.1
  173.7 15.6 %copy-start.5 = (bf16[1024,128]{1,0:T(8,128)(2,1)S(1)}, bf16[1024,128]{1,0:T(8,128)(2,1)}, u32[]{:S(2)}) copy-start(bf16[1024,128]{1,0:T(8,128)(2,1)} %convolution_convert_fusion) | copy-start | bytes 786436
  189.3 5.3 %copy-start.7 = (bf16[256,128]{1,0:T(8,128)(2,1)S(1)}, bf16[256,128]{1,0:T(8,128)(2,1)}, u32[]{:S(2)}) copy-start(bf16[256,128]{1,0:T(8,128)(2,1)} %param.21) | copy-start | bytes 196612
  189.3 5.3 %copy-start.8 = (bf16[128,256]{1,0:T(8,128)(2,1)S(1)}, bf16[128,256]{1,0:T(8,128)(2,1)}, u32[]{:S(2)}) copy-start(bf16[128,256]{1,0:T(8,128)(2,1)} %param.20) | copy-start | bytes 196612
  189.3 5.3 %copy-start.9 = (f32[128]{0:T(128)S(1)}, f32[128]{0:T(128)}, u32[]{:S(2)}) copy-start(f32[128]{0:T(128)} %param.19) | copy-start | bytes 1540
Sparse Core Ops, SparseCore 0:
  33.2 132.2 all-reduce.2
where the time goes:
time: 203 us
  waiting for transfers between devices  127 us (63%)
  matrix products  34.5 us (17%)
  starting transfers between devices  16 us (8%)
  between operations  13.7 us (7%)
  other arithmetic  4.48 us (2%)
  loops' own time  4.29 us (2%)
  local copies, waits for them, and re-layouts  2.54 us (1%)
    psum x1, waiting for transfers between devices, on_device(): lax.psum((partial_cos, partial_sin), ('gx', 'gy', 'gz'))  119 us
    ppermute x6, starting transfers between devices, extended(): after = lax.ppermute(first, axis, down)  11 us
    dot_general x1, matrix products, on_device(): jnp.dot(sin_table, charges, preferred_element_type=jnp.float32)  6.43 us
    dot_general x1, matrix products, on_device(): jnp.dot(cos_table, charges, preferred_element_type=jnp.float32)  6.4 us
    dot_general x2, matrix products, one_tile(): jnp.einsum('irj,jd->ird', radial, neighbour.reshape(27 * tile_size, feat_...  5.84 us
    dot_general x1, matrix products, on_device(): lax.dot_general(sin_table, filtered_sin, CONTRACT_FIRST, preferred_elemen...  5.26 us
    dot_general x1, matrix products, on_device(): lax.dot_general(cos_table, filtered_cos, CONTRACT_FIRST, preferred_elemen...  5.13 us
    ppermute x6, starting transfers between devices, extended(): before = lax.ppermute(last, axis, up)  5.03 us
  transfers between devices with their start and end apart: 13, of which 5 were waited for; matrix products, arithmetic and copies ran while one was open for 12% of the time, Pallas kernels for 0%

commit v1 on v0

--- a/solution.py
+++ b/solution.py
@@ -1,8 +1,12 @@
+import functools
 import math
 
 import jax
 import jax.numpy as jnp
+import numpy as np
 from jax import lax
+from jax.experimental import pallas as pl
+from jax.experimental.pallas import tpu as pltpu
 from jax.sharding import PartitionSpec as P
 
 NRBF = 6
@@ -154,6 +158,367 @@
     return updated.reshape(features.shape).astype(jnp.bfloat16)
 
 
+LOG2E = 1.4426950408889634
+POS_ROWS = 16
+ROUND = 12582912.0
+
+
+def shift(array, axis, step):
+    size = lax.axis_size(axis)
+    return lax.ppermute(array, axis, [(i, (i + step) % size) for i in range(size)])
+
+
+def sin_coefficients():
+    nodes = np.cos((np.arange(400) + 0.5) / 400 * np.pi) * 0.25
+    powers = np.stack([nodes ** (2 * n + 1) for n in range(6)], axis=1)
+    scale = np.abs(powers).max(axis=0)
+    fit = np.linalg.lstsq(powers / scale, np.sin(2 * np.pi * nodes), rcond=None)[0] / scale
+    return [float(value) for value in fit]
+
+
+SIN_FIT = sin_coefficients()
+
+
+def sin_turns(u):
+    square = u * u
+    value = square * SIN_FIT[-1] + SIN_FIT[-2]
+    for coefficient in SIN_FIT[-3::-1]:
+        value = value * square + coefficient
+    return value * u
+
+
+def from_nearest(turns):
+    return turns - ((turns + ROUND) - ROUND)
+
+
+def table_kernel(n_blocks, z_tiles, place_ref, waves_ref, charge_ref, *refs):
+    z_size = len(refs) - 1 - n_blocks
+    columns, table_ref, parts = refs[:z_size], refs[z_size], refs[z_size + 1 :]
+    tile = columns[0].shape[2]
+    block = waves_ref.shape[1] // n_blocks
+    row = lax.broadcasted_iota(jnp.int32, (POS_ROWS, tile), 0)
+    coords, charges = [], []
+    for step in range(z_size):
+        for t in range(z_tiles):
+            pos = columns[step][t, tile : tile + POS_ROWS, :].astype(jnp.float32)
+            z = lax.rem(place_ref[2] + step, z_size) * z_tiles + t
+            pos = jnp.where(row == 3, place_ref[0].astype(jnp.float32), pos)
+            pos = jnp.where(row == 4, place_ref[1].astype(jnp.float32), pos)
+            pos = jnp.where(row == 5, z.astype(jnp.float32), pos)
+            coords.append(pos.astype(jnp.bfloat16))
+            charges.append(
+                jnp.dot(
+                    columns[step][t, :tile, :], charge_ref[...], preferred_element_type=jnp.float32
+                ).astype(jnp.bfloat16)
+            )
+    coords = jnp.concatenate(coords, axis=1)
+    charges = jnp.concatenate(charges, axis=0)
+    for n in range(n_blocks):
+        turns = lax.dot_general(
+            waves_ref[:, n * block : (n + 1) * block],
+            coords,
+            CONTRACT_FIRST,
+            preferred_element_type=jnp.float32,
+        )
+        cos_part = sin_turns(0.25 - jnp.abs(from_nearest(turns)))
+        sin_part = sin_turns(0.25 - jnp.abs(from_nearest(turns - 0.25)))
+        base = 2 * n * block
+        table_ref[base : base + block, :] = cos_part.astype(jnp.bfloat16)
+        table_ref[base + block : base + 2 * block, :] = sin_part.astype(jnp.bfloat16)
+        parts[n][...] = jnp.dot(
+            table_ref[base : base + 2 * block, :], charges, preferred_element_type=jnp.float32
+        ).astype(jnp.bfloat16)
+
+
+def add_kernel(*refs):
+    total = refs[0][...].astype(jnp.float32)
+    for ref in refs[1:-1]:
+        total = total + ref[...].astype(jnp.float32)
+    refs[-1][...] = total.astype(refs[-1].dtype)
+
+
+def mix_kernel(scale, place_ref, filters_ref, mix_ref, *refs):
+    total = refs[0][...].astype(jnp.float32)
+    for ref in refs[1:-1]:
+        total = total + ref[...].astype(jnp.float32)
+    both = jnp.concatenate([filters_ref[...], filters_ref[...]], axis=0)
+    refs[-1][...] = jnp.dot(
+        both * (total * scale),
+        mix_ref[...],
+        precision=lax.Precision.HIGHEST,
+        preferred_element_type=jnp.float32,
+    ).astype(jnp.bfloat16)
+
+
+def rows_of(row, values):
+    out = jnp.zeros(row.shape, jnp.float32)
+    for n, value in enumerate(values):
+        out = jnp.where(row == n, value, out)
+    return out.astype(jnp.bfloat16)
+
+
+def split_norm(x, y, z):
+    norm = x * x + y * y + z * z
+    high = jnp.floor(norm * 16.0) * 0.0625
+    return high, norm - high
+
+
+def radial_kernel(offsets, z_tiles, has_extra, *refs):
+    own_ref, before_ref, after_ref = refs[:3]
+    groups = refs[3 : 3 + len(offsets)]
+    mix_ref = refs[3 + len(offsets)]
+    extra_ref = refs[4 + len(offsets)] if has_extra else None
+    out_ref, radial_ref, feature_ref = refs[-3:]
+    tile = own_ref.shape[2]
+    row = lax.broadcasted_iota(jnp.int32, (POS_ROWS, tile), 0)
+    columns = [(g, c, dx, dy) for g, per in enumerate(offsets) for c, (dx, dy) in enumerate(per)]
+
+    def unit(ref_rows):
+        pos = ref_rows.astype(jnp.float32) * (1.0 / GRID)
+        return pos[0:1, :], pos[1:2, :], pos[2:3, :]
+
+    sources = {}
+    for slot, (g, c, dx, dy) in enumerate(columns):
+        for sz in range(z_tiles):
+            x, y, z = unit(groups[g][c, sz, tile : tile + POS_ROWS, :])
+            high, low = split_norm(x, y, z)
+            one = jnp.ones_like(x)
+            sources[slot, sz] = rows_of(row, [x, y, z, one, one, high, low])
+            feature_ref[sz, slot * tile : (slot + 1) * tile, :] = groups[g][c, sz, :tile, :]
+    targets = [(-1, before_ref, z_tiles - 1)]
+    targets += [(t, own_ref, t) for t in range(z_tiles)]
+    targets += [(z_tiles, after_ref, 0)]
+    for index, (tz, ref, at) in enumerate(targets):
+        x0, y0, z0 = unit(ref[at, tile : tile + POS_ROWS, :])
+        near = [sz for sz in range(z_tiles) if abs(sz - tz) <= 1]
+        pooled = [None] * NRBF
+        for place, sz in enumerate(near):
+            buffer = radial_ref.at[(index + place) % 2]
+            for slot, (g, c, dx, dy) in enumerate(columns):
+                x, y, z = x0 - dx, y0 - dy, z0 - (sz - tz)
+                high, low = split_norm(x, y, z)
+                one = jnp.ones_like(x)
+                target = rows_of(row, [-2 * x, -2 * y, -2 * z, high, low, one, one])
+                square = lax.dot_general(
+                    target, sources[slot, sz], CONTRACT_FIRST, preferred_element_type=jnp.float32
+                )
+                square = jnp.where(square == 0.0, 1.0, jnp.minimum(square, 1.0))
+                dist = square * lax.rsqrt(square)
+                lack = 1.0 - square
+                value = jnp.exp2(dist * (3.0 * LOG2E - (SHARP * LOG2E) * dist)) * (lack * lack)
+                growth = jnp.exp2(dist * (6.0 * LOG2E))
+                for r in range(NRBF):
+                    buffer[r * tile : (r + 1) * tile, slot * tile : (slot + 1) * tile] = (
+                        value.astype(jnp.bfloat16)
+                    )
+                    if r + 1 < NRBF:
+                        value = value * growth
+            part = jnp.dot(buffer[...], feature_ref[sz], preferred_element_type=jnp.float32)
+            for r in range(NRBF):
+                piece = part[r * tile : (r + 1) * tile, :]
+                pooled[r] = piece if pooled[r] is None else pooled[r] + piece
+        message = extra_ref[index] if has_extra else None
+        for r in range(NRBF):
+            level = math.exp(-SHARP * ((r + 0.5) / NRBF) ** 2)
+            part = jnp.dot(
+                (pooled[r] * level).astype(jnp.bfloat16),
+                mix_ref[r * tile : (r + 1) * tile, :],
+                preferred_element_type=jnp.float32,
+            )
+            message = part if message is None else message + part
+        out_ref[index] = message
+
+
+def long_kernel(z_tiles, n_blocks, table_ref, message_ref, *refs):
+    blocks, outs = refs[:n_blocks], refs[n_blocks:]
+    z_size, tile = len(outs), message_ref.shape[1]
+    filtered = jnp.concatenate([ref[...] for ref in blocks], axis=0)
+    flipped = lax.dot_general(
+        filtered, table_ref[...], CONTRACT_FIRST, preferred_element_type=jnp.float32
+    )
+    for step in range(z_size):
+        for t in range(z_tiles):
+            at = (step * z_tiles + t) * tile
+            value = flipped[:, at : at + tile].T
+            if step == 0:
+                value = value + message_ref[1 + t]
+            if step == (z_size - 1) % z_size and t == z_tiles - 1:
+                value = value + message_ref[0]
+            if step == 1 % z_size and t == 0:
+                value = value + message_ref[z_tiles + 1]
+            outs[step][t * tile : (t + 1) * tile, :] = value
+
+
+def node_kernel(features_ref, gain_ref, up_ref, down_ref, *refs):
+    total = features_ref[...].astype(jnp.float32)
+    for ref in refs[:-1]:
+        total = total + ref[...]
+    normed = (
+        total
+        * lax.rsqrt(jnp.mean(total * total, axis=-1, keepdims=True) + EPS)
+        * gain_ref[...]
+    )
+    inner = jnp.dot(normed.astype(jnp.bfloat16), up_ref[...], preferred_element_type=jnp.float32)
+    hidden = (inner / (1.0 + jnp.exp(-inner))).astype(jnp.bfloat16)
+    updated = total + jnp.dot(hidden, down_ref[...], preferred_element_type=jnp.float32)
+    refs[-1][...] = updated.astype(jnp.bfloat16)
+
+
+def call(kernel, out_shape, *args, scalars=0, scratch=(), blocks=None, name=None):
+    def whole(a):
+        return pl.BlockSpec(a.shape, lambda i, *s: (0,) * len(a.shape))
+
+    specs = [whole(a) for a in args[scalars:]]
+    for at, spec in (blocks or {}).items():
+        specs[at] = spec
+    single = not isinstance(out_shape, (list, tuple))
+    outs = whole(out_shape) if single else [whole(o) for o in out_shape]
+    return pl.pallas_call(
+        kernel,
+        out_shape=out_shape,
+        grid_spec=pltpu.PrefetchScalarGridSpec(
+            num_scalar_prefetch=scalars,
+            grid=(1,),
+            in_specs=specs,
+            out_specs=outs,
+            scratch_shapes=list(scratch),
+        ),
+        name=name,
+    )(*args)
+
+
+def fast_device(
+    features,
+    positions,
+    wavevectors,
+    radial_mix,
+    charge_weight,
+    filters,
+    mix_weight,
+    norm_gain,
+    up_weight,
+    down_weight,
+):
+    z_tiles, tile, width = features.shape[2:]
+    sizes = tuple(lax.axis_size(axis) for axis in ("gx", "gy", "gz"))
+    place = jnp.stack([lax.axis_index(axis) for axis in ("gx", "gy", "gz")]).astype(jnp.int32)
+    counts = (sizes[0], sizes[1], sizes[2] * z_tiles)
+    n_blocks, waves = sizes[0], wavevectors.shape[1] // sizes[2]
+    block = waves // n_blocks
+    atoms = z_tiles * tile
+    shape = jax.ShapeDtypeStruct
+
+    pos = jnp.moveaxis(positions.reshape(3, z_tiles, tile), 0, 1).astype(jnp.bfloat16)
+    payload = jnp.concatenate(
+        [
+            features.reshape(z_tiles, tile, width),
+            jnp.pad(pos, ((0, 0), (0, POS_ROWS - 3), (0, 0))),
+        ],
+        axis=1,
+    )
+    column = [payload] + [shift(payload, "gz", -step) for step in range(1, sizes[2])]
+    south, north = shift(payload, "gy", 1), shift(payload, "gy", -1)
+    middle = jnp.stack([south, payload, north])
+
+    mine = lax.dynamic_slice_in_dim(wavevectors, place[2] * waves, waves, axis=1)
+    mine = jnp.concatenate([mine, mine], axis=1)
+    mine = lax.dynamic_slice_in_dim(mine, place[0] * block, waves, axis=1).astype(jnp.float32)
+    fine = jnp.array([1.0 / (count * GRID) for count in counts], jnp.float32)[:, None]
+    coarse = jnp.array([1.0 / count for count in counts], jnp.float32)[:, None]
+    mine = jnp.concatenate([mine * fine, mine * coarse], axis=0)
+    mine = jnp.pad(mine, ((0, POS_ROWS - 6), (0, 0))).astype(jnp.bfloat16)
+
+    table, *parts = call(
+        functools.partial(table_kernel, n_blocks, z_tiles),
+        [shape((2 * waves, sizes[2] * atoms), jnp.bfloat16)]
+        + [shape((2 * block, width), jnp.bfloat16)] * n_blocks,
+        place,
+        mine,
+        charge_weight,
+        *column,
+        scalars=1,
+        name="tables",
+    )
+    arrived = [parts[0]] + [shift(parts[n], "gx", n) for n in range(1, n_blocks)]
+    west, east = shift(middle, "gx", 1), shift(middle, "gx", -1)
+    line = call(add_kernel, shape((2 * block, width), jnp.bfloat16), *arrived, name="add_line")
+    lines = [line] + [shift(line, "gy", n) for n in range(1, sizes[1])]
+
+    ring = [(dx, dy) for dx in (-1, 0, 1) for dy in (-1, 0, 1)]
+    targets = z_tiles + 2
+    before, after = column[-1], column[1 % sizes[2]]
+
+    def messages(sources, offsets, extra, name):
+        n_columns = sum(len(o) for o in offsets)
+        extras = [] if extra is None else [extra]
+        return call(
+            functools.partial(radial_kernel, offsets, z_tiles, extra is not None),
+            shape((targets, tile, width), jnp.float32),
+            payload,
+            before,
+            after,
+            *sources,
+            radial_mix,
+            *extras,
+            scratch=[
+                pltpu.VMEM((2, NRBF * tile, n_columns * tile), jnp.bfloat16),
+                pltpu.VMEM((z_tiles, n_columns * tile, width), jnp.bfloat16),
+            ],
+            name=name,
+        )
+
+    message = messages([middle], [ring[3:6]], None, "radial_near")
+    scale = 1.0 / math.sqrt(atoms * sizes[0] * sizes[1] * sizes[2])
+    spot = (place[2] * n_blocks + place[0]).reshape(1)
+    filtered = call(
+        functools.partial(mix_kernel, scale),
+        shape((2 * block, width), jnp.bfloat16),
+        spot,
+        filters,
+        mix_weight,
+        *lines,
+        scalars=1,
+        blocks={0: pl.BlockSpec((block, width), lambda i, s: (s[0], 0))},
+        name="mix",
+    )
+    blocks = [filtered] + [shift(filtered, "gx", -n) for n in range(1, n_blocks)]
+    message = messages([west, east], [ring[:3], ring[6:]], message, "radial_far")
+    sums = call(
+        functools.partial(long_kernel, z_tiles, n_blocks),
+        [shape((atoms, width), jnp.float32)] * sizes[2],
+        table,
+        message,
+        *blocks,
+        name="longrange",
+    )
+    sums = [sums[0]] + [shift(sums[step], "gz", step) for step in range(1, sizes[2])]
+    updated = call(
+        node_kernel,
+        shape((atoms, width), jnp.bfloat16),
+        features.reshape(atoms, width),
+        norm_gain.reshape(1, width),
+        up_weight,
+        down_weight,
+        *sums,
+        name="node",
+    )
+    return updated.reshape(features.shape)
+
+
+def fits(mesh, features, wavevectors):
+    count_x, count_y, count_z, tile, width = features
+    per = mesh.shape["gx"] * mesh.shape["gz"]
+    lengths = [n * GRID for n in (count_x, count_y, count_z)]
+    return (
+        count_x == mesh.shape["gx"]
+        and count_y == mesh.shape["gy"]
+        and tile == 128
+        and width == 128
+        and wavevectors[1] % (16 * per) == 0
+        and all(n & (n - 1) == 0 and n <= 2**14 for n in lengths)
+    )
+
+
 def solution(mesh):
     in_specs = (
         P("gx", "gy", "gz", None, None),
@@ -168,6 +533,11 @@
         P(),
     )
     out_specs = P("gx", "gy", "gz", None, None)
-    return jax.shard_map(
-        on_device, mesh=mesh, in_specs=in_specs, out_specs=out_specs, check_vma=False
-    )
+
+    def layer(*args):
+        body = fast_device if fits(mesh, args[0].shape, args[2].shape) else on_device
+        return jax.shard_map(
+            body, mesh=mesh, in_specs=in_specs, out_specs=out_specs, check_vma=False
+        )(*args)
+
+    return layer

time: 203 us -> 66.7 us (0.33)
  waiting for transfers between devices: 127 us -> 16.5 us
  matrix products: 34.5 us -> 0 us
  Pallas kernels: 0 us -> 25 us
  between operations: 13.7 us -> 0.11 us
  loops' own time: 4.29 us -> 0 us
  local copies, waits for them, and re-layouts: 2.54 us -> 4.59 us
    psum x1 -> x0, waiting for transfers between devices: 119 us -> none  [on_device(): lax.psum((partial_cos, partial_sin), ('gx', 'gy', 'gz'))]
    dot_general x12 -> x0, matrix products: 34.5 us -> none  [the longest x1 6.43 us: on_device(): jnp.dot(sin_table, charges, preferred_element_type=jnp.float32)]
    pallas_call x0 -> x7, Pallas kernels: none -> 25 us  [call(): pl.pallas_call(kernel, out_shape=out_shape, grid_spec=pltpu.PrefetchScala...]
    ppermute x12 -> x15, waiting for transfers between devices: 7.94 us -> 16.5 us  [shift(): lax.ppermute(array, axis, [(i, (i + step) % size) for i in range(size)])]
    unnamed x24 -> x32, local copies, waits for them, and re-layouts: 0.08 us -> 4.58 us
    another operation x1 -> x0, loops' own time: 4.29 us -> none  [on_device(): lax.map(one_tile, jnp.arange(count_x * count_y * count_z, dtype=jnp.int32))]
    ppermute x12 -> x15, starting transfers between devices: 16 us -> 17.1 us  [shift(): lax.ppermute(array, axis, [(i, (i + step) % size) for i in range(size)])]
  transfers between devices with their start and end apart: 13 -> 15, of which waited for: 5 -> 9; matrix products, arithmetic and copies ran while one was open for 12% -> 2% of each run, Pallas kernels for 0% -> 31%
where the time goes in v1:
time: 66.7 us; the launch traced here: 66.2 us
  Pallas kernels  25 us (37%)
  starting transfers between devices  17.1 us (26%)
  waiting for transfers between devices  16.5 us (25%)
  local copies, waits for them, and re-layouts  4.59 us (7%)
  other arithmetic  2.89 us (4%)
    pallas_call x7, Pallas kernels, call(): pl.pallas_call(kernel, out_shape=out_shape, grid_spec=pltpu.PrefetchScala...  25 us
    ppermute x15, starting transfers between devices, shift(): lax.ppermute(array, axis, [(i, (i + step) % size) for i in range(size)])  17.1 us
    ppermute x15, waiting for transfers between devices, shift(): lax.ppermute(array, axis, [(i, (i + step) % size) for i in range(size)])  16.5 us
    unnamed x32, local copies, waits for them, and re-layouts  4.58 us
  transfers between devices with their start and end apart: 15, of which 9 were waited for; matrix products, arithmetic and copies ran while one was open for 2% of the time, Pallas kernels for 31%

profile of v1, /device:TPU:0, one launch (start us, length us, event | category | flops | bytes accessed | tf_op | source)
XLA Modules:
  0.0 66.2 jit_solution(7001856612296519468)
XLA Ops:
  0.0 0.7 %fusion.7 = bf16[2,3,128]{2,1,0:T(4,128)(2,1)S(1)} fusion(s32[3,1,1,2,128]{4,3,2,1,0:T(2,128)} %param.13), kind=kLoop, calls=%fused_computation.15 | loop fusion | flops 768 | bytes 4608 | tf_op jit(solution)/shard_map/convert_element_type | solution.py:411
  0.7 0.9 %fusion.8 = (bf16[1,2,144,128]{3,2,1,0:T(8,128)(2,1)S(1)}, bf16[2,144,128]{2,1,0:T(8,128)(2,1)S(1)}) fusion(bf16[2,3,128]{2,1,0:T(4,128)(2,1)S(1)} %fusion.7, bf16[2,128,128]{2,1,0:T(8,128)(2,1)} %bitcast.16), kind=kLoop, calls=%fused_computation.18 | loop fusion | flops 221184 | bytes 214528 | tf_op jit(solution)/shard_map/stack | solution.py:421
  1.6 5.1 %collective-permute-start.2 = (bf16[2,144,128]{2,1,0:T(8,128)(2,1)S(1)}, bf16[2,144,128]{2,1,0:T(8,128)(2,1)S(1)}, u32[]{:S(2)}, u32[]{:S(2)}) collective-permute-start(bf16[2,144,128]{2,1,0:T(8,128)(2,1)S(1)} %get-tuple-element.20.refs_0_), channel_id=1, source_target_pairs={{0,6},{2,0},{4,2},{6,4},{1,7},{3,1},{5,3},{7,5},{8,14},{10,8},{12,... | collective-permute-start | bytes 221192 | tf_op jit(solution)/shard_map/ppermute | solution.py:168
  7.4 1.6 %collective-permute-done.2 = bf16[2,144,128]{2,1,0:T(8,128)(2,1)S(1)} collective-permute-done((bf16[2,144,128]{2,1,0:T(8,128)(2,1)S(1)}, bf16[2,144,128]{2,1,0:T(8,128)(2,1)S(1)}, u32[]{:S(2)}, u32[]{:S(2)}) %collective-permute-start.2) | collective-permute-done | bytes 73760 | tf_op jit(solution)/shard_map/ppermute | solution.py:168
  9.0 3.8 %collective-permute-done.1 = bf16[2,144,128]{2,1,0:T(8,128)(2,1)S(1)} collective-permute-done((bf16[2,144,128]{2,1,0:T(8,128)(2,1)S(1)}, bf16[2,144,128]{2,1,0:T(8,128)(2,1)S(1)}, u32[]{:S(2)}, u32[]{:S(2)}) %collective-permute-start.1) | collective-permute-done | bytes 73760 | tf_op jit(solution)/shard_map/ppermute | solution.py:168
  12.9 2.5 %collective-permute-start.4 = (bf16[3,2,144,128]{3,2,1,0:T(8,128)(2,1)S(1)}, bf16[3,2,144,128]{3,2,1,0:T(8,128)(2,1)S(1)}, u32[]{:S(2)}, u32[]{:S(2)}) collective-permute-start(bf16[3,2,144,128]{3,2,1,0:T(8,128)(2,1)S(1)} %pad_maximum_fusion.refs_3_), channel_id=1, source_target_pairs={{0,24},{8,0},{16,8},{24,16},{1,25},{9,1},{17,9},{25,17},{2,26},{10... | collective-permute-start | bytes 663560 | tf_op jit(solution)/shard_map/ppermute | solution.py:168
  15.4 0.7 %pad_add_fusion.place_ref = s32[3]{0:T(128)} fusion(s32[1]{0:T(128)} %bitcast.4, s32[1]{0:T(128)} %bitcast.3, s32[1]{0:T(128)} %bitcast.2), kind=kLoop, calls=%fused_computation.17 | loop fusion | flops 6 | bytes 24 | tf_op jit(solution)/shard_map/stack | solution.py:404
  16.1 0.6 copy-done.1
  16.7 4.6 %tables.1 = (bf16[1024,512]{1,0:T(8,128)(2,1)}, bf16[256,128]{1,0:T(8,128)(2,1)}, bf16[256,128]{1,0:T(8,128)(2,1)}, bf16[256,128]{1,0:T(8,128)(2,1)}, bf16[256,128]{1,0:T(8,128)(2,1)}) custom-call(s32[3]{0:T(128)} %pad_add_fusion.place_ref, bf16[16,512]{1,0:T(8,128)(2,1)} %fusion.4.waves_ref, bf16[128,128]{1,0:T(8,128)(2,1)} %charge_ref.1, ...), custom_call_target="tpu_custom_call" | custom-call | tf_op jit(solution)/shard_map/tables/pallas_call | solution.py:376
  21.3 2.0 %collective-permute-start.5 = (bf16[256,128]{1,0:T(8,128)(2,1)}, bf16[256,128]{1,0:T(8,128)(2,1)S(1)}, u32[]{:S(2)}, u32[]{:S(2)}) collective-permute-start(bf16[256,128]{1,0:T(8,128)(2,1)} %get-tuple-element.14), channel_id=1, source_target_pairs={{0,8},{8,16},{16,24},{24,0},{1,9},{9,17},{17,25},{25,1},{2,10},{10... | collective-permute-start | bytes 196616 | tf_op jit(solution)/shard_map/ppermute | solution.py:168
  23.2 1.5 %collective-permute-start.6 = (bf16[256,128]{1,0:T(8,128)(2,1)}, bf16[256,128]{1,0:T(8,128)(2,1)S(1)}, u32[]{:S(2)}, u32[]{:S(2)}) collective-permute-start(bf16[256,128]{1,0:T(8,128)(2,1)} %get-tuple-element.15), channel_id=1, source_target_pairs={{0,16},{8,24},{16,0},{24,8},{1,17},{9,25},{17,1},{25,9},{2,18},{10... | collective-permute-start | bytes 196616 | tf_op jit(solution)/shard_map/ppermute | solution.py:168
  25.3 1.4 %collective-permute-done.5.refs_1_ = bf16[256,128]{1,0:T(8,128)(2,1)S(1)} collective-permute-done((bf16[256,128]{1,0:T(8,128)(2,1)}, bf16[256,128]{1,0:T(8,128)(2,1)S(1)}, u32[]{:S(2)}, u32[]{:S(2)}) %collective-permute-start.5) | collective-permute-done | bytes 65568 | tf_op jit(solution)/shard_map/ppermute | solution.py:168
  26.6 1.1 %collective-permute-done.6.refs_2_ = bf16[256,128]{1,0:T(8,128)(2,1)S(1)} collective-permute-done((bf16[256,128]{1,0:T(8,128)(2,1)}, bf16[256,128]{1,0:T(8,128)(2,1)S(1)}, u32[]{:S(2)}, u32[]{:S(2)}) %collective-permute-start.6) | collective-permute-done | bytes 65568 | tf_op jit(solution)/shard_map/ppermute | solution.py:168
  27.7 1.5 %collective-permute-done.7.refs_3_ = bf16[256,128]{1,0:T(8,128)(2,1)S(1)} collective-permute-done((bf16[256,128]{1,0:T(8,128)(2,1)}, bf16[256,128]{1,0:T(8,128)(2,1)S(1)}, u32[]{:S(2)}, u32[]{:S(2)}) %collective-permute-start.7) | collective-permute-done | bytes 65568 | tf_op jit(solution)/shard_map/ppermute | solution.py:168
  29.8 1.6 %add_line.1.refs_0_ = bf16[256,128]{1,0:T(8,128)(2,1)} custom-call(bf16[256,128]{1,0:T(8,128)(2,1)} %get-tuple-element.13.refs_0_, bf16[256,128]{1,0:T(8,128)(2,1)} %copy-done.11, bf16[256,128]{1,0:T(8,128)(2,1)} %copy-done.13, bf16[256,128]{1,0:T(8,128)(2,1)} %copy-done.15), custom_call_target="tpu_custom_call" | custom-call | tf_op jit(solution)/shard_map/add_line/pallas_call | solution.py:376
  32.3 1.1 %collective-permute-start.8 = (bf16[256,128]{1,0:T(8,128)(2,1)}, bf16[256,128]{1,0:T(8,128)(2,1)S(1)}, u32[]{:S(2)}, u32[]{:S(2)}) collective-permute-start(bf16[256,128]{1,0:T(8,128)(2,1)} %add_line.1.refs_0_), channel_id=1, source_target_pairs={{0,2},{2,4},{4,6},{6,0},{1,3},{3,5},{5,7},{7,1},{8,10},{10,12},{12... | collective-permute-start | bytes 196616 | tf_op jit(solution)/shard_map/ppermute | solution.py:168
  33.5 2.4 %collective-permute-done.10.refs_3_ = bf16[256,128]{1,0:T(8,128)(2,1)S(1)} collective-permute-done((bf16[256,128]{1,0:T(8,128)(2,1)}, bf16[256,128]{1,0:T(8,128)(2,1)S(1)}, u32[]{:S(2)}, u32[]{:S(2)}) %collective-permute-start.10) | collective-permute-done | bytes 65568 | tf_op jit(solution)/shard_map/ppermute | solution.py:168
  35.9 1.4 %collective-permute-done.9.refs_2_ = bf16[256,128]{1,0:T(8,128)(2,1)S(1)} collective-permute-done((bf16[256,128]{1,0:T(8,128)(2,1)}, bf16[256,128]{1,0:T(8,128)(2,1)S(1)}, u32[]{:S(2)}, u32[]{:S(2)}) %collective-permute-start.9) | collective-permute-done | bytes 65568 | tf_op jit(solution)/shard_map/ppermute | solution.py:168
  37.3 1.7 %collective-permute-done.8.refs_1_ = bf16[256,128]{1,0:T(8,128)(2,1)S(1)} collective-permute-done((bf16[256,128]{1,0:T(8,128)(2,1)}, bf16[256,128]{1,0:T(8,128)(2,1)S(1)}, u32[]{:S(2)}, u32[]{:S(2)}) %collective-permute-start.8) | collective-permute-done | bytes 65568 | tf_op jit(solution)/shard_map/ppermute | solution.py:168
  39.0 0.6 copy-done.14
  39.6 1.9 %mix.1.refs_0_ = bf16[256,128]{1,0:T(8,128)(2,1)} custom-call(s32[1]{0:T(128)} %bitcast.11.place_ref, f32[1024,128]{1,0:T(8,128)} %filters_ref.1, f32[128,128]{1,0:T(8,128)} %mix_ref.1, bf16[256,128]{1,0:T(8,128)(2,1)} %add_line.1.refs_0_, bf16[256,128]{1,0:T(8,128)(2,1)} %copy-done.14, bf16[256,128]{1,0:T(8,128)(2,1)} %copy-done.12, bf16[256,128]{1,0:T(8,128)(2,1)} %copy-done.10), custom_call_target="tpu_custom_call" | custom-call | tf_op jit(solution)/shard_map/mix/pallas_call | solution.py:376
  41.5 1.0 %collective-permute-start.13 = (bf16[256,128]{1,0:T(8,128)(2,1)}, bf16[256,128]{1,0:T(8,128)(2,1)S(1)}, u32[]{:S(2)}, u32[]{:S(2)}) collective-permute-start(bf16[256,128]{1,0:T(8,128)(2,1)} %mix.1.refs_0_), channel_id=1, source_target_pairs={{0,8},{8,16},{16,24},{24,0},{1,9},{9,17},{17,25},{25,1},{2,10},{10... | collective-permute-start | bytes 196616 | tf_op jit(solution)/shard_map/ppermute | solution.py:168
  42.5 1.0 %collective-permute-start.12 = (bf16[256,128]{1,0:T(8,128)(2,1)}, bf16[256,128]{1,0:T(8,128)(2,1)S(1)}, u32[]{:S(2)}, u32[]{:S(2)}) collective-permute-start(bf16[256,128]{1,0:T(8,128)(2,1)} %mix.1.refs_0_), channel_id=1, source_target_pairs={{0,16},{8,24},{16,0},{24,8},{1,17},{9,25},{17,1},{25,9},{2,18},{10... | collective-permute-start | bytes 196616 | tf_op jit(solution)/shard_map/ppermute | solution.py:168
  43.5 1.4 %collective-permute-start.11 = (bf16[256,128]{1,0:T(8,128)(2,1)}, bf16[256,128]{1,0:T(8,128)(2,1)S(1)}, u32[]{:S(2)}, u32[]{:S(2)}) collective-permute-start(bf16[256,128]{1,0:T(8,128)(2,1)} %mix.1.refs_0_), channel_id=1, source_target_pairs={{0,24},{8,0},{16,8},{24,16},{1,25},{9,1},{17,9},{25,17},{2,26},{10... | collective-permute-start | bytes 196616 | tf_op jit(solution)/shard_map/ppermute | solution.py:168
  44.9 4.8 %radial_near.1.refs_6_ = f32[4,128,128]{2,1,0:T(8,128)} custom-call(bf16[2,144,128]{2,1,0:T(8,128)(2,1)} %copy-done.2, bf16[2,144,128]{2,1,0:T(8,128)(2,1)} %copy-done.1, bf16[2,144,128]{2,1,0:T(8,128)(2,1)} %copy-done.1, bf16[3,2,144,128]{3,2,1,0:T(8,128)(2,1)} %copy-done.3, bf16[768,128]{1,0:T(8,128)(2,1)} %refs_5_.1), custom_call_target="tpu_custom_call" | custom-call | tf_op jit(solution)/shard_map/radial_near/pallas_call | solution.py:376
  49.8 0.7 %copy-done.4 = bf16[3,2,144,128]{3,2,1,0:T(8,128)(2,1)} copy-done((bf16[3,2,144,128]{3,2,1,0:T(8,128)(2,1)}, bf16[3,2,144,128]{3,2,1,0:T(8,128)(2,1)S(1)}, u32[]{:S(2)}) %copy-start.4) | copy-done | bytes 221208
  50.5 0.7 %copy-done.5 = bf16[3,2,144,128]{3,2,1,0:T(8,128)(2,1)} copy-done((bf16[3,2,144,128]{3,2,1,0:T(8,128)(2,1)}, bf16[3,2,144,128]{3,2,1,0:T(8,128)(2,1)S(1)}, u32[]{:S(2)}) %copy-start.5) | copy-done | bytes 221208
  51.2 7.6 %radial_far.1.message_ref = f32[4,128,128]{2,1,0:T(8,128)} custom-call(bf16[2,144,128]{2,1,0:T(8,128)(2,1)} %copy-done.2, bf16[2,144,128]{2,1,0:T(8,128)(2,1)} %copy-done.1, bf16[2,144,128]{2,1,0:T(8,128)(2,1)} %copy-done.1, bf16[3,2,144,128]{3,2,1,0:T(8,128)(2,1)} %copy-done.5, bf16[3,2,144,128]{3,2,1,0:T(8,128)(2,1)} %copy-done.4, ...), custom_call_target="tpu_custom_call" | custom-call | tf_op jit(solution)/shard_map/radial_far/pallas_call | solution.py:376
  59.5 2.4 %longrange.1 = (f32[256,128]{1,0:T(8,128)}, f32[256,128]{1,0:T(8,128)}) custom-call(bf16[1024,512]{1,0:T(8,128)(2,1)} %get-tuple-element.12.table_ref, f32[4,128,128]{2,1,0:T(8,128)} %radial_far.1.message_ref, bf16[256,128]{1,0:T(8,128)(2,1)} %mix.1.refs_0_, bf16[256,128]{1,0:T(8,128)(2,1)} %copy-done.9, bf16[256,128]{1,0:T(8,128)(2,1)} %copy-done.8, ...), custom_call_target="tpu_custom_call" | custom-call | tf_op jit(solution)/shard_map/longrange/pallas_call | solution.py:376
  61.9 1.6 %collective-permute-done.14.refs_1_ = f32[256,128]{1,0:T(8,128)S(1)} collective-permute-done((f32[256,128]{1,0:T(8,128)}, f32[256,128]{1,0:T(8,128)S(1)}, u32[]{:S(2)}, u32[]{:S(2)}) %collective-permute-start.14) | collective-permute-done | bytes 131104 | tf_op jit(solution)/shard_map/ppermute | solution.py:168
  63.5 0.6 copy-done.6
  64.1 2.1 %node.1 = bf16[256,128]{1,0:T(8,128)(2,1)} custom-call(bf16[256,128]{1,0:T(8,128)(2,1)} %bitcast.17, f32[1,128]{1,0:T(1,128)} %bitcast.20, bf16[128,256]{1,0:T(8,128)(2,1)} %up_ref.1, bf16[256,128]{1,0:T(8,128)(2,1)} %down_ref.1, f32[256,128]{1,0:T(8,128)} %get-tuple-element.17.refs_0_, f32[256,128]{1,0:T(8,128)} %copy-done.6), custom_call_target="tpu_custom_call" | custom-call | tf_op jit(solution)/shard_map/node/pallas_call | solution.py:376
  (44 shorter events, 3.4 us)
Async XLA Ops:
  0.0 6.7 %copy-start = (s32[3,1024]{1,0:T(4,128)S(1)}, s32[3,1024]{1,0:T(4,128)}, u32[]{:S(2)}) copy-start(s32[3,1024]{1,0:T(4,128)} %param.14) | copy-start | bytes 36868
  1.6 11.3 %copy-start.2 = (bf16[2,144,128]{2,1,0:T(8,128)(2,1)}, bf16[2,144,128]{2,1,0:T(8,128)(2,1)S(1)}, u32[]{:S(2)}) copy-start(bf16[2,144,128]{2,1,0:T(8,128)(2,1)S(1)} %get-tuple-element.20.refs_0_) | copy-start | bytes 221188
  1.6 7.4 %collective-permute-start.2 = (bf16[2,144,128]{2,1,0:T(8,128)(2,1)S(1)}, bf16[2,144,128]{2,1,0:T(8,128)(2,1)S(1)}, u32[]{:S(2)}, u32[]{:S(2)}) collective-permute-start(bf16[2,144,128]{2,1,0:T(8,128)(2,1)S(1)} %get-tuple-element.20.refs_0_), channel_id=1, source_target_pairs={{0,6},{2,0},{4,2},{6,4},{1,7},{3,1},{5,3},{7,5},{8,14},{10,8},{12,... | collective-permute-start | bytes 221192 | tf_op jit(solution)/shard_map/ppermute | solution.py:168
  6.7 6.2 %collective-permute-start.1 = (bf16[2,144,128]{2,1,0:T(8,128)(2,1)S(1)}, bf16[2,144,128]{2,1,0:T(8,128)(2,1)S(1)}, u32[]{:S(2)}, u32[]{:S(2)}) collective-permute-start(bf16[2,144,128]{2,1,0:T(8,128)(2,1)S(1)} %get-tuple-element.20.refs_0_), channel_id=1, source_target_pairs={{0,2},{2,4},{4,6},{6,0},{1,3},{3,5},{5,7},{7,1},{8,10},{10,12},{12... | collective-permute-start | bytes 221192 | tf_op jit(solution)/shard_map/ppermute | solution.py:168
  6.7 9.4 %collective-permute-start = (bf16[2,144,128]{2,1,0:T(8,128)(2,1)S(1)}, bf16[2,144,128]{2,1,0:T(8,128)(2,1)S(1)}, u32[]{:S(2)}, u32[]{:S(2)}) collective-permute-start(bf16[2,144,128]{2,1,0:T(8,128)(2,1)S(1)} %get-tuple-element.20.refs_0_), channel_id=1, source_target_pairs={{0,1},{1,0},{2,3},{3,2},{4,5},{5,4},{6,7},{7,6},{8,9},{9,8},{10,11... | collective-permute-start | bytes 221192 | tf_op jit(solution)/shard_map/ppermute | solution.py:168
  12.9 28.6 %copy-start.3 = (bf16[3,2,144,128]{3,2,1,0:T(8,128)(2,1)}, bf16[3,2,144,128]{3,2,1,0:T(8,128)(2,1)S(1)}, u32[]{:S(2)}) copy-start(bf16[3,2,144,128]{3,2,1,0:T(8,128)(2,1)S(1)} %pad_maximum_fusion.refs_3_) | copy-start | bytes 663556
  12.9 36.9 %collective-permute-start.4 = (bf16[3,2,144,128]{3,2,1,0:T(8,128)(2,1)S(1)}, bf16[3,2,144,128]{3,2,1,0:T(8,128)(2,1)S(1)}, u32[]{:S(2)}, u32[]{:S(2)}) collective-permute-start(bf16[3,2,144,128]{3,2,1,0:T(8,128)(2,1)S(1)} %pad_maximum_fusion.refs_3_), channel_id=1, source_target_pairs={{0,24},{8,0},{16,8},{24,16},{1,25},{9,1},{17,9},{25,17},{2,26},{10... | collective-permute-start | bytes 663560 | tf_op jit(solution)/shard_map/ppermute | solution.py:168
  15.4 34.4 %collective-permute-start.3 = (bf16[3,2,144,128]{3,2,1,0:T(8,128)(2,1)S(1)}, bf16[3,2,144,128]{3,2,1,0:T(8,128)(2,1)S(1)}, u32[]{:S(2)}, u32[]{:S(2)}) collective-permute-start(bf16[3,2,144,128]{3,2,1,0:T(8,128)(2,1)S(1)} %pad_maximum_fusion.refs_3_), channel_id=1, source_target_pairs={{0,8},{8,16},{16,24},{24,0},{1,9},{9,17},{17,25},{25,1},{2,10},{10... | collective-permute-start | bytes 663560 | tf_op jit(solution)/shard_map/ppermute | solution.py:168
  16.1 0.6 copy-start.1
  21.3 5.4 %collective-permute-start.5 = (bf16[256,128]{1,0:T(8,128)(2,1)}, bf16[256,128]{1,0:T(8,128)(2,1)S(1)}, u32[]{:S(2)}, u32[]{:S(2)}) collective-permute-start(bf16[256,128]{1,0:T(8,128)(2,1)} %get-tuple-element.14), channel_id=1, source_target_pairs={{0,8},{8,16},{16,24},{24,0},{1,9},{9,17},{17,25},{25,1},{2,10},{10... | collective-permute-start | bytes 196616 | tf_op jit(solution)/shard_map/ppermute | solution.py:168
  23.2 4.5 %collective-permute-start.6 = (bf16[256,128]{1,0:T(8,128)(2,1)}, bf16[256,128]{1,0:T(8,128)(2,1)S(1)}, u32[]{:S(2)}, u32[]{:S(2)}) collective-permute-start(bf16[256,128]{1,0:T(8,128)(2,1)} %get-tuple-element.15), channel_id=1, source_target_pairs={{0,16},{8,24},{16,0},{24,8},{1,17},{9,25},{17,1},{25,9},{2,18},{10... | collective-permute-start | bytes 196616 | tf_op jit(solution)/shard_map/ppermute | solution.py:168
  24.7 4.5 %collective-permute-start.7 = (bf16[256,128]{1,0:T(8,128)(2,1)}, bf16[256,128]{1,0:T(8,128)(2,1)S(1)}, u32[]{:S(2)}, u32[]{:S(2)}) collective-permute-start(bf16[256,128]{1,0:T(8,128)(2,1)} %get-tuple-element.16), channel_id=1, source_target_pairs={{0,24},{8,0},{16,8},{24,16},{1,25},{9,1},{17,9},{25,17},{2,26},{10... | collective-permute-start | bytes 196616 | tf_op jit(solution)/shard_map/ppermute | solution.py:168
  26.6 2.6 %copy-start.11 = (bf16[256,128]{1,0:T(8,128)(2,1)}, bf16[256,128]{1,0:T(8,128)(2,1)S(1)}, u32[]{:S(2)}) copy-start(bf16[256,128]{1,0:T(8,128)(2,1)S(1)} %collective-permute-done.5.refs_1_) | copy-start | bytes 196612
  27.7 1.5 %copy-start.13 = (bf16[256,128]{1,0:T(8,128)(2,1)}, bf16[256,128]{1,0:T(8,128)(2,1)S(1)}, u32[]{:S(2)}) copy-start(bf16[256,128]{1,0:T(8,128)(2,1)S(1)} %collective-permute-done.6.refs_2_) | copy-start | bytes 196612
  29.2 0.6 copy-start.15
  31.4 4.5 %collective-permute-start.10 = (bf16[256,128]{1,0:T(8,128)(2,1)}, bf16[256,128]{1,0:T(8,128)(2,1)S(1)}, u32[]{:S(2)}, u32[]{:S(2)}) collective-permute-start(bf16[256,128]{1,0:T(8,128)(2,1)} %add_line.1.refs_0_), channel_id=1, source_target_pairs={{0,6},{2,0},{4,2},{6,4},{1,7},{3,1},{5,3},{7,5},{8,14},{10,8},{12,... | collective-permute-start | bytes 196616 | tf_op jit(solution)/shard_map/ppermute | solution.py:168
  31.9 5.4 %collective-permute-start.9 = (bf16[256,128]{1,0:T(8,128)(2,1)}, bf16[256,128]{1,0:T(8,128)(2,1)S(1)}, u32[]{:S(2)}, u32[]{:S(2)}) collective-permute-start(bf16[256,128]{1,0:T(8,128)(2,1)} %add_line.1.refs_0_), channel_id=1, source_target_pairs={{0,4},{2,6},{4,0},{6,2},{1,5},{3,7},{5,1},{7,3},{8,12},{10,14},{12... | collective-permute-start | bytes 196616 | tf_op jit(solution)/shard_map/ppermute | solution.py:168
  32.3 6.6 %collective-permute-start.8 = (bf16[256,128]{1,0:T(8,128)(2,1)}, bf16[256,128]{1,0:T(8,128)(2,1)S(1)}, u32[]{:S(2)}, u32[]{:S(2)}) collective-permute-start(bf16[256,128]{1,0:T(8,128)(2,1)} %add_line.1.refs_0_), channel_id=1, source_target_pairs={{0,2},{2,4},{4,6},{6,0},{1,3},{3,5},{5,7},{7,1},{8,10},{10,12},{12... | collective-permute-start | bytes 196616 | tf_op jit(solution)/shard_map/ppermute | solution.py:168
  35.9 3.1 %copy-start.10 = (bf16[256,128]{1,0:T(8,128)(2,1)}, bf16[256,128]{1,0:T(8,128)(2,1)S(1)}, u32[]{:S(2)}) copy-start(bf16[256,128]{1,0:T(8,128)(2,1)S(1)} %collective-permute-done.10.refs_3_) | copy-start | bytes 196612
  37.3 1.7 %copy-start.12 = (bf16[256,128]{1,0:T(8,128)(2,1)}, bf16[256,128]{1,0:T(8,128)(2,1)S(1)}, u32[]{:S(2)}) copy-start(bf16[256,128]{1,0:T(8,128)(2,1)S(1)} %collective-permute-done.9.refs_2_) | copy-start | bytes 196612
  39.0 0.6 copy-start.14
  41.5 17.3 %collective-permute-start.13 = (bf16[256,128]{1,0:T(8,128)(2,1)}, bf16[256,128]{1,0:T(8,128)(2,1)S(1)}, u32[]{:S(2)}, u32[]{:S(2)}) collective-permute-start(bf16[256,128]{1,0:T(8,128)(2,1)} %mix.1.refs_0_), channel_id=1, source_target_pairs={{0,8},{8,16},{16,24},{24,0},{1,9},{9,17},{17,25},{25,1},{2,10},{10... | collective-permute-start | bytes 196616 | tf_op jit(solution)/shard_map/ppermute | solution.py:168
  42.5 16.3 %collective-permute-start.12 = (bf16[256,128]{1,0:T(8,128)(2,1)}, bf16[256,128]{1,0:T(8,128)(2,1)S(1)}, u32[]{:S(2)}, u32[]{:S(2)}) collective-permute-start(bf16[256,128]{1,0:T(8,128)(2,1)} %mix.1.refs_0_), channel_id=1, source_target_pairs={{0,16},{8,24},{16,0},{24,8},{1,17},{9,25},{17,1},{25,9},{2,18},{10... | collective-permute-start | bytes 196616 | tf_op jit(solution)/shard_map/ppermute | solution.py:168
  43.5 15.3 %collective-permute-start.11 = (bf16[256,128]{1,0:T(8,128)(2,1)}, bf16[256,128]{1,0:T(8,128)(2,1)S(1)}, u32[]{:S(2)}, u32[]{:S(2)}) collective-permute-start(bf16[256,128]{1,0:T(8,128)(2,1)} %mix.1.refs_0_), channel_id=1, source_target_pairs={{0,24},{8,0},{16,8},{24,16},{1,25},{9,1},{17,9},{25,17},{2,26},{10... | collective-permute-start | bytes 196616 | tf_op jit(solution)/shard_map/ppermute | solution.py:168
  49.8 0.7 %copy-start.4 = (bf16[3,2,144,128]{3,2,1,0:T(8,128)(2,1)}, bf16[3,2,144,128]{3,2,1,0:T(8,128)(2,1)S(1)}, u32[]{:S(2)}) copy-start(bf16[3,2,144,128]{3,2,1,0:T(8,128)(2,1)S(1)} %collective-permute-done.4.refs_4_) | copy-start | bytes 663556
  50.5 0.7 %copy-start.5 = (bf16[3,2,144,128]{3,2,1,0:T(8,128)(2,1)}, bf16[3,2,144,128]{3,2,1,0:T(8,128)(2,1)S(1)}, u32[]{:S(2)}) copy-start(bf16[3,2,144,128]{3,2,1,0:T(8,128)(2,1)S(1)} %collective-permute-done.3.refs_3_) | copy-start | bytes 663556
  58.8 0.6 copy-start.7
  58.8 0.7 copy-start.8
  58.8 0.6 copy-start.9
  61.9 1.6 %collective-permute-start.14 = (f32[256,128]{1,0:T(8,128)}, f32[256,128]{1,0:T(8,128)S(1)}, u32[]{:S(2)}, u32[]{:S(2)}) collective-permute-start(f32[256,128]{1,0:T(8,128)} %get-tuple-element.18), channel_id=1, source_target_pairs={{0,1},{1,0},{2,3},{3,2},{4,5},{5,4},{6,7},{7,6},{8,9},{9,8},{10,11... | collective-permute-start | bytes 393224 | tf_op jit(solution)/shard_map/ppermute | solution.py:168
  63.5 0.6 copy-start.6

commit v2 on v1

--- a/solution.py
+++ b/solution.py
@@ -237,7 +237,7 @@
     refs[-1][...] = total.astype(refs[-1].dtype)
 
 
-def mix_kernel(scale, place_ref, filters_ref, mix_ref, *refs):
+def mix_kernel(scale, filters_ref, mix_ref, *refs):
     total = refs[0][...].astype(jnp.float32)
     for ref in refs[1:-1]:
         total = total + ref[...].astype(jnp.float32)
@@ -364,25 +364,18 @@
     refs[-1][...] = updated.astype(jnp.bfloat16)
 
 
-def call(kernel, out_shape, *args, scalars=0, scratch=(), blocks=None, name=None):
-    def whole(a):
-        return pl.BlockSpec(a.shape, lambda i, *s: (0,) * len(a.shape))
-
-    specs = [whole(a) for a in args[scalars:]]
-    for at, spec in (blocks or {}).items():
-        specs[at] = spec
+def call(kernel, out_shape, *args, scalars=0, scratch=(), name=None):
+    in_vmem = pl.BlockSpec(memory_space=pltpu.VMEM)
+    held = [pltpu.with_memory_space_constraint(a, pltpu.VMEM) for a in args[scalars:]]
+    args = list(args[:scalars]) + held
+    specs = [pl.BlockSpec(memory_space=pltpu.SMEM)] * scalars
     single = not isinstance(out_shape, (list, tuple))
-    outs = whole(out_shape) if single else [whole(o) for o in out_shape]
     return pl.pallas_call(
         kernel,
-        out_shape=out_shape,
-        grid_spec=pltpu.PrefetchScalarGridSpec(
-            num_scalar_prefetch=scalars,
-            grid=(1,),
-            in_specs=specs,
-            out_specs=outs,
-            scratch_shapes=list(scratch),
-        ),
+        out_shape=jax.tree.map(lambda o: pltpu.VMEM(o.shape, o.dtype), out_shape),
+        in_specs=specs + [in_vmem] * (len(args) - scalars),
+        out_specs=in_vmem if single else [in_vmem] * len(out_shape),
+        scratch_shapes=list(scratch),
         name=name,
     )(*args)
 
@@ -469,16 +462,14 @@
 
     message = messages([middle], [ring[3:6]], None, "radial_near")
     scale = 1.0 / math.sqrt(atoms * sizes[0] * sizes[1] * sizes[2])
-    spot = (place[2] * n_blocks + place[0]).reshape(1)
+    spot = place[2] * waves + place[0] * block
+    mine_filters = lax.dynamic_slice_in_dim(filters, spot, block, axis=0)
     filtered = call(
         functools.partial(mix_kernel, scale),
         shape((2 * block, width), jnp.bfloat16),
-        spot,
-        filters,
+        mine_filters,
         mix_weight,
         *lines,
-        scalars=1,
-        blocks={0: pl.BlockSpec((block, width), lambda i, s: (s[0], 0))},
         name="mix",
     )
     blocks = [filtered] + [shift(filtered, "gx", -n) for n in range(1, n_blocks)]

time: 66.7 us -> 53.3 us (0.80)
  Pallas kernels: 25 us -> 13.4 us
  waiting for transfers between devices: 16.5 us -> 8.75 us
  starting transfers between devices: 17.1 us -> 22.4 us
  local copies, waits for them, and re-layouts: 4.59 us -> 6.08 us
    pallas_call x7, Pallas kernels: 25 us -> 13.4 us  [call(): pl.pallas_call(kernel, out_shape=jax.tree.map(lambda o: pltpu.VMEM(o.shap...]
    ppermute x15, waiting for transfers between devices: 16.5 us -> 8.75 us  [shift(): lax.ppermute(array, axis, [(i, (i + step) % size) for i in range(size)])]
    ppermute x15, starting transfers between devices: 17.1 us -> 22.4 us  [shift(): lax.ppermute(array, axis, [(i, (i + step) % size) for i in range(size)])]
    unnamed x32 -> x31, local copies, waits for them, and re-layouts: 4.58 us -> 6.06 us
  transfers between devices with their start and end apart: 15 -> 15, of which waited for: 9 -> 6; matrix products, arithmetic and copies ran while one was open for 2% -> 1% of each run, Pallas kernels for 31% -> 24%
where the time goes in v2:
time: 53.3 us; the launch traced here: 53 us
  starting transfers between devices  22.4 us (42%)
  Pallas kernels  13.4 us (25%)
  waiting for transfers between devices  8.75 us (16%)
  local copies, waits for them, and re-layouts  6.08 us (11%)
  other arithmetic  2.26 us (4%)
    ppermute x15, starting transfers between devices, shift(): lax.ppermute(array, axis, [(i, (i + step) % size) for i in range(size)])  22.4 us
    pallas_call x7, Pallas kernels, call(): pl.pallas_call(kernel, out_shape=jax.tree.map(lambda o: pltpu.VMEM(o.shap...  13.4 us
    ppermute x15, waiting for transfers between devices, shift(): lax.ppermute(array, axis, [(i, (i + step) % size) for i in range(size)])  8.75 us
    unnamed x31, local copies, waits for them, and re-layouts  6.06 us
  transfers between devices with their start and end apart: 15, of which 6 were waited for; matrix products, arithmetic and copies ran while one was open for 1% of the time, Pallas kernels for 24%

profile of v2, /device:TPU:0, one launch (start us, length us, event | category | flops | bytes accessed | tf_op | source)
XLA Modules:
  0.0 53.0 jit_solution(3530315969943795149)
XLA Ops:
  0.0 0.7 %fusion.7 = bf16[2,3,128]{2,1,0:T(4,128)(2,1)S(1)} fusion(s32[3,1,1,2,128]{4,3,2,1,0:T(2,128)} %param.13), kind=kLoop, calls=%fused_computation.15 | loop fusion | flops 768 | bytes 4608 | tf_op jit(solution)/shard_map/convert_element_type | solution.py:404
  0.7 0.9 %fusion.8 = (bf16[1,2,144,128]{3,2,1,0:T(8,128)(2,1)S(1)}, bf16[2,144,128]{2,1,0:T(8,128)(2,1)S(1)}) fusion(bf16[2,3,128]{2,1,0:T(4,128)(2,1)S(1)} %fusion.7, bf16[2,128,128]{2,1,0:T(8,128)(2,1)} %bitcast.16), kind=kLoop, calls=%fused_computation.19 | loop fusion | flops 221184 | bytes 214528 | tf_op jit(solution)/shard_map/stack | solution.py:414
  1.6 5.1 %collective-permute-start.2 = (bf16[2,144,128]{2,1,0:T(8,128)(2,1)S(1)}, bf16[2,144,128]{2,1,0:T(8,128)(2,1)S(1)}, u32[]{:S(2)}, u32[]{:S(2)}) collective-permute-start(bf16[2,144,128]{2,1,0:T(8,128)(2,1)S(1)} %get-tuple-element.20.refs_0_), channel_id=1, source_target_pairs={{0,6},{2,0},{4,2},{6,4},{1,7},{3,1},{5,3},{7,5},{8,14},{10,8},{12,... | collective-permute-start | bytes 221192 | tf_op jit(solution)/shard_map/ppermute | solution.py:168
  6.9 0.6 %pad_add_fusion.place_ref = s32[3]{0:T(128)} fusion(s32[1]{0:T(128)} %bitcast.4, s32[1]{0:T(128)} %bitcast.3, s32[1]{0:T(128)} %bitcast.2), kind=kLoop, calls=%fused_computation.18 | loop fusion | flops 6 | bytes 24 | tf_op jit(solution)/shard_map/stack | solution.py:397
  7.4 0.6 %collective-permute-done.refs_1_.refs_2_ = bf16[2,144,128]{2,1,0:T(8,128)(2,1)S(1)} collective-permute-done((bf16[2,144,128]{2,1,0:T(8,128)(2,1)S(1)}, bf16[2,144,128]{2,1,0:T(8,128)(2,1)S(1)}, u32[]{:S(2)}, u32[]{:S(2)}) %collective-permute-start) | collective-permute-done | bytes 73760 | tf_op jit(solution)/shard_map/ppermute | solution.py:168
  8.0 2.8 %tables.1 = (bf16[1024,512]{1,0:T(8,128)(2,1)S(1)}, bf16[256,128]{1,0:T(8,128)(2,1)S(1)}, bf16[256,128]{1,0:T(8,128)(2,1)S(1)}, bf16[256,128]{1,0:T(8,128)(2,1)S(1)}, bf16[256,128]{1,0:T(8,128)(2,1)S(1)}) custom-call(s32[3]{0:T(128)} %pad_add_fusion.place_ref, bf16[16,512]{1,0:T(8,128)(2,1)S(1)} %fusion.4.waves_ref, bf16[128,128]{1,0:T(8,128)(2,1)S(1)} %copy-done.12, ...), custom_call_target="tpu_custom_call" | custom-call | tf_op jit(solution)/shard_map/tables/pallas_call | solution.py:373
  10.8 1.6 %collective-permute-start.5 = (bf16[256,128]{1,0:T(8,128)(2,1)S(1)}, bf16[256,128]{1,0:T(8,128)(2,1)S(1)}, u32[]{:S(2)}, u32[]{:S(2)}) collective-permute-start(bf16[256,128]{1,0:T(8,128)(2,1)S(1)} %get-tuple-element.14), channel_id=1, source_target_pairs={{0,8},{8,16},{16,24},{24,0},{1,9},{9,17},{17,25},{25,1},{2,10},{10... | collective-permute-start | bytes 196616 | tf_op jit(solution)/shard_map/ppermute | solution.py:168
  12.3 1.5 %collective-permute-start.6 = (bf16[256,128]{1,0:T(8,128)(2,1)S(1)}, bf16[256,128]{1,0:T(8,128)(2,1)S(1)}, u32[]{:S(2)}, u32[]{:S(2)}) collective-permute-start(bf16[256,128]{1,0:T(8,128)(2,1)S(1)} %get-tuple-element.15), channel_id=1, source_target_pairs={{0,16},{8,24},{16,0},{24,8},{1,17},{9,25},{17,1},{25,9},{2,18},{10... | collective-permute-start | bytes 196616 | tf_op jit(solution)/shard_map/ppermute | solution.py:168
  13.9 1.4 %collective-permute-start.7 = (bf16[256,128]{1,0:T(8,128)(2,1)S(1)}, bf16[256,128]{1,0:T(8,128)(2,1)S(1)}, u32[]{:S(2)}, u32[]{:S(2)}) collective-permute-start(bf16[256,128]{1,0:T(8,128)(2,1)S(1)} %get-tuple-element.16), channel_id=1, source_target_pairs={{0,24},{8,0},{16,8},{24,16},{1,25},{9,1},{17,9},{25,17},{2,26},{10... | collective-permute-start | bytes 196616 | tf_op jit(solution)/shard_map/ppermute | solution.py:168
  15.3 0.6 %collective-permute-start.4 = (bf16[3,2,144,128]{3,2,1,0:T(8,128)(2,1)S(1)}, bf16[3,2,144,128]{3,2,1,0:T(8,128)(2,1)S(1)}, u32[]{:S(2)}, u32[]{:S(2)}) collective-permute-start(bf16[3,2,144,128]{3,2,1,0:T(8,128)(2,1)S(1)} %pad_maximum_fusion.refs_3_), channel_id=1, source_target_pairs={{0,24},{8,0},{16,8},{24,16},{1,25},{9,1},{17,9},{25,17},{2,26},{10... | collective-permute-start | bytes 663560 | tf_op jit(solution)/shard_map/ppermute | solution.py:168
  15.9 1.5 %collective-permute-start.3 = (bf16[3,2,144,128]{3,2,1,0:T(8,128)(2,1)S(1)}, bf16[3,2,144,128]{3,2,1,0:T(8,128)(2,1)}, u32[]{:S(2)}, u32[]{:S(2)}) collective-permute-start(bf16[3,2,144,128]{3,2,1,0:T(8,128)(2,1)S(1)} %pad_maximum_fusion.refs_3_), channel_id=1, source_target_pairs={{0,8},{8,16},{16,24},{24,0},{1,9},{9,17},{17,25},{25,1},{2,10},{10... | collective-permute-start | bytes 663560 | tf_op jit(solution)/shard_map/ppermute | solution.py:168
  17.4 1.4 %collective-permute-done.7.refs_3_ = bf16[256,128]{1,0:T(8,128)(2,1)S(1)} collective-permute-done((bf16[256,128]{1,0:T(8,128)(2,1)S(1)}, bf16[256,128]{1,0:T(8,128)(2,1)S(1)}, u32[]{:S(2)}, u32[]{:S(2)}) %collective-permute-start.7) | collective-permute-done | bytes 65568 | tf_op jit(solution)/shard_map/ppermute | solution.py:168
  18.9 3.9 %collective-permute-start.10 = (bf16[256,128]{1,0:T(8,128)(2,1)S(1)}, bf16[256,128]{1,0:T(8,128)(2,1)S(1)}, u32[]{:S(2)}, u32[]{:S(2)}) collective-permute-start(bf16[256,128]{1,0:T(8,128)(2,1)S(1)} %add_line.1.refs_0_), channel_id=1, source_target_pairs={{0,6},{2,0},{4,2},{6,4},{1,7},{3,1},{5,3},{7,5},{8,14},{10,8},{12,... | collective-permute-start | bytes 196616 | tf_op jit(solution)/shard_map/ppermute | solution.py:168
  22.7 0.6 %collective-permute-start.8 = (bf16[256,128]{1,0:T(8,128)(2,1)S(1)}, bf16[256,128]{1,0:T(8,128)(2,1)S(1)}, u32[]{:S(2)}, u32[]{:S(2)}) collective-permute-start(bf16[256,128]{1,0:T(8,128)(2,1)S(1)} %add_line.1.refs_0_), channel_id=1, source_target_pairs={{0,2},{2,4},{4,6},{6,0},{1,3},{3,5},{5,7},{7,1},{8,10},{10,12},{12... | collective-permute-start | bytes 196616 | tf_op jit(solution)/shard_map/ppermute | solution.py:168
  23.4 1.2 %collective-permute-done.10.refs_3_ = bf16[256,128]{1,0:T(8,128)(2,1)S(1)} collective-permute-done((bf16[256,128]{1,0:T(8,128)(2,1)S(1)}, bf16[256,128]{1,0:T(8,128)(2,1)S(1)}, u32[]{:S(2)}, u32[]{:S(2)}) %collective-permute-start.10) | collective-permute-done | bytes 65568 | tf_op jit(solution)/shard_map/ppermute | solution.py:168
  24.7 3.3 %collective-permute-done.9.refs_2_ = bf16[256,128]{1,0:T(8,128)(2,1)S(1)} collective-permute-done((bf16[256,128]{1,0:T(8,128)(2,1)S(1)}, bf16[256,128]{1,0:T(8,128)(2,1)S(1)}, u32[]{:S(2)}, u32[]{:S(2)}) %collective-permute-start.9) | collective-permute-done | bytes 65568 | tf_op jit(solution)/shard_map/ppermute | solution.py:168
  27.9 0.9 %collective-permute-done.8.refs_1_ = bf16[256,128]{1,0:T(8,128)(2,1)S(1)} collective-permute-done((bf16[256,128]{1,0:T(8,128)(2,1)S(1)}, bf16[256,128]{1,0:T(8,128)(2,1)S(1)}, u32[]{:S(2)}, u32[]{:S(2)}) %collective-permute-start.8) | collective-permute-done | bytes 65568 | tf_op jit(solution)/shard_map/ppermute | solution.py:168
  29.1 4.5 %collective-permute-start.13 = (bf16[256,128]{1,0:T(8,128)(2,1)S(1)}, bf16[256,128]{1,0:T(8,128)(2,1)S(1)}, u32[]{:S(2)}, u32[]{:S(2)}) collective-permute-start(bf16[256,128]{1,0:T(8,128)(2,1)S(1)} %mix.1.refs_0_), channel_id=1, source_target_pairs={{0,8},{8,16},{16,24},{24,0},{1,9},{9,17},{17,25},{25,1},{2,10},{10... | collective-permute-start | bytes 196616 | tf_op jit(solution)/shard_map/ppermute | solution.py:168
  33.6 1.5 %collective-permute-start.11 = (bf16[256,128]{1,0:T(8,128)(2,1)S(1)}, bf16[256,128]{1,0:T(8,128)(2,1)S(1)}, u32[]{:S(2)}, u32[]{:S(2)}) collective-permute-start(bf16[256,128]{1,0:T(8,128)(2,1)S(1)} %mix.1.refs_0_), channel_id=1, source_target_pairs={{0,24},{8,0},{16,8},{24,16},{1,25},{9,1},{17,9},{25,17},{2,26},{10... | collective-permute-start | bytes 196616 | tf_op jit(solution)/shard_map/ppermute | solution.py:168
  35.2 3.0 %radial_near.1.refs_6_ = f32[4,128,128]{2,1,0:T(8,128)S(1)} custom-call(bf16[2,144,128]{2,1,0:T(8,128)(2,1)S(1)} %get-tuple-element.20.refs_0_, bf16[2,144,128]{2,1,0:T(8,128)(2,1)S(1)} %collective-permute-done.refs_1_.refs_2_, bf16[2,144,128]{2,1,0:T(8,128)(2,1)S(1)} %collective-permute-done.refs_1_.refs_2_, ...), custom_call_target="tpu_custom_call" | custom-call | tf_op jit(solution)/shard_map/radial_near/pallas_call | solution.py:373
  38.2 0.7 %copy-done.1 = f32[4,128,128]{2,1,0:T(8,128)} copy-done((f32[4,128,128]{2,1,0:T(8,128)}, f32[4,128,128]{2,1,0:T(8,128)S(1)}, u32[]{:S(2)}) %copy-start.1) | copy-done | bytes 262168
  38.9 0.7 %copy-done.5 = bf16[3,2,144,128]{3,2,1,0:T(8,128)(2,1)} copy-done((bf16[3,2,144,128]{3,2,1,0:T(8,128)(2,1)}, bf16[3,2,144,128]{3,2,1,0:T(8,128)(2,1)S(1)}, u32[]{:S(2)}) %copy-start.5) | copy-done | bytes 221208
  39.6 0.9 %copy-done.2 = f32[4,128,128]{2,1,0:T(8,128)S(1)} copy-done((f32[4,128,128]{2,1,0:T(8,128)S(1)}, f32[4,128,128]{2,1,0:T(8,128)}, u32[]{:S(2)}) %copy-start.2) | copy-done | bytes 262168
  40.5 0.9 %copy-done.6 = bf16[3,2,144,128]{3,2,1,0:T(8,128)(2,1)S(1)} copy-done((bf16[3,2,144,128]{3,2,1,0:T(8,128)(2,1)S(1)}, bf16[3,2,144,128]{3,2,1,0:T(8,128)(2,1)}, u32[]{:S(2)}) %copy-start.6) | copy-done | bytes 221208
  41.4 6.5 %radial_far.1.message_ref = f32[4,128,128]{2,1,0:T(8,128)S(1)} custom-call(bf16[2,144,128]{2,1,0:T(8,128)(2,1)S(1)} %get-tuple-element.20.refs_0_, bf16[2,144,128]{2,1,0:T(8,128)(2,1)S(1)} %collective-permute-done.refs_1_.refs_2_, bf16[2,144,128]{2,1,0:T(8,128)(2,1)S(1)} %collective-permute-done.refs_1_.refs_2_, ...), custom_call_target="tpu_custom_call" | custom-call | tf_op jit(solution)/shard_map/radial_far/pallas_call | solution.py:373
  48.0 0.6 %copy-done.10 = bf16[256,128]{1,0:T(8,128)(2,1)} copy-done((bf16[256,128]{1,0:T(8,128)(2,1)}, bf16[256,128]{1,0:T(8,128)(2,1)S(1)}, u32[]{:S(2)}) %copy-start.10) | copy-done | bytes 65560
  48.6 0.8 %copy-done.11 = bf16[256,128]{1,0:T(8,128)(2,1)S(1)} copy-done((bf16[256,128]{1,0:T(8,128)(2,1)S(1)}, bf16[256,128]{1,0:T(8,128)(2,1)}, u32[]{:S(2)}) %copy-start.11) | copy-done | bytes 65560
  49.5 0.4 longrange.1
  50.0 1.3 %collective-permute-done.14.refs_1_ = f32[256,128]{1,0:T(8,128)S(1)} collective-permute-done((f32[256,128]{1,0:T(8,128)S(1)}, f32[256,128]{1,0:T(8,128)S(1)}, u32[]{:S(2)}, u32[]{:S(2)}) %collective-permute-start.14) | collective-permute-done | bytes 131104 | tf_op jit(solution)/shard_map/ppermute | solution.py:168
  51.3 0.6 %copy-done.13 = f32[128]{0:T(128)S(1)} copy-done((f32[128]{0:T(128)S(1)}, f32[128]{0:T(128)}, u32[]{:S(2)}) %copy-start.13) | copy-done | bytes 536
  52.0 0.4 node.1
  52.4 0.6 %copy.17 = bf16[1,1,2,128,128]{4,3,2,1,0:T(8,128)(2,1)} copy(bf16[1,1,2,128,128]{4,3,2,1,0:T(8,128)(2,1)S(1)} %bitcast.15) | data formatting | bytes 131072
  (44 shorter events, 0.6 us)
Async XLA Ops:
  0.0 23.4 %copy-start = (f32[1024,128]{1,0:T(8,128)S(1)}, f32[1024,128]{1,0:T(8,128)}, u32[]{:S(2)}) copy-start(f32[1024,128]{1,0:T(8,128)} %param.17) | copy-start | bytes 1572868
  1.6 5.2 %copy-start.14 = (s32[3,1024]{1,0:T(4,128)S(1)}, s32[3,1024]{1,0:T(4,128)}, u32[]{:S(2)}) copy-start(s32[3,1024]{1,0:T(4,128)} %param.14) | copy-start | bytes 36868
  1.6 13.7 %collective-permute-start.2 = (bf16[2,144,128]{2,1,0:T(8,128)(2,1)S(1)}, bf16[2,144,128]{2,1,0:T(8,128)(2,1)S(1)}, u32[]{:S(2)}, u32[]{:S(2)}) collective-permute-start(bf16[2,144,128]{2,1,0:T(8,128)(2,1)S(1)} %get-tuple-element.20.refs_0_), channel_id=1, source_target_pairs={{0,6},{2,0},{4,2},{6,4},{1,7},{3,1},{5,3},{7,5},{8,14},{10,8},{12,... | collective-permute-start | bytes 221192 | tf_op jit(solution)/shard_map/ppermute | solution.py:168
  6.8 8.5 %collective-permute-start.1 = (bf16[2,144,128]{2,1,0:T(8,128)(2,1)S(1)}, bf16[2,144,128]{2,1,0:T(8,128)(2,1)S(1)}, u32[]{:S(2)}, u32[]{:S(2)}) collective-permute-start(bf16[2,144,128]{2,1,0:T(8,128)(2,1)S(1)} %get-tuple-element.20.refs_0_), channel_id=1, source_target_pairs={{0,2},{2,4},{4,6},{6,0},{1,3},{3,5},{5,7},{7,1},{8,10},{10,12},{12... | collective-permute-start | bytes 221192 | tf_op jit(solution)/shard_map/ppermute | solution.py:168
  6.8 1.3 %collective-permute-start = (bf16[2,144,128]{2,1,0:T(8,128)(2,1)S(1)}, bf16[2,144,128]{2,1,0:T(8,128)(2,1)S(1)}, u32[]{:S(2)}, u32[]{:S(2)}) collective-permute-start(bf16[2,144,128]{2,1,0:T(8,128)(2,1)S(1)} %get-tuple-element.20.refs_0_), channel_id=1, source_target_pairs={{0,1},{1,0},{2,3},{3,2},{4,5},{5,4},{6,7},{7,6},{8,9},{9,8},{10,11... | collective-permute-start | bytes 221192 | tf_op jit(solution)/shard_map/ppermute | solution.py:168
  6.8 1.3 %copy-start.12 = (bf16[128,128]{1,0:T(8,128)(2,1)S(1)}, bf16[128,128]{1,0:T(8,128)(2,1)}, u32[]{:S(2)}) copy-start(bf16[128,128]{1,0:T(8,128)(2,1)} %charge_ref.1) | copy-start | bytes 98308
  10.8 6.6 %collective-permute-start.5 = (bf16[256,128]{1,0:T(8,128)(2,1)S(1)}, bf16[256,128]{1,0:T(8,128)(2,1)S(1)}, u32[]{:S(2)}, u32[]{:S(2)}) collective-permute-start(bf16[256,128]{1,0:T(8,128)(2,1)S(1)} %get-tuple-element.14), channel_id=1, source_target_pairs={{0,8},{8,16},{16,24},{24,0},{1,9},{9,17},{17,25},{25,1},{2,10},{10... | collective-permute-start | bytes 196616 | tf_op jit(solution)/shard_map/ppermute | solution.py:168
  12.3 5.1 %collective-permute-start.6 = (bf16[256,128]{1,0:T(8,128)(2,1)S(1)}, bf16[256,128]{1,0:T(8,128)(2,1)S(1)}, u32[]{:S(2)}, u32[]{:S(2)}) collective-permute-start(bf16[256,128]{1,0:T(8,128)(2,1)S(1)} %get-tuple-element.15), channel_id=1, source_target_pairs={{0,16},{8,24},{16,0},{24,8},{1,17},{9,25},{17,1},{25,9},{2,18},{10... | collective-permute-start | bytes 196616 | tf_op jit(solution)/shard_map/ppermute | solution.py:168
  13.9 5.0 %collective-permute-start.7 = (bf16[256,128]{1,0:T(8,128)(2,1)S(1)}, bf16[256,128]{1,0:T(8,128)(2,1)S(1)}, u32[]{:S(2)}, u32[]{:S(2)}) collective-permute-start(bf16[256,128]{1,0:T(8,128)(2,1)S(1)} %get-tuple-element.16), channel_id=1, source_target_pairs={{0,24},{8,0},{16,8},{24,16},{1,25},{9,1},{17,9},{25,17},{2,26},{10... | collective-permute-start | bytes 196616 | tf_op jit(solution)/shard_map/ppermute | solution.py:168
  15.3 23.5 %collective-permute-start.4 = (bf16[3,2,144,128]{3,2,1,0:T(8,128)(2,1)S(1)}, bf16[3,2,144,128]{3,2,1,0:T(8,128)(2,1)S(1)}, u32[]{:S(2)}, u32[]{:S(2)}) collective-permute-start(bf16[3,2,144,128]{3,2,1,0:T(8,128)(2,1)S(1)} %pad_maximum_fusion.refs_3_), channel_id=1, source_target_pairs={{0,24},{8,0},{16,8},{24,16},{1,25},{9,1},{17,9},{25,17},{2,26},{10... | collective-permute-start | bytes 663560 | tf_op jit(solution)/shard_map/ppermute | solution.py:168
  15.9 23.6 %collective-permute-start.3 = (bf16[3,2,144,128]{3,2,1,0:T(8,128)(2,1)S(1)}, bf16[3,2,144,128]{3,2,1,0:T(8,128)(2,1)}, u32[]{:S(2)}, u32[]{:S(2)}) collective-permute-start(bf16[3,2,144,128]{3,2,1,0:T(8,128)(2,1)S(1)} %pad_maximum_fusion.refs_3_), channel_id=1, source_target_pairs={{0,8},{8,16},{16,24},{24,0},{1,9},{9,17},{17,25},{25,1},{2,10},{10... | collective-permute-start | bytes 663560 | tf_op jit(solution)/shard_map/ppermute | solution.py:168
  18.9 10.0 %copy-start.7 = (f32[128,128]{1,0:T(8,128)S(1)}, f32[128,128]{1,0:T(8,128)}, u32[]{:S(2)}) copy-start(f32[128,128]{1,0:T(8,128)} %mix_ref.1) | copy-start | bytes 196612
  18.9 5.8 %collective-permute-start.10 = (bf16[256,128]{1,0:T(8,128)(2,1)S(1)}, bf16[256,128]{1,0:T(8,128)(2,1)S(1)}, u32[]{:S(2)}, u32[]{:S(2)}) collective-permute-start(bf16[256,128]{1,0:T(8,128)(2,1)S(1)} %add_line.1.refs_0_), channel_id=1, source_target_pairs={{0,6},{2,0},{4,2},{6,4},{1,7},{3,1},{5,3},{7,5},{8,14},{10,8},{12,... | collective-permute-start | bytes 196616 | tf_op jit(solution)/shard_map/ppermute | solution.py:168
  22.7 5.2 %collective-permute-start.9 = (bf16[256,128]{1,0:T(8,128)(2,1)S(1)}, bf16[256,128]{1,0:T(8,128)(2,1)S(1)}, u32[]{:S(2)}, u32[]{:S(2)}) collective-permute-start(bf16[256,128]{1,0:T(8,128)(2,1)S(1)} %add_line.1.refs_0_), channel_id=1, source_target_pairs={{0,4},{2,6},{4,0},{6,2},{1,5},{3,7},{5,1},{7,3},{8,12},{10,14},{12... | collective-permute-start | bytes 196616 | tf_op jit(solution)/shard_map/ppermute | solution.py:168
  22.7 6.1 %collective-permute-start.8 = (bf16[256,128]{1,0:T(8,128)(2,1)S(1)}, bf16[256,128]{1,0:T(8,128)(2,1)S(1)}, u32[]{:S(2)}, u32[]{:S(2)}) collective-permute-start(bf16[256,128]{1,0:T(8,128)(2,1)S(1)} %add_line.1.refs_0_), channel_id=1, source_target_pairs={{0,2},{2,4},{4,6},{6,0},{1,3},{3,5},{5,7},{7,1},{8,10},{10,12},{12... | collective-permute-start | bytes 196616 | tf_op jit(solution)/shard_map/ppermute | solution.py:168
  23.4 11.8 %copy-start.3 = (bf16[768,128]{1,0:T(8,128)(2,1)S(1)}, bf16[768,128]{1,0:T(8,128)(2,1)}, u32[]{:S(2)}) copy-start(bf16[768,128]{1,0:T(8,128)(2,1)} %refs_5_.1) | copy-start | bytes 589828
  29.1 18.9 %collective-permute-start.13 = (bf16[256,128]{1,0:T(8,128)(2,1)S(1)}, bf16[256,128]{1,0:T(8,128)(2,1)S(1)}, u32[]{:S(2)}, u32[]{:S(2)}) collective-permute-start(bf16[256,128]{1,0:T(8,128)(2,1)S(1)} %mix.1.refs_0_), channel_id=1, source_target_pairs={{0,8},{8,16},{16,24},{24,0},{1,9},{9,17},{17,25},{25,1},{2,10},{10... | collective-permute-start | bytes 196616 | tf_op jit(solution)/shard_map/ppermute | solution.py:168
  33.6 14.4 %collective-permute-start.12 = (bf16[256,128]{1,0:T(8,128)(2,1)S(1)}, bf16[256,128]{1,0:T(8,128)(2,1)S(1)}, u32[]{:S(2)}, u32[]{:S(2)}) collective-permute-start(bf16[256,128]{1,0:T(8,128)(2,1)S(1)} %mix.1.refs_0_), channel_id=1, source_target_pairs={{0,16},{8,24},{16,0},{24,8},{1,17},{9,25},{17,1},{25,9},{2,18},{10... | collective-permute-start | bytes 196616 | tf_op jit(solution)/shard_map/ppermute | solution.py:168
  33.6 14.4 %collective-permute-start.11 = (bf16[256,128]{1,0:T(8,128)(2,1)S(1)}, bf16[256,128]{1,0:T(8,128)(2,1)S(1)}, u32[]{:S(2)}, u32[]{:S(2)}) collective-permute-start(bf16[256,128]{1,0:T(8,128)(2,1)S(1)} %mix.1.refs_0_), channel_id=1, source_target_pairs={{0,24},{8,0},{16,8},{24,16},{1,25},{9,1},{17,9},{25,17},{2,26},{10... | collective-permute-start | bytes 196616 | tf_op jit(solution)/shard_map/ppermute | solution.py:168
  38.2 0.7 %copy-start.1 = (f32[4,128,128]{2,1,0:T(8,128)}, f32[4,128,128]{2,1,0:T(8,128)S(1)}, u32[]{:S(2)}) copy-start(f32[4,128,128]{2,1,0:T(8,128)S(1)} %radial_near.1.refs_6_) | copy-start | bytes 786436
  38.9 0.7 %copy-start.5 = (bf16[3,2,144,128]{3,2,1,0:T(8,128)(2,1)}, bf16[3,2,144,128]{3,2,1,0:T(8,128)(2,1)S(1)}, u32[]{:S(2)}) copy-start(bf16[3,2,144,128]{3,2,1,0:T(8,128)(2,1)S(1)} %collective-permute-done.4.refs_4_) | copy-start | bytes 663556
  39.6 1.0 %copy-start.2 = (f32[4,128,128]{2,1,0:T(8,128)S(1)}, f32[4,128,128]{2,1,0:T(8,128)}, u32[]{:S(2)}) copy-start(f32[4,128,128]{2,1,0:T(8,128)} %copy-done.1) | copy-start | bytes 786436
  40.5 0.9 %copy-start.6 = (bf16[3,2,144,128]{3,2,1,0:T(8,128)(2,1)S(1)}, bf16[3,2,144,128]{3,2,1,0:T(8,128)(2,1)}, u32[]{:S(2)}) copy-start(bf16[3,2,144,128]{3,2,1,0:T(8,128)(2,1)} %copy-done.5) | copy-start | bytes 663556
  48.0 0.6 %copy-start.10 = (bf16[256,128]{1,0:T(8,128)(2,1)}, bf16[256,128]{1,0:T(8,128)(2,1)S(1)}, u32[]{:S(2)}) copy-start(bf16[256,128]{1,0:T(8,128)(2,1)S(1)} %collective-permute-done.11.refs_1_) | copy-start | bytes 196612
  48.6 0.8 %copy-start.11 = (bf16[256,128]{1,0:T(8,128)(2,1)S(1)}, bf16[256,128]{1,0:T(8,128)(2,1)}, u32[]{:S(2)}) copy-start(bf16[256,128]{1,0:T(8,128)(2,1)} %copy-done.10) | copy-start | bytes 196612
  49.5 1.9 %copy-start.4 = (bf16[1,1,2,128,128]{4,3,2,1,0:T(8,128)(2,1)S(1)}, bf16[1,1,2,128,128]{4,3,2,1,0:T(8,128)(2,1)}, u32[]{:S(2)}) copy-start(bf16[1,1,2,128,128]{4,3,2,1,0:T(8,128)(2,1)} %param.12) | copy-start | bytes 196612
  49.5 1.9 %copy-start.8 = (bf16[128,256]{1,0:T(8,128)(2,1)S(1)}, bf16[128,256]{1,0:T(8,128)(2,1)}, u32[]{:S(2)}) copy-start(bf16[128,256]{1,0:T(8,128)(2,1)} %up_ref.1) | copy-start | bytes 196612
  49.5 1.9 %copy-start.9 = (bf16[256,128]{1,0:T(8,128)(2,1)S(1)}, bf16[256,128]{1,0:T(8,128)(2,1)}, u32[]{:S(2)}) copy-start(bf16[256,128]{1,0:T(8,128)(2,1)} %down_ref.1) | copy-start | bytes 196612
  49.9 1.4 %collective-permute-start.14 = (f32[256,128]{1,0:T(8,128)S(1)}, f32[256,128]{1,0:T(8,128)S(1)}, u32[]{:S(2)}, u32[]{:S(2)}) collective-permute-start(f32[256,128]{1,0:T(8,128)S(1)} %get-tuple-element.18), channel_id=1, source_target_pairs={{0,1},{1,0},{2,3},{3,2},{4,5},{5,4},{6,7},{7,6},{8,9},{9,8},{10,11... | collective-permute-start | bytes 393224 | tf_op jit(solution)/shard_map/ppermute | solution.py:168
  51.3 0.7 %copy-start.13 = (f32[128]{0:T(128)S(1)}, f32[128]{0:T(128)}, u32[]{:S(2)}) copy-start(f32[128]{0:T(128)} %param.19) | copy-start | bytes 1540

commit v3 on v2

--- a/solution.py
+++ b/solution.py
@@ -161,6 +161,8 @@
 LOG2E = 1.4426950408889634
 POS_ROWS = 16
 ROUND = 12582912.0
+PIECE = 2
+VMEM_GRANT = 16 * 2**20
 
 
 def shift(array, axis, step):
@@ -170,7 +172,7 @@
 
 def sin_coefficients():
     nodes = np.cos((np.arange(400) + 0.5) / 400 * np.pi) * 0.25
-    powers = np.stack([nodes ** (2 * n + 1) for n in range(6)], axis=1)
+    powers = np.stack([nodes ** (2 * n + 1) for n in range(5)], axis=1)
     scale = np.abs(powers).max(axis=0)
     fit = np.linalg.lstsq(powers / scale, np.sin(2 * np.pi * nodes), rcond=None)[0] / scale
     return [float(value) for value in fit]
@@ -192,8 +194,9 @@
 
 
 def table_kernel(n_blocks, z_tiles, place_ref, waves_ref, charge_ref, *refs):
-    z_size = len(refs) - 1 - n_blocks
-    columns, table_ref, parts = refs[:z_size], refs[z_size], refs[z_size + 1 :]
+    z_size = len(refs) - 2 - n_blocks
+    columns, copy_ref, table_ref, parts = refs[:z_size], *refs[z_size : z_size + 2], refs[z_size + 2 :]
+    copy_ref[...] = columns[0][...]
     tile = columns[0].shape[2]
     block = waves_ref.shape[1] // n_blocks
     row = lax.broadcasted_iota(jnp.int32, (POS_ROWS, tile), 0)
@@ -288,45 +291,78 @@
     targets = [(-1, before_ref, z_tiles - 1)]
     targets += [(t, own_ref, t) for t in range(z_tiles)]
     targets += [(z_tiles, after_ref, 0)]
-    for index, (tz, ref, at) in enumerate(targets):
+    blocks = [
+        (index, sz)
+        for index, (tz, ref, at) in enumerate(targets)
+        for sz in range(z_tiles)
+        if abs(sz - tz) <= 1
+    ]
+    pooled = {}
+
+    def basis(block_at, slot):
+        index, sz = blocks[block_at]
+        tz, ref, at = targets[index]
+        dx, dy = columns[slot][2:]
         x0, y0, z0 = unit(ref[at, tile : tile + POS_ROWS, :])
-        near = [sz for sz in range(z_tiles) if abs(sz - tz) <= 1]
-        pooled = [None] * NRBF
-        for place, sz in enumerate(near):
-            buffer = radial_ref.at[(index + place) % 2]
-            for slot, (g, c, dx, dy) in enumerate(columns):
-                x, y, z = x0 - dx, y0 - dy, z0 - (sz - tz)
-                high, low = split_norm(x, y, z)
-                one = jnp.ones_like(x)
-                target = rows_of(row, [-2 * x, -2 * y, -2 * z, high, low, one, one])
-                square = lax.dot_general(
-                    target, sources[slot, sz], CONTRACT_FIRST, preferred_element_type=jnp.float32
-                )
-                square = jnp.where(square == 0.0, 1.0, jnp.minimum(square, 1.0))
-                dist = square * lax.rsqrt(square)
-                lack = 1.0 - square
-                value = jnp.exp2(dist * (3.0 * LOG2E - (SHARP * LOG2E) * dist)) * (lack * lack)
-                growth = jnp.exp2(dist * (6.0 * LOG2E))
-                for r in range(NRBF):
-                    buffer[r * tile : (r + 1) * tile, slot * tile : (slot + 1) * tile] = (
-                        value.astype(jnp.bfloat16)
-                    )
-                    if r + 1 < NRBF:
-                        value = value * growth
-            part = jnp.dot(buffer[...], feature_ref[sz], preferred_element_type=jnp.float32)
-            for r in range(NRBF):
-                piece = part[r * tile : (r + 1) * tile, :]
-                pooled[r] = piece if pooled[r] is None else pooled[r] + piece
+        x, y, z = x0 - dx, y0 - dy, z0 - (sz - tz)
+        high, low = split_norm(x, y, z)
+        one = jnp.ones_like(x)
+        target = rows_of(row, [-2 * x, -2 * y, -2 * z, high, low, one, one])
+        square = lax.dot_general(
+            target, sources[slot, sz], CONTRACT_FIRST, preferred_element_type=jnp.float32
+        )
+        square = jnp.where(square == 0.0, 1.0, jnp.minimum(square, 1.0))
+        dist = square * lax.rsqrt(square)
+        lack = 1.0 - square
+        value = jnp.exp2(dist * (3.0 * LOG2E - (SHARP * LOG2E) * dist)) * (lack * lack)
+        growth = jnp.exp2(dist * (6.0 * LOG2E))
+        for r in range(NRBF):
+            radial_ref[
+                block_at % 2, r * tile : (r + 1) * tile, slot * tile : (slot + 1) * tile
+            ] = value.astype(jnp.bfloat16)
+            if r + 1 < NRBF:
+                value = value * growth
+
+    def pool(block_at, r):
+        index, sz = blocks[block_at]
+        part = jnp.dot(
+            radial_ref[block_at % 2, r * tile : (r + PIECE) * tile, :],
+            feature_ref[sz],
+            preferred_element_type=jnp.float32,
+        )
+        for step in range(PIECE):
+            piece = part[step * tile : (step + 1) * tile, :]
+            key = index, r + step
+            pooled[key] = pooled[key] + piece if key in pooled else piece
+
+    def finish(index):
         message = extra_ref[index] if has_extra else None
         for r in range(NRBF):
             level = math.exp(-SHARP * ((r + 0.5) / NRBF) ** 2)
             part = jnp.dot(
-                (pooled[r] * level).astype(jnp.bfloat16),
+                (pooled.pop((index, r)) * level).astype(jnp.bfloat16),
                 mix_ref[r * tile : (r + 1) * tile, :],
                 preferred_element_type=jnp.float32,
             )
             message = part if message is None else message + part
         out_ref[index] = message
+
+    n_pieces = NRBF // PIECE
+    for block_at in range(len(blocks) + 1):
+        work = []
+        if block_at < len(blocks):
+            work += [(slot / len(columns), 0, slot) for slot in range(len(columns))]
+        if block_at > 0:
+            work += [((n + 0.5) / n_pieces, 1, n) for n in range(n_pieces)]
+        for _, kind, n in sorted(work):
+            if kind:
+                pool(block_at - 1, n * PIECE)
+            else:
+                basis(block_at, n)
+        if block_at > 0:
+            index = blocks[block_at - 1][0]
+            if block_at == len(blocks) or blocks[block_at][0] != index:
+                finish(index)
 
 
 def long_kernel(z_tiles, n_blocks, table_ref, message_ref, *refs):
@@ -364,20 +400,29 @@
     refs[-1][...] = updated.astype(jnp.bfloat16)
 
 
-def call(kernel, out_shape, *args, scalars=0, scratch=(), name=None):
+def call(kernel, out_shape, *args, scalars=0, after=(), scratch=(), name=None, keep=True):
     in_vmem = pl.BlockSpec(memory_space=pltpu.VMEM)
+    anywhere = pl.BlockSpec(memory_space=pl.ANY)
+    single = not isinstance(out_shape, (list, tuple))
     held = [pltpu.with_memory_space_constraint(a, pltpu.VMEM) for a in args[scalars:]]
-    args = list(args[:scalars]) + held
-    specs = [pl.BlockSpec(memory_space=pltpu.SMEM)] * scalars
-    single = not isinstance(out_shape, (list, tuple))
+    n_args, n_after = len(args), len(after)
+    if keep:
+        out_shape = jax.tree.map(lambda o: pltpu.VMEM(o.shape, o.dtype), out_shape)
+
+    def body(*refs):
+        kernel(*refs[:n_args], *refs[n_args + n_after :])
+
     return pl.pallas_call(
-        kernel,
-        out_shape=jax.tree.map(lambda o: pltpu.VMEM(o.shape, o.dtype), out_shape),
-        in_specs=specs + [in_vmem] * (len(args) - scalars),
+        body,
+        out_shape=out_shape,
+        in_specs=[pl.BlockSpec(memory_space=pltpu.SMEM)] * scalars
+        + [in_vmem] * len(held)
+        + [anywhere] * n_after,
         out_specs=in_vmem if single else [in_vmem] * len(out_shape),
         scratch_shapes=list(scratch),
+        compiler_params=pltpu.CompilerParams(vmem_limit_bytes=VMEM_GRANT),
         name=name,
-    )(*args)
+    )(*args[:scalars], *held, *after)
 
 
 def fast_device(
@@ -410,9 +455,6 @@
         axis=1,
     )
     column = [payload] + [shift(payload, "gz", -step) for step in range(1, sizes[2])]
-    south, north = shift(payload, "gy", 1), shift(payload, "gy", -1)
-    middle = jnp.stack([south, payload, north])
-
     mine = lax.dynamic_slice_in_dim(wavevectors, place[2] * waves, waves, axis=1)
     mine = jnp.concatenate([mine, mine], axis=1)
     mine = lax.dynamic_slice_in_dim(mine, place[0] * block, waves, axis=1).astype(jnp.float32)
@@ -421,9 +463,9 @@
     mine = jnp.concatenate([mine * fine, mine * coarse], axis=0)
     mine = jnp.pad(mine, ((0, POS_ROWS - 6), (0, 0))).astype(jnp.bfloat16)
 
-    table, *parts = call(
+    later, table, *parts = call(
         functools.partial(table_kernel, n_blocks, z_tiles),
-        [shape((2 * waves, sizes[2] * atoms), jnp.bfloat16)]
+        [shape(payload.shape, payload.dtype), shape((2 * waves, sizes[2] * atoms), jnp.bfloat16)]
         + [shape((2 * block, width), jnp.bfloat16)] * n_blocks,
         place,
         mine,
@@ -432,6 +474,8 @@
         scalars=1,
         name="tables",
     )
+    south, north = shift(later, "gy", 1), shift(later, "gy", -1)
+    middle = jnp.stack([south, later, north])
     arrived = [parts[0]] + [shift(parts[n], "gx", n) for n in range(1, n_blocks)]
     west, east = shift(middle, "gx", 1), shift(middle, "gx", -1)
     line = call(add_kernel, shape((2 * block, width), jnp.bfloat16), *arrived, name="add_line")
@@ -441,7 +485,7 @@
     targets = z_tiles + 2
     before, after = column[-1], column[1 % sizes[2]]
 
-    def messages(sources, offsets, extra, name):
+    def messages(sources, offsets, extra, waits, name):
         n_columns = sum(len(o) for o in offsets)
         extras = [] if extra is None else [extra]
         return call(
@@ -457,10 +501,11 @@
                 pltpu.VMEM((2, NRBF * tile, n_columns * tile), jnp.bfloat16),
                 pltpu.VMEM((z_tiles, n_columns * tile, width), jnp.bfloat16),
             ],
+            after=waits,
             name=name,
         )
 
-    message = messages([middle], [ring[3:6]], None, "radial_near")
+    message = messages([middle], [ring[3:6]], None, [line], "radial_near")
     scale = 1.0 / math.sqrt(atoms * sizes[0] * sizes[1] * sizes[2])
     spot = place[2] * waves + place[0] * block
     mine_filters = lax.dynamic_slice_in_dim(filters, spot, block, axis=0)
@@ -470,10 +515,11 @@
         mine_filters,
         mix_weight,
         *lines,
+        after=[message],
         name="mix",
     )
     blocks = [filtered] + [shift(filtered, "gx", -n) for n in range(1, n_blocks)]
-    message = messages([west, east], [ring[:3], ring[6:]], message, "radial_far")
+    message = messages([west, east], [ring[:3], ring[6:]], message, [filtered], "radial_far")
     sums = call(
         functools.partial(long_kernel, z_tiles, n_blocks),
         [shape((atoms, width), jnp.float32)] * sizes[2],
@@ -491,6 +537,7 @@
         up_weight,
         down_weight,
         *sums,
+        keep=False,
         name="node",
     )
     return updated.reshape(features.shape)

time: 53.3 us -> 40.9 us (0.77)
  local copies, waits for them, and re-layouts: 6.08 us -> 0.97 us
  starting transfers between devices: 22.4 us -> 19.4 us
  Pallas kernels: 13.4 us -> 10.7 us
  waiting for transfers between devices: 8.75 us -> 7.59 us
    unnamed x31 -> x18, local copies, waits for them, and re-layouts: 6.06 us -> 0.96 us
    ppermute x15, starting transfers between devices: 22.4 us -> 19.4 us  [shift(): lax.ppermute(array, axis, [(i, (i + step) % size) for i in range(size)])]
    pallas_call x7, Pallas kernels: 13.4 us -> 10.7 us  [call(): pl.pallas_call(body, out_shape=out_shape, in_specs=[pl.BlockSpec(memory_s...]
    ppermute x15, waiting for transfers between devices: 8.75 us -> 7.59 us  [shift(): lax.ppermute(array, axis, [(i, (i + step) % size) for i in range(size)])]
    another operation x2 -> x1, other arithmetic: 0.89 us -> 0.03 us  [fast_device(): middle = jnp.stack([south, later, north])]
    concatenate x0 -> x1, other arithmetic: none -> 0.84 us  [fast_device(): jnp.concatenate([features.reshape(z_tiles, tile, width), jnp.pad(pos, ((0...]
  transfers between devices with their start and end apart: 15 -> 15, of which waited for: 6 -> 6; matrix products, arithmetic and copies ran while one was open for 1% -> 0% of each run, Pallas kernels for 24% -> 17%
where the time goes in v3:
time: 40.9 us; the launch traced here: 40.6 us
  starting transfers between devices  19.4 us (47%)
  Pallas kernels  10.7 us (26%)
  waiting for transfers between devices  7.59 us (19%)
  other arithmetic  1.73 us (4%)
  local copies, waits for them, and re-layouts  0.97 us (2%)
    ppermute x15, starting transfers between devices, shift(): lax.ppermute(array, axis, [(i, (i + step) % size) for i in range(size)])  19.4 us
    pallas_call x7, Pallas kernels, call(): pl.pallas_call(body, out_shape=out_shape, in_specs=[pl.BlockSpec(memory_s...  10.7 us
    ppermute x15, waiting for transfers between devices, shift(): lax.ppermute(array, axis, [(i, (i + step) % size) for i in range(size)])  7.59 us
    unnamed x18, local copies, waits for them, and re-layouts  0.96 us
    concatenate x1, other arithmetic, fast_device(): jnp.concatenate([features.reshape(z_tiles, tile, width), jnp.pad(pos, ((0...  0.84 us
  transfers between devices with their start and end apart: 15, of which 6 were waited for; matrix products, arithmetic and copies ran while one was open for 0% of the time, Pallas kernels for 17%

profile of v3, /device:TPU:0, one launch (start us, length us, event | category | flops | bytes accessed | tf_op | source)
XLA Modules:
  0.0 40.6 jit_solution(12191094503555827303)
XLA Ops:
  0.0 0.7 %fusion.7 = bf16[2,3,128]{2,1,0:T(4,128)(2,1)S(1)} fusion(s32[3,1,1,2,128]{4,3,2,1,0:T(2,128)} %param.13), kind=kLoop, calls=%fused_computation.15 | loop fusion | flops 768 | bytes 4608 | tf_op jit(solution)/shard_map/convert_element_type | solution.py:449
  0.7 0.8 %fusion.1.refs_3_.refs_0_ = bf16[2,144,128]{2,1,0:T(8,128)(2,1)S(1)} fusion(bf16[2,3,128]{2,1,0:T(4,128)(2,1)S(1)} %fusion.7, bf16[2,128,128]{2,1,0:T(8,128)(2,1)} %bitcast.14), kind=kLoop, calls=%fused_computation.3 | loop fusion | flops 221184 | bytes 140800 | tf_op jit(solution)/shard_map/concatenate | solution.py:450
  1.6 0.5 %collective-permute-start = (bf16[2,144,128]{2,1,0:T(8,128)(2,1)S(1)}, bf16[2,144,128]{2,1,0:T(8,128)(2,1)S(1)}, u32[]{:S(2)}, u32[]{:S(2)}) collective-permute-start(bf16[2,144,128]{2,1,0:T(8,128)(2,1)S(1)} %fusion.1.refs_3_.refs_0_), channel_id=1, source_target_pairs={{0,1},{1,0},{2,3},{3,2},{4,5},{5,4},{6,7},{7,6},{8,9},{9,8},{10,11... | collective-permute-start | bytes 221192 | tf_op jit(solution)/shard_map/ppermute | solution.py:170
  2.1 0.2 copy-done.8
  2.4 0.1 pad_add_fusion.refs_0_
  2.4 0.6 %collective-permute-done.refs_4_.refs_1_.refs_2_ = bf16[2,144,128]{2,1,0:T(8,128)(2,1)S(1)} collective-permute-done((bf16[2,144,128]{2,1,0:T(8,128)(2,1)S(1)}, bf16[2,144,128]{2,1,0:T(8,128)(2,1)S(1)}, u32[]{:S(2)}, u32[]{:S(2)}) %collective-permute-start) | collective-permute-done | bytes 73760 | tf_op jit(solution)/shard_map/ppermute | solution.py:170
  3.0 0.1 copy-done.6
  3.1 2.5 %tables.1 = (bf16[2,144,128]{2,1,0:T(8,128)(2,1)S(1)}, bf16[1024,512]{1,0:T(8,128)(2,1)S(1)}, bf16[256,128]{1,0:T(8,128)(2,1)S(1)}, bf16[256,128]{1,0:T(8,128)(2...) custom-call(s32[3]{0:T(128)S(1)} %pad_add_fusion.refs_0_, bf16[16,512]{1,0:T(8,128)(2,1)S(1)} %fusion.4.refs_1_, ...), custom_call_target="tpu_custom_call" | custom-call | tf_op jit(solution)/shard_map/tables/pallas_call | solution.py:415
  5.6 5.1 %collective-permute-start.2 = (bf16[2,144,128]{2,1,0:T(8,128)(2,1)S(1)}, bf16[2,144,128]{2,1,0:T(8,128)(2,1)S(1)}, u32[]{:S(2)}, u32[]{:S(2)}) collective-permute-start(bf16[2,144,128]{2,1,0:T(8,128)(2,1)S(1)} %get-tuple-element.14), channel_id=1, source_target_pairs={{0,6},{2,0},{4,2},{6,4},{1,7},{3,1},{5,3},{7,5},{8,14},{10,8},{12,... | collective-permute-start | bytes 221192 | tf_op jit(solution)/shard_map/ppermute | solution.py:170
  10.7 1.5 %collective-permute-start.5 = (bf16[256,128]{1,0:T(8,128)(2,1)S(1)}, bf16[256,128]{1,0:T(8,128)(2,1)S(1)}, u32[]{:S(2)}, u32[]{:S(2)}) collective-permute-start(bf16[256,128]{1,0:T(8,128)(2,1)S(1)} %get-tuple-element.16), channel_id=1, source_target_pairs={{0,8},{8,16},{16,24},{24,0},{1,9},{9,17},{17,25},{25,1},{2,10},{10... | collective-permute-start | bytes 196616 | tf_op jit(solution)/shard_map/ppermute | solution.py:170
  12.2 1.5 %collective-permute-start.6 = (bf16[256,128]{1,0:T(8,128)(2,1)S(1)}, bf16[256,128]{1,0:T(8,128)(2,1)S(1)}, u32[]{:S(2)}, u32[]{:S(2)}) collective-permute-start(bf16[256,128]{1,0:T(8,128)(2,1)S(1)} %get-tuple-element.17), channel_id=1, source_target_pairs={{0,16},{8,24},{16,0},{24,8},{1,17},{9,25},{17,1},{25,9},{2,18},{10... | collective-permute-start | bytes 196616 | tf_op jit(solution)/shard_map/ppermute | solution.py:170
  13.7 1.4 %collective-permute-start.7 = (bf16[256,128]{1,0:T(8,128)(2,1)S(1)}, bf16[256,128]{1,0:T(8,128)(2,1)S(1)}, u32[]{:S(2)}, u32[]{:S(2)}) collective-permute-start(bf16[256,128]{1,0:T(8,128)(2,1)S(1)} %get-tuple-element.18), channel_id=1, source_target_pairs={{0,24},{8,0},{16,8},{24,16},{1,25},{9,1},{17,9},{25,17},{2,26},{10... | collective-permute-start | bytes 196616 | tf_op jit(solution)/shard_map/ppermute | solution.py:170
  15.2 1.7 %collective-permute-done.1 = bf16[2,144,128]{2,1,0:T(8,128)(2,1)S(1)} collective-permute-done((bf16[2,144,128]{2,1,0:T(8,128)(2,1)S(1)}, bf16[2,144,128]{2,1,0:T(8,128)(2,1)S(1)}, u32[]{:S(2)}, u32[]{:S(2)}) %collective-permute-start.1) | collective-permute-done | bytes 73760 | tf_op jit(solution)/shard_map/ppermute | solution.py:170
  16.9 1.5 %collective-permute-start.3 = (bf16[3,2,144,128]{3,2,1,0:T(8,128)(2,1)S(1)}, bf16[3,2,144,128]{3,2,1,0:T(8,128)(2,1)S(1)}, u32[]{:S(2)}, u32[]{:S(2)}) collective-permute-start(bf16[3,2,144,128]{3,2,1,0:T(8,128)(2,1)S(1)} %pad_maximum_fusion.refs_3_), channel_id=1, source_target_pairs={{0,8},{8,16},{16,24},{24,0},{1,9},{9,17},{17,25},{25,1},{2,10},{10... | collective-permute-start | bytes 663560 | tf_op jit(solution)/shard_map/ppermute | solution.py:170
  18.4 1.4 %collective-permute-start.4 = (bf16[3,2,144,128]{3,2,1,0:T(8,128)(2,1)S(1)}, bf16[3,2,144,128]{3,2,1,0:T(8,128)(2,1)S(1)}, u32[]{:S(2)}, u32[]{:S(2)}) collective-permute-start(bf16[3,2,144,128]{3,2,1,0:T(8,128)(2,1)S(1)} %pad_maximum_fusion.refs_3_), channel_id=1, source_target_pairs={{0,24},{8,0},{16,8},{24,16},{1,25},{9,1},{17,9},{25,17},{2,26},{10... | collective-permute-start | bytes 663560 | tf_op jit(solution)/shard_map/ppermute | solution.py:170
  19.9 0.0 copy-start.1
  20.0 2.7 %collective-permute-start.10 = (bf16[256,128]{1,0:T(8,128)(2,1)S(1)}, bf16[256,128]{1,0:T(8,128)(2,1)S(1)}, u32[]{:S(2)}, u32[]{:S(2)}) collective-permute-start(bf16[256,128]{1,0:T(8,128)(2,1)S(1)} %add_line.1.refs_5_.refs_2_), channel_id=1, source_target_pairs={{0,6},{2,0},{4,2},{6,4},{1,7},{3,1},{5,3},{7,5},{8,14},{10,8},{12,... | collective-permute-start | bytes 196616 | tf_op jit(solution)/shard_map/ppermute | solution.py:170
  22.6 0.6 %collective-permute-start.9 = (bf16[256,128]{1,0:T(8,128)(2,1)S(1)}, bf16[256,128]{1,0:T(8,128)(2,1)S(1)}, u32[]{:S(2)}, u32[]{:S(2)}) collective-permute-start(bf16[256,128]{1,0:T(8,128)(2,1)S(1)} %add_line.1.refs_5_.refs_2_), channel_id=1, source_target_pairs={{0,4},{2,6},{4,0},{6,2},{1,5},{3,7},{5,1},{7,3},{8,12},{10,14},{12... | collective-permute-start | bytes 196616 | tf_op jit(solution)/shard_map/ppermute | solution.py:170
  23.3 2.3 %radial_near.1.refs_6_ = f32[4,128,128]{2,1,0:T(8,128)S(1)} custom-call(bf16[2,144,128]{2,1,0:T(8,128)(2,1)S(1)} %fusion.1.refs_3_.refs_0_, bf16[2,144,128]{2,1,0:T(8,128)(2,1)S(1)} %collective-permute-done.refs_4_.refs_1_.refs_2_, bf16[2,144,128]{2,1,0:T(8,128)(2,1)S(1)} %collective-permute-done.refs_4_.refs_1_.refs_2_, ...), custom_call_target="tpu_custom_call" | custom-call | tf_op jit(solution)/shard_map/radial_near/pallas_call | solution.py:415
  25.6 0.1 collective-permute-done.10.refs_5_
  25.7 3.0 %collective-permute-done.8.refs_3_ = bf16[256,128]{1,0:T(8,128)(2,1)S(1)} collective-permute-done((bf16[256,128]{1,0:T(8,128)(2,1)S(1)}, bf16[256,128]{1,0:T(8,128)(2,1)S(1)}, u32[]{:S(2)}, u32[]{:S(2)}) %collective-permute-start.8) | collective-permute-done | bytes 65568 | tf_op jit(solution)/shard_map/ppermute | solution.py:170
  28.7 0.3 mix.1.refs_7_.refs_2_
  29.0 2.4 %collective-permute-start.11 = (bf16[256,128]{1,0:T(8,128)(2,1)S(1)}, bf16[256,128]{1,0:T(8,128)(2,1)S(1)}, u32[]{:S(2)}, u32[]{:S(2)}) collective-permute-start(bf16[256,128]{1,0:T(8,128)(2,1)S(1)} %mix.1.refs_7_.refs_2_), channel_id=1, source_target_pairs={{0,24},{8,0},{16,8},{24,16},{1,25},{9,1},{17,9},{25,17},{2,26},{10... | collective-permute-start | bytes 196616 | tf_op jit(solution)/shard_map/ppermute | solution.py:170
  31.4 0.5 %collective-permute-start.12 = (bf16[256,128]{1,0:T(8,128)(2,1)S(1)}, bf16[256,128]{1,0:T(8,128)(2,1)S(1)}, u32[]{:S(2)}, u32[]{:S(2)}) collective-permute-start(bf16[256,128]{1,0:T(8,128)(2,1)S(1)} %mix.1.refs_7_.refs_2_), channel_id=1, source_target_pairs={{0,16},{8,24},{16,0},{24,8},{1,17},{9,25},{17,1},{25,9},{2,18},{10... | collective-permute-start | bytes 196616 | tf_op jit(solution)/shard_map/ppermute | solution.py:170
  31.9 0.1 collective-permute-start.13
  32.0 4.1 %radial_far.1.refs_1_ = f32[4,128,128]{2,1,0:T(8,128)S(1)} custom-call(bf16[2,144,128]{2,1,0:T(8,128)(2,1)S(1)} %fusion.1.refs_3_.refs_0_, bf16[2,144,128]{2,1,0:T(8,128)(2,1)S(1)} %collective-permute-done.refs_4_.refs_1_.refs_2_, bf16[2,144,128]{2,1,0:T(8,128)(2,1)S(1)} %collective-permute-done.refs_4_.refs_1_.refs_2_, ...), custom_call_target="tpu_custom_call" | custom-call | tf_op jit(solution)/shard_map/radial_far/pallas_call | solution.py:415
  36.2 0.9 %collective-permute-done.13.refs_5_ = bf16[256,128]{1,0:T(8,128)(2,1)S(1)} collective-permute-done((bf16[256,128]{1,0:T(8,128)(2,1)S(1)}, bf16[256,128]{1,0:T(8,128)(2,1)S(1)}, u32[]{:S(2)}, u32[]{:S(2)}) %collective-permute-start.13) | collective-permute-done | bytes 65568 | tf_op jit(solution)/shard_map/ppermute | solution.py:170
  37.0 0.4 %longrange.1 = (f32[256,128]{1,0:T(8,128)S(1)}, f32[256,128]{1,0:T(8,128)S(1)}) custom-call(bf16[1024,512]{1,0:T(8,128)(2,1)S(1)} %get-tuple-element.13.refs_0_, f32[4,128,128]{2,1,0:T(8,128)S(1)} %radial_far.1.refs_1_, bf16[256,128]{1,0:T(8,128)(2,1)S(1)} %mix.1.refs_7_.refs_2_, bf16[256,128]{1,0:T(8,128)(2,1)S(1)} %collective-permute-done.11.refs_3_, ...), custom_call_target="tpu_custom_call" | custom-call | tf_op jit(solution)/shard_map/longrange/pallas_call | solution.py:415
  37.5 0.1 collective-permute-start.14
  37.5 1.3 %collective-permute-done.14.refs_5_ = f32[256,128]{1,0:T(8,128)S(1)} collective-permute-done((f32[256,128]{1,0:T(8,128)S(1)}, f32[256,128]{1,0:T(8,128)S(1)}, u32[]{:S(2)}, u32[]{:S(2)}) %collective-permute-start.14) | collective-permute-done | bytes 131104 | tf_op jit(solution)/shard_map/ppermute | solution.py:170
  38.9 0.6 %copy-done.7 = f32[128]{0:T(128)S(1)} copy-done((f32[128]{0:T(128)S(1)}, f32[128]{0:T(128)}, u32[]{:S(2)}) %copy-start.7) | copy-done | bytes 536
  39.5 1.0 %node.1 = bf16[256,128]{1,0:T(8,128)(2,1)} custom-call(bf16[256,128]{1,0:T(8,128)(2,1)S(1)} %bitcast.15, f32[1,128]{1,0:T(1,128)S(1)} %bitcast.17, bf16[128,256]{1,0:T(8,128)(2,1)S(1)} %copy-done.3, bf16[256,128]{1,0:T(8,128)(2,1)S(1)} %copy-done.4, f32[256,128]{1,0:T(8,128)S(1)} %get-tuple-element.19.refs_4_, f32[256,128]{1,0:T(8,128)S(1)} %collective-permute-done.14.refs_5_), custom_call_target="tpu_custom_call" | custom-call | tf_op jit(solution)/shard_map/node/pallas_call | solution.py:415
  (31 shorter events, 0.2 us)
Async XLA Ops:
  0.0 23.3 %copy-start = (f32[1024,128]{1,0:T(8,128)S(1)}, f32[1024,128]{1,0:T(8,128)}, u32[]{:S(2)}) copy-start(f32[1024,128]{1,0:T(8,128)} %param.17) | copy-start | bytes 1572868
  1.6 0.7 %copy-start.8 = (s32[3,1024]{1,0:T(4,128)S(1)}, s32[3,1024]{1,0:T(4,128)}, u32[]{:S(2)}) copy-start(s32[3,1024]{1,0:T(4,128)} %param.14) | copy-start | bytes 36868
  1.6 1.4 %collective-permute-start = (bf16[2,144,128]{2,1,0:T(8,128)(2,1)S(1)}, bf16[2,144,128]{2,1,0:T(8,128)(2,1)S(1)}, u32[]{:S(2)}, u32[]{:S(2)}) collective-permute-start(bf16[2,144,128]{2,1,0:T(8,128)(2,1)S(1)} %fusion.1.refs_3_.refs_0_), channel_id=1, source_target_pairs={{0,1},{1,0},{2,3},{3,2},{4,5},{5,4},{6,7},{7,6},{8,9},{9,8},{10,11... | collective-permute-start | bytes 221192 | tf_op jit(solution)/shard_map/ppermute | solution.py:170
  2.3 0.8 %copy-start.6 = (bf16[128,128]{1,0:T(8,128)(2,1)S(1)}, bf16[128,128]{1,0:T(8,128)(2,1)}, u32[]{:S(2)}) copy-start(bf16[128,128]{1,0:T(8,128)(2,1)} %refs_2_.2) | copy-start | bytes 98308
  5.6 9.6 %collective-permute-start.2 = (bf16[2,144,128]{2,1,0:T(8,128)(2,1)S(1)}, bf16[2,144,128]{2,1,0:T(8,128)(2,1)S(1)}, u32[]{:S(2)}, u32[]{:S(2)}) collective-permute-start(bf16[2,144,128]{2,1,0:T(8,128)(2,1)S(1)} %get-tuple-element.14), channel_id=1, source_target_pairs={{0,6},{2,0},{4,2},{6,4},{1,7},{3,1},{5,3},{7,5},{8,14},{10,8},{12,... | collective-permute-start | bytes 221192 | tf_op jit(solution)/shard_map/ppermute | solution.py:170
  10.7 6.2 %collective-permute-start.1 = (bf16[2,144,128]{2,1,0:T(8,128)(2,1)S(1)}, bf16[2,144,128]{2,1,0:T(8,128)(2,1)S(1)}, u32[]{:S(2)}, u32[]{:S(2)}) collective-permute-start(bf16[2,144,128]{2,1,0:T(8,128)(2,1)S(1)} %get-tuple-element.14), channel_id=1, source_target_pairs={{0,2},{2,4},{4,6},{6,0},{1,3},{3,5},{5,7},{7,1},{8,10},{10,12},{12... | collective-permute-start | bytes 221192 | tf_op jit(solution)/shard_map/ppermute | solution.py:170
  10.7 9.2 %collective-permute-start.5 = (bf16[256,128]{1,0:T(8,128)(2,1)S(1)}, bf16[256,128]{1,0:T(8,128)(2,1)S(1)}, u32[]{:S(2)}, u32[]{:S(2)}) collective-permute-start(bf16[256,128]{1,0:T(8,128)(2,1)S(1)} %get-tuple-element.16), channel_id=1, source_target_pairs={{0,8},{8,16},{16,24},{24,0},{1,9},{9,17},{17,25},{25,1},{2,10},{10... | collective-permute-start | bytes 196616 | tf_op jit(solution)/shard_map/ppermute | solution.py:170
  12.2 7.7 %collective-permute-start.6 = (bf16[256,128]{1,0:T(8,128)(2,1)S(1)}, bf16[256,128]{1,0:T(8,128)(2,1)S(1)}, u32[]{:S(2)}, u32[]{:S(2)}) collective-permute-start(bf16[256,128]{1,0:T(8,128)(2,1)S(1)} %get-tuple-element.17), channel_id=1, source_target_pairs={{0,16},{8,24},{16,0},{24,8},{1,17},{9,25},{17,1},{25,9},{2,18},{10... | collective-permute-start | bytes 196616 | tf_op jit(solution)/shard_map/ppermute | solution.py:170
  13.7 6.2 %collective-permute-start.7 = (bf16[256,128]{1,0:T(8,128)(2,1)S(1)}, bf16[256,128]{1,0:T(8,128)(2,1)S(1)}, u32[]{:S(2)}, u32[]{:S(2)}) collective-permute-start(bf16[256,128]{1,0:T(8,128)(2,1)S(1)} %get-tuple-element.18), channel_id=1, source_target_pairs={{0,24},{8,0},{16,8},{24,16},{1,25},{9,1},{17,9},{25,17},{2,26},{10... | collective-permute-start | bytes 196616 | tf_op jit(solution)/shard_map/ppermute | solution.py:170
  16.9 15.1 %collective-permute-start.3 = (bf16[3,2,144,128]{3,2,1,0:T(8,128)(2,1)S(1)}, bf16[3,2,144,128]{3,2,1,0:T(8,128)(2,1)S(1)}, u32[]{:S(2)}, u32[]{:S(2)}) collective-permute-start(bf16[3,2,144,128]{3,2,1,0:T(8,128)(2,1)S(1)} %pad_maximum_fusion.refs_3_), channel_id=1, source_target_pairs={{0,8},{8,16},{16,24},{24,0},{1,9},{9,17},{17,25},{25,1},{2,10},{10... | collective-permute-start | bytes 663560 | tf_op jit(solution)/shard_map/ppermute | solution.py:170
  18.4 13.6 %collective-permute-start.4 = (bf16[3,2,144,128]{3,2,1,0:T(8,128)(2,1)S(1)}, bf16[3,2,144,128]{3,2,1,0:T(8,128)(2,1)S(1)}, u32[]{:S(2)}, u32[]{:S(2)}) collective-permute-start(bf16[3,2,144,128]{3,2,1,0:T(8,128)(2,1)S(1)} %pad_maximum_fusion.refs_3_), channel_id=1, source_target_pairs={{0,24},{8,0},{16,8},{24,16},{1,25},{9,1},{17,9},{25,17},{2,26},{10... | collective-permute-start | bytes 663560 | tf_op jit(solution)/shard_map/ppermute | solution.py:170
  19.9 3.4 %copy-start.1 = (bf16[768,128]{1,0:T(8,128)(2,1)S(1)}, bf16[768,128]{1,0:T(8,128)(2,1)}, u32[]{:S(2)}) copy-start(bf16[768,128]{1,0:T(8,128)(2,1)} %refs_5_.1) | copy-start | bytes 589828
  20.0 5.7 %collective-permute-start.10 = (bf16[256,128]{1,0:T(8,128)(2,1)S(1)}, bf16[256,128]{1,0:T(8,128)(2,1)S(1)}, u32[]{:S(2)}, u32[]{:S(2)}) collective-permute-start(bf16[256,128]{1,0:T(8,128)(2,1)S(1)} %add_line.1.refs_5_.refs_2_), channel_id=1, source_target_pairs={{0,6},{2,0},{4,2},{6,4},{1,7},{3,1},{5,3},{7,5},{8,14},{10,8},{12,... | collective-permute-start | bytes 196616 | tf_op jit(solution)/shard_map/ppermute | solution.py:170
  22.6 6.1 %collective-permute-start.8 = (bf16[256,128]{1,0:T(8,128)(2,1)S(1)}, bf16[256,128]{1,0:T(8,128)(2,1)S(1)}, u32[]{:S(2)}, u32[]{:S(2)}) collective-permute-start(bf16[256,128]{1,0:T(8,128)(2,1)S(1)} %add_line.1.refs_5_.refs_2_), channel_id=1, source_target_pairs={{0,2},{2,4},{4,6},{6,0},{1,3},{3,5},{5,7},{7,1},{8,10},{10,12},{12... | collective-permute-start | bytes 196616 | tf_op jit(solution)/shard_map/ppermute | solution.py:170
  22.6 6.1 %collective-permute-start.9 = (bf16[256,128]{1,0:T(8,128)(2,1)S(1)}, bf16[256,128]{1,0:T(8,128)(2,1)S(1)}, u32[]{:S(2)}, u32[]{:S(2)}) collective-permute-start(bf16[256,128]{1,0:T(8,128)(2,1)S(1)} %add_line.1.refs_5_.refs_2_), channel_id=1, source_target_pairs={{0,4},{2,6},{4,0},{6,2},{1,5},{3,7},{5,1},{7,3},{8,12},{10,14},{12... | collective-permute-start | bytes 196616 | tf_op jit(solution)/shard_map/ppermute | solution.py:170
  23.3 5.4 %copy-start.5 = (f32[128,128]{1,0:T(8,128)S(1)}, f32[128,128]{1,0:T(8,128)}, u32[]{:S(2)}) copy-start(f32[128,128]{1,0:T(8,128)} %refs_1_.1) | copy-start | bytes 196612
  29.0 7.2 %collective-permute-start.11 = (bf16[256,128]{1,0:T(8,128)(2,1)S(1)}, bf16[256,128]{1,0:T(8,128)(2,1)S(1)}, u32[]{:S(2)}, u32[]{:S(2)}) collective-permute-start(bf16[256,128]{1,0:T(8,128)(2,1)S(1)} %mix.1.refs_7_.refs_2_), channel_id=1, source_target_pairs={{0,24},{8,0},{16,8},{24,16},{1,25},{9,1},{17,9},{25,17},{2,26},{10... | collective-permute-start | bytes 196616 | tf_op jit(solution)/shard_map/ppermute | solution.py:170
  31.4 4.8 %collective-permute-start.12 = (bf16[256,128]{1,0:T(8,128)(2,1)S(1)}, bf16[256,128]{1,0:T(8,128)(2,1)S(1)}, u32[]{:S(2)}, u32[]{:S(2)}) collective-permute-start(bf16[256,128]{1,0:T(8,128)(2,1)S(1)} %mix.1.refs_7_.refs_2_), channel_id=1, source_target_pairs={{0,16},{8,24},{16,0},{24,8},{1,17},{9,25},{17,1},{25,9},{2,18},{10... | collective-permute-start | bytes 196616 | tf_op jit(solution)/shard_map/ppermute | solution.py:170
  31.9 5.2 %collective-permute-start.13 = (bf16[256,128]{1,0:T(8,128)(2,1)S(1)}, bf16[256,128]{1,0:T(8,128)(2,1)S(1)}, u32[]{:S(2)}, u32[]{:S(2)}) collective-permute-start(bf16[256,128]{1,0:T(8,128)(2,1)S(1)} %mix.1.refs_7_.refs_2_), channel_id=1, source_target_pairs={{0,8},{8,16},{16,24},{24,0},{1,9},{9,17},{17,25},{25,1},{2,10},{10... | collective-permute-start | bytes 196616 | tf_op jit(solution)/shard_map/ppermute | solution.py:170
  37.0 1.9 %copy-start.2 = (bf16[1,1,2,128,128]{4,3,2,1,0:T(8,128)(2,1)S(1)}, bf16[1,1,2,128,128]{4,3,2,1,0:T(8,128)(2,1)}, u32[]{:S(2)}) copy-start(bf16[1,1,2,128,128]{4,3,2,1,0:T(8,128)(2,1)} %param.12) | copy-start | bytes 196612
  37.0 1.9 %copy-start.3 = (bf16[128,256]{1,0:T(8,128)(2,1)S(1)}, bf16[128,256]{1,0:T(8,128)(2,1)}, u32[]{:S(2)}) copy-start(bf16[128,256]{1,0:T(8,128)(2,1)} %refs_2_.3) | copy-start | bytes 196612
  37.0 1.9 %copy-start.4 = (bf16[256,128]{1,0:T(8,128)(2,1)S(1)}, bf16[256,128]{1,0:T(8,128)(2,1)}, u32[]{:S(2)}) copy-start(bf16[256,128]{1,0:T(8,128)(2,1)} %refs_3_.1) | copy-start | bytes 196612
  37.5 1.4 %collective-permute-start.14 = (f32[256,128]{1,0:T(8,128)S(1)}, f32[256,128]{1,0:T(8,128)S(1)}, u32[]{:S(2)}, u32[]{:S(2)}) collective-permute-start(f32[256,128]{1,0:T(8,128)S(1)} %get-tuple-element.20), channel_id=1, source_target_pairs={{0,1},{1,0},{2,3},{3,2},{4,5},{5,4},{6,7},{7,6},{8,9},{9,8},{10,11... | collective-permute-start | bytes 393224 | tf_op jit(solution)/shard_map/ppermute | solution.py:170
  38.9 0.7 %copy-start.7 = (f32[128]{0:T(128)S(1)}, f32[128]{0:T(128)}, u32[]{:S(2)}) copy-start(f32[128]{0:T(128)} %param.19) | copy-start | bytes 1540

commit v4 on v3

--- a/solution.py
+++ b/solution.py
@@ -400,7 +400,7 @@
     refs[-1][...] = updated.astype(jnp.bfloat16)
 
 
-def call(kernel, out_shape, *args, scalars=0, after=(), scratch=(), name=None, keep=True):
+def call(kernel, out_shape, *args, scalars=0, after=(), scratch=(), keep=True):
     in_vmem = pl.BlockSpec(memory_space=pltpu.VMEM)
     anywhere = pl.BlockSpec(memory_space=pl.ANY)
     single = not isinstance(out_shape, (list, tuple))
@@ -421,7 +421,6 @@
         out_specs=in_vmem if single else [in_vmem] * len(out_shape),
         scratch_shapes=list(scratch),
         compiler_params=pltpu.CompilerParams(vmem_limit_bytes=VMEM_GRANT),
-        name=name,
     )(*args[:scalars], *held, *after)
 
 
@@ -472,20 +471,19 @@
         charge_weight,
         *column,
         scalars=1,
-        name="tables",
     )
     south, north = shift(later, "gy", 1), shift(later, "gy", -1)
     middle = jnp.stack([south, later, north])
     arrived = [parts[0]] + [shift(parts[n], "gx", n) for n in range(1, n_blocks)]
     west, east = shift(middle, "gx", 1), shift(middle, "gx", -1)
-    line = call(add_kernel, shape((2 * block, width), jnp.bfloat16), *arrived, name="add_line")
+    line = call(add_kernel, shape((2 * block, width), jnp.bfloat16), *arrived)
     lines = [line] + [shift(line, "gy", n) for n in range(1, sizes[1])]
 
     ring = [(dx, dy) for dx in (-1, 0, 1) for dy in (-1, 0, 1)]
     targets = z_tiles + 2
     before, after = column[-1], column[1 % sizes[2]]
 
-    def messages(sources, offsets, extra, waits, name):
+    def messages(sources, offsets, extra, waits):
         n_columns = sum(len(o) for o in offsets)
         extras = [] if extra is None else [extra]
         return call(
@@ -502,10 +500,9 @@
                 pltpu.VMEM((z_tiles, n_columns * tile, width), jnp.bfloat16),
             ],
             after=waits,
-            name=name,
-        )
-
-    message = messages([middle], [ring[3:6]], None, [line], "radial_near")
+        )
+
+    message = messages([middle], [ring[3:6]], None, [line])
     scale = 1.0 / math.sqrt(atoms * sizes[0] * sizes[1] * sizes[2])
     spot = place[2] * waves + place[0] * block
     mine_filters = lax.dynamic_slice_in_dim(filters, spot, block, axis=0)
@@ -516,17 +513,16 @@
         mix_weight,
         *lines,
         after=[message],
-        name="mix",
     )
     blocks = [filtered] + [shift(filtered, "gx", -n) for n in range(1, n_blocks)]
-    message = messages([west, east], [ring[:3], ring[6:]], message, [filtered], "radial_far")
+    message = messages([west], [ring[:3]], message, [filtered])
+    message = messages([east], [ring[6:]], message, [])
     sums = call(
         functools.partial(long_kernel, z_tiles, n_blocks),
         [shape((atoms, width), jnp.float32)] * sizes[2],
         table,
         message,
         *blocks,
-        name="longrange",
     )
     sums = [sums[0]] + [shift(sums[step], "gz", step) for step in range(1, sizes[2])]
     updated = call(
@@ -538,7 +534,6 @@
         down_weight,
         *sums,
         keep=False,
-        name="node",
     )
     return updated.reshape(features.shape)
 
@@ -572,10 +567,18 @@
     )
     out_specs = P("gx", "gy", "gz", None, None)
 
+    def fast(*args):
+        return fast_device(*args)
+
     def layer(*args):
-        body = fast_device if fits(mesh, args[0].shape, args[2].shape) else on_device
-        return jax.shard_map(
-            body, mesh=mesh, in_specs=in_specs, out_specs=out_specs, check_vma=False
-        )(*args)
+        quick = fits(mesh, args[0].shape, args[2].shape)
+        mapped = jax.shard_map(
+            fast if quick else on_device,
+            mesh=mesh,
+            in_specs=in_specs,
+            out_specs=out_specs,
+            check_vma=False,
+        )
+        return mapped(*args)
 
     return layer

time: 40.9 us -> 40.9 us (level)
  Pallas kernels: 10.7 us -> 11.2 us
  waiting for transfers between devices: 7.59 us -> 7.1 us
    ppermute x15, waiting for transfers between devices: 7.59 us -> 7.1 us  [shift(): lax.ppermute(array, axis, [(i, (i + step) % size) for i in range(size)])]
    pallas_call x7 -> x8, Pallas kernels: 10.7 us -> 11.2 us  [call(): pl.pallas_call(body, out_shape=out_shape, in_specs=[pl.BlockSpec(memory_s...]
  transfers between devices with their start and end apart: 15 -> 15, of which waited for: 6 -> 6; matrix products, arithmetic and copies ran while one was open for 0% -> 0% of each run, Pallas kernels for 17% -> 18%
where the time goes in v4:
time: 40.9 us; the launch traced here: 40.6 us
  starting transfers between devices  19.4 us (47%)
  Pallas kernels  11.2 us (27%)
  waiting for transfers between devices  7.1 us (17%)
  other arithmetic  1.73 us (4%)
  local copies, waits for them, and re-layouts  0.97 us (2%)
    ppermute x15, starting transfers between devices, shift(): lax.ppermute(array, axis, [(i, (i + step) % size) for i in range(size)])  19.4 us
    pallas_call x8, Pallas kernels, call(): pl.pallas_call(body, out_shape=out_shape, in_specs=[pl.BlockSpec(memory_s...  11.2 us
    ppermute x15, waiting for transfers between devices, shift(): lax.ppermute(array, axis, [(i, (i + step) % size) for i in range(size)])  7.1 us
    unnamed x18, local copies, waits for them, and re-layouts  0.96 us
    concatenate x1, other arithmetic, fast_device(): jnp.concatenate([features.reshape(z_tiles, tile, width), jnp.pad(pos, ((0...  0.84 us
  transfers between devices with their start and end apart: 15, of which 6 were waited for; matrix products, arithmetic and copies ran while one was open for 0% of the time, Pallas kernels for 18%

profile of v4, /device:TPU:0, one launch (start us, length us, event | category | flops | bytes accessed | tf_op | source)
XLA Modules:
  0.0 40.6 jit_solution(11519341894492214852)
XLA Ops:
  0.0 0.7 %fusion.7 = bf16[2,3,128]{2,1,0:T(4,128)(2,1)S(1)} fusion(s32[3,1,1,2,128]{4,3,2,1,0:T(2,128)} %param.13), kind=kLoop, calls=%fused_computation.15 | loop fusion | flops 768 | bytes 4608 | tf_op jit(solution)/shard_map/convert_element_type | solution.py:448
  0.7 0.8 %fusion.1.refs_3_.refs_0_ = bf16[2,144,128]{2,1,0:T(8,128)(2,1)S(1)} fusion(bf16[2,3,128]{2,1,0:T(4,128)(2,1)S(1)} %fusion.7, bf16[2,128,128]{2,1,0:T(8,128)(2,1)} %bitcast.14), kind=kLoop, calls=%fused_computation.3 | loop fusion | flops 221184 | bytes 140800 | tf_op jit(solution)/shard_map/concatenate | solution.py:449
  1.6 0.5 %collective-permute-start = (bf16[2,144,128]{2,1,0:T(8,128)(2,1)S(1)}, bf16[2,144,128]{2,1,0:T(8,128)(2,1)S(1)}, u32[]{:S(2)}, u32[]{:S(2)}) collective-permute-start(bf16[2,144,128]{2,1,0:T(8,128)(2,1)S(1)} %fusion.1.refs_3_.refs_0_), channel_id=1, source_target_pairs={{0,1},{1,0},{2,3},{3,2},{4,5},{5,4},{6,7},{7,6},{8,9},{9,8},{10,11... | collective-permute-start | bytes 221192 | tf_op jit(solution)/shard_map/ppermute | solution.py:170
  2.1 0.2 copy-done.8
  2.4 0.1 pad_add_fusion.refs_0_
  2.4 0.6 %collective-permute-done.refs_4_.refs_1_.refs_2_ = bf16[2,144,128]{2,1,0:T(8,128)(2,1)S(1)} collective-permute-done((bf16[2,144,128]{2,1,0:T(8,128)(2,1)S(1)}, bf16[2,144,128]{2,1,0:T(8,128)(2,1)S(1)}, u32[]{:S(2)}, u32[]{:S(2)}) %collective-permute-start) | collective-permute-done | bytes 73760 | tf_op jit(solution)/shard_map/ppermute | solution.py:170
  3.0 0.1 copy-done.6
  3.1 2.5 %shard_map.118 = (bf16[2,144,128]{2,1,0:T(8,128)(2,1)S(1)}, bf16[1024,512]{1,0:T(8,128)(2,1)S(1)}, bf16[256,128]{1,0:T(8,128)(2,1)S(1)}, bf16[256,128]{1,0:T(8,1...) custom-call(s32[3]{0:T(128)S(1)} %pad_add_fusion.refs_0_, bf16[16,512]{1,0:T(8,128)(2,1)S(1)} %fusion.4.refs_1_, ...), custom_call_target="tpu_custom_call" | custom-call | tf_op jit(solution)/shard_map/pallas_call | solution.py:415
  5.6 5.1 %collective-permute-start.2 = (bf16[2,144,128]{2,1,0:T(8,128)(2,1)S(1)}, bf16[2,144,128]{2,1,0:T(8,128)(2,1)S(1)}, u32[]{:S(2)}, u32[]{:S(2)}) collective-permute-start(bf16[2,144,128]{2,1,0:T(8,128)(2,1)S(1)} %get-tuple-element.14), channel_id=1, source_target_pairs={{0,6},{2,0},{4,2},{6,4},{1,7},{3,1},{5,3},{7,5},{8,14},{10,8},{12,... | collective-permute-start | bytes 221192 | tf_op jit(solution)/shard_map/ppermute | solution.py:170
  10.7 1.5 %collective-permute-start.5 = (bf16[256,128]{1,0:T(8,128)(2,1)S(1)}, bf16[256,128]{1,0:T(8,128)(2,1)S(1)}, u32[]{:S(2)}, u32[]{:S(2)}) collective-permute-start(bf16[256,128]{1,0:T(8,128)(2,1)S(1)} %get-tuple-element.16), channel_id=1, source_target_pairs={{0,8},{8,16},{16,24},{24,0},{1,9},{9,17},{17,25},{25,1},{2,10},{10... | collective-permute-start | bytes 196616 | tf_op jit(solution)/shard_map/ppermute | solution.py:170
  12.2 1.5 %collective-permute-start.6 = (bf16[256,128]{1,0:T(8,128)(2,1)S(1)}, bf16[256,128]{1,0:T(8,128)(2,1)S(1)}, u32[]{:S(2)}, u32[]{:S(2)}) collective-permute-start(bf16[256,128]{1,0:T(8,128)(2,1)S(1)} %get-tuple-element.17), channel_id=1, source_target_pairs={{0,16},{8,24},{16,0},{24,8},{1,17},{9,25},{17,1},{25,9},{2,18},{10... | collective-permute-start | bytes 196616 | tf_op jit(solution)/shard_map/ppermute | solution.py:170
  13.7 1.4 %collective-permute-start.7 = (bf16[256,128]{1,0:T(8,128)(2,1)S(1)}, bf16[256,128]{1,0:T(8,128)(2,1)S(1)}, u32[]{:S(2)}, u32[]{:S(2)}) collective-permute-start(bf16[256,128]{1,0:T(8,128)(2,1)S(1)} %get-tuple-element.18), channel_id=1, source_target_pairs={{0,24},{8,0},{16,8},{24,16},{1,25},{9,1},{17,9},{25,17},{2,26},{10... | collective-permute-start | bytes 196616 | tf_op jit(solution)/shard_map/ppermute | solution.py:170
  15.2 1.7 %collective-permute-done.1 = bf16[2,144,128]{2,1,0:T(8,128)(2,1)S(1)} collective-permute-done((bf16[2,144,128]{2,1,0:T(8,128)(2,1)S(1)}, bf16[2,144,128]{2,1,0:T(8,128)(2,1)S(1)}, u32[]{:S(2)}, u32[]{:S(2)}) %collective-permute-start.1) | collective-permute-done | bytes 73760 | tf_op jit(solution)/shard_map/ppermute | solution.py:170
  16.9 1.5 %collective-permute-start.4 = (bf16[3,2,144,128]{3,2,1,0:T(8,128)(2,1)S(1)}, bf16[3,2,144,128]{3,2,1,0:T(8,128)(2,1)S(1)}, u32[]{:S(2)}, u32[]{:S(2)}) collective-permute-start(bf16[3,2,144,128]{3,2,1,0:T(8,128)(2,1)S(1)} %pad_maximum_fusion.refs_3_), channel_id=1, source_target_pairs={{0,8},{8,16},{16,24},{24,0},{1,9},{9,17},{17,25},{25,1},{2,10},{10... | collective-permute-start | bytes 663560 | tf_op jit(solution)/shard_map/ppermute | solution.py:170
  18.4 1.4 %collective-permute-start.3 = (bf16[3,2,144,128]{3,2,1,0:T(8,128)(2,1)S(1)}, bf16[3,2,144,128]{3,2,1,0:T(8,128)(2,1)S(1)}, u32[]{:S(2)}, u32[]{:S(2)}) collective-permute-start(bf16[3,2,144,128]{3,2,1,0:T(8,128)(2,1)S(1)} %pad_maximum_fusion.refs_3_), channel_id=1, source_target_pairs={{0,24},{8,0},{16,8},{24,16},{1,25},{9,1},{17,9},{25,17},{2,26},{10... | collective-permute-start | bytes 663560 | tf_op jit(solution)/shard_map/ppermute | solution.py:170
  20.0 2.7 %collective-permute-start.10 = (bf16[256,128]{1,0:T(8,128)(2,1)S(1)}, bf16[256,128]{1,0:T(8,128)(2,1)S(1)}, u32[]{:S(2)}, u32[]{:S(2)}) collective-permute-start(bf16[256,128]{1,0:T(8,128)(2,1)S(1)} %shard_map.119.refs_5_.refs_2_), channel_id=1, source_target_pairs={{0,6},{2,0},{4,2},{6,4},{1,7},{3,1},{5,3},{7,5},{8,14},{10,8},{12,... | collective-permute-start | bytes 196616 | tf_op jit(solution)/shard_map/ppermute | solution.py:170
  22.6 0.6 %collective-permute-start.9 = (bf16[256,128]{1,0:T(8,128)(2,1)S(1)}, bf16[256,128]{1,0:T(8,128)(2,1)S(1)}, u32[]{:S(2)}, u32[]{:S(2)}) collective-permute-start(bf16[256,128]{1,0:T(8,128)(2,1)S(1)} %shard_map.119.refs_5_.refs_2_), channel_id=1, source_target_pairs={{0,4},{2,6},{4,0},{6,2},{1,5},{3,7},{5,1},{7,3},{8,12},{10,14},{12... | collective-permute-start | bytes 196616 | tf_op jit(solution)/shard_map/ppermute | solution.py:170
  23.3 2.3 %shard_map.120.refs_6_.refs_5_ = f32[4,128,128]{2,1,0:T(8,128)S(1)} custom-call(bf16[2,144,128]{2,1,0:T(8,128)(2,1)S(1)} %fusion.1.refs_3_.refs_0_, bf16[2,144,128]{2,1,0:T(8,128)(2,1)S(1)} %collective-permute-done.refs_4_.refs_1_.refs_2_, bf16[2,144,128]{2,1,0:T(8,128)(2,1)S(1)} %collective-permute-done.refs_4_.refs_1_.refs_2_, ...), custom_call_target="tpu_custom_call" | custom-call | tf_op jit(solution)/shard_map/pallas_call | solution.py:415
  25.6 0.1 collective-permute-done.10.refs_5_
  25.7 3.0 %collective-permute-done.8.refs_3_ = bf16[256,128]{1,0:T(8,128)(2,1)S(1)} collective-permute-done((bf16[256,128]{1,0:T(8,128)(2,1)S(1)}, bf16[256,128]{1,0:T(8,128)(2,1)S(1)}, u32[]{:S(2)}, u32[]{:S(2)}) %collective-permute-start.8) | collective-permute-done | bytes 65568 | tf_op jit(solution)/shard_map/ppermute | solution.py:170
  28.7 0.3 shard_map.121.refs_6_.refs_2_
  29.0 2.4 %collective-permute-start.11 = (bf16[256,128]{1,0:T(8,128)(2,1)S(1)}, bf16[256,128]{1,0:T(8,128)(2,1)S(1)}, u32[]{:S(2)}, u32[]{:S(2)}) collective-permute-start(bf16[256,128]{1,0:T(8,128)(2,1)S(1)} %shard_map.121.refs_6_.refs_2_), channel_id=1, source_target_pairs={{0,24},{8,0},{16,8},{24,16},{1,25},{9,1},{17,9},{25,17},{2,26},{10... | collective-permute-start | bytes 196616 | tf_op jit(solution)/shard_map/ppermute | solution.py:170
  31.4 0.5 %collective-permute-start.12 = (bf16[256,128]{1,0:T(8,128)(2,1)S(1)}, bf16[256,128]{1,0:T(8,128)(2,1)S(1)}, u32[]{:S(2)}, u32[]{:S(2)}) collective-permute-start(bf16[256,128]{1,0:T(8,128)(2,1)S(1)} %shard_map.121.refs_6_.refs_2_), channel_id=1, source_target_pairs={{0,16},{8,24},{16,0},{24,8},{1,17},{9,25},{17,1},{25,9},{2,18},{10... | collective-permute-start | bytes 196616 | tf_op jit(solution)/shard_map/ppermute | solution.py:170
  31.9 0.1 collective-permute-start.13
  32.0 2.3 %shard_map.122.refs_5_ = f32[4,128,128]{2,1,0:T(8,128)S(1)} custom-call(bf16[2,144,128]{2,1,0:T(8,128)(2,1)S(1)} %fusion.1.refs_3_.refs_0_, bf16[2,144,128]{2,1,0:T(8,128)(2,1)S(1)} %collective-permute-done.refs_4_.refs_1_.refs_2_, bf16[2,144,128]{2,1,0:T(8,128)(2,1)S(1)} %collective-permute-done.refs_4_.refs_1_.refs_2_, ...), custom_call_target="tpu_custom_call" | custom-call | tf_op jit(solution)/shard_map/pallas_call | solution.py:415
  34.3 2.3 %shard_map.123.refs_1_ = f32[4,128,128]{2,1,0:T(8,128)S(1)} custom-call(bf16[2,144,128]{2,1,0:T(8,128)(2,1)S(1)} %fusion.1.refs_3_.refs_0_, bf16[2,144,128]{2,1,0:T(8,128)(2,1)S(1)} %collective-permute-done.refs_4_.refs_1_.refs_2_, bf16[2,144,128]{2,1,0:T(8,128)(2,1)S(1)} %collective-permute-done.refs_4_.refs_1_.refs_2_, ...), custom_call_target="tpu_custom_call" | custom-call | tf_op jit(solution)/shard_map/pallas_call | solution.py:415
  36.6 0.4 collective-permute-done.13.refs_5_
  37.0 0.4 %shard_map.124 = (f32[256,128]{1,0:T(8,128)S(1)}, f32[256,128]{1,0:T(8,128)S(1)}) custom-call(bf16[1024,512]{1,0:T(8,128)(2,1)S(1)} %get-tuple-element.13.refs_0_, f32[4,128,128]{2,1,0:T(8,128)S(1)} %shard_map.123.refs_1_, bf16[256,128]{1,0:T(8,128)(2,1)S(1)} %shard_map.121.refs_6_.refs_2_, bf16[256,128]{1,0:T(8,128)(2,1)S(1)} %collective-permute-done.11.refs_3_, ...), custom_call_target="tpu_custom_call" | custom-call | tf_op jit(solution)/shard_map/pallas_call | solution.py:415
  37.5 0.1 collective-permute-start.14
  37.5 1.3 %collective-permute-done.14.refs_5_ = f32[256,128]{1,0:T(8,128)S(1)} collective-permute-done((f32[256,128]{1,0:T(8,128)S(1)}, f32[256,128]{1,0:T(8,128)S(1)}, u32[]{:S(2)}, u32[]{:S(2)}) %collective-permute-start.14) | collective-permute-done | bytes 131104 | tf_op jit(solution)/shard_map/ppermute | solution.py:170
  38.9 0.6 %copy-done.7 = f32[128]{0:T(128)S(1)} copy-done((f32[128]{0:T(128)S(1)}, f32[128]{0:T(128)}, u32[]{:S(2)}) %copy-start.7) | copy-done | bytes 536
  39.5 1.0 %shard_map.125 = bf16[256,128]{1,0:T(8,128)(2,1)} custom-call(bf16[256,128]{1,0:T(8,128)(2,1)S(1)} %bitcast.15, f32[1,128]{1,0:T(1,128)S(1)} %bitcast.17, bf16[128,256]{1,0:T(8,128)(2,1)S(1)} %copy-done.3, bf16[256,128]{1,0:T(8,128)(2,1)S(1)} %copy-done.4, f32[256,128]{1,0:T(8,128)S(1)} %get-tuple-element.19.refs_4_, ...), custom_call_target="tpu_custom_call" | custom-call | tf_op jit(solution)/shard_map/pallas_call | solution.py:415
  (32 shorter events, 0.2 us)
Async XLA Ops:
  0.0 23.3 %copy-start = (f32[1024,128]{1,0:T(8,128)S(1)}, f32[1024,128]{1,0:T(8,128)}, u32[]{:S(2)}) copy-start(f32[1024,128]{1,0:T(8,128)} %param.17) | copy-start | bytes 1572868
  1.6 0.7 %copy-start.8 = (s32[3,1024]{1,0:T(4,128)S(1)}, s32[3,1024]{1,0:T(4,128)}, u32[]{:S(2)}) copy-start(s32[3,1024]{1,0:T(4,128)} %param.14) | copy-start | bytes 36868
  1.6 1.4 %collective-permute-start = (bf16[2,144,128]{2,1,0:T(8,128)(2,1)S(1)}, bf16[2,144,128]{2,1,0:T(8,128)(2,1)S(1)}, u32[]{:S(2)}, u32[]{:S(2)}) collective-permute-start(bf16[2,144,128]{2,1,0:T(8,128)(2,1)S(1)} %fusion.1.refs_3_.refs_0_), channel_id=1, source_target_pairs={{0,1},{1,0},{2,3},{3,2},{4,5},{5,4},{6,7},{7,6},{8,9},{9,8},{10,11... | collective-permute-start | bytes 221192 | tf_op jit(solution)/shard_map/ppermute | solution.py:170
  2.3 0.8 %copy-start.6 = (bf16[128,128]{1,0:T(8,128)(2,1)S(1)}, bf16[128,128]{1,0:T(8,128)(2,1)}, u32[]{:S(2)}) copy-start(bf16[128,128]{1,0:T(8,128)(2,1)} %refs_2_.2) | copy-start | bytes 98308
  5.6 9.6 %collective-permute-start.2 = (bf16[2,144,128]{2,1,0:T(8,128)(2,1)S(1)}, bf16[2,144,128]{2,1,0:T(8,128)(2,1)S(1)}, u32[]{:S(2)}, u32[]{:S(2)}) collective-permute-start(bf16[2,144,128]{2,1,0:T(8,128)(2,1)S(1)} %get-tuple-element.14), channel_id=1, source_target_pairs={{0,6},{2,0},{4,2},{6,4},{1,7},{3,1},{5,3},{7,5},{8,14},{10,8},{12,... | collective-permute-start | bytes 221192 | tf_op jit(solution)/shard_map/ppermute | solution.py:170
  10.7 6.2 %collective-permute-start.1 = (bf16[2,144,128]{2,1,0:T(8,128)(2,1)S(1)}, bf16[2,144,128]{2,1,0:T(8,128)(2,1)S(1)}, u32[]{:S(2)}, u32[]{:S(2)}) collective-permute-start(bf16[2,144,128]{2,1,0:T(8,128)(2,1)S(1)} %get-tuple-element.14), channel_id=1, source_target_pairs={{0,2},{2,4},{4,6},{6,0},{1,3},{3,5},{5,7},{7,1},{8,10},{10,12},{12... | collective-permute-start | bytes 221192 | tf_op jit(solution)/shard_map/ppermute | solution.py:170
  10.7 9.2 %collective-permute-start.5 = (bf16[256,128]{1,0:T(8,128)(2,1)S(1)}, bf16[256,128]{1,0:T(8,128)(2,1)S(1)}, u32[]{:S(2)}, u32[]{:S(2)}) collective-permute-start(bf16[256,128]{1,0:T(8,128)(2,1)S(1)} %get-tuple-element.16), channel_id=1, source_target_pairs={{0,8},{8,16},{16,24},{24,0},{1,9},{9,17},{17,25},{25,1},{2,10},{10... | collective-permute-start | bytes 196616 | tf_op jit(solution)/shard_map/ppermute | solution.py:170
  12.2 7.7 %collective-permute-start.6 = (bf16[256,128]{1,0:T(8,128)(2,1)S(1)}, bf16[256,128]{1,0:T(8,128)(2,1)S(1)}, u32[]{:S(2)}, u32[]{:S(2)}) collective-permute-start(bf16[256,128]{1,0:T(8,128)(2,1)S(1)} %get-tuple-element.17), channel_id=1, source_target_pairs={{0,16},{8,24},{16,0},{24,8},{1,17},{9,25},{17,1},{25,9},{2,18},{10... | collective-permute-start | bytes 196616 | tf_op jit(solution)/shard_map/ppermute | solution.py:170
  13.7 6.2 %collective-permute-start.7 = (bf16[256,128]{1,0:T(8,128)(2,1)S(1)}, bf16[256,128]{1,0:T(8,128)(2,1)S(1)}, u32[]{:S(2)}, u32[]{:S(2)}) collective-permute-start(bf16[256,128]{1,0:T(8,128)(2,1)S(1)} %get-tuple-element.18), channel_id=1, source_target_pairs={{0,24},{8,0},{16,8},{24,16},{1,25},{9,1},{17,9},{25,17},{2,26},{10... | collective-permute-start | bytes 196616 | tf_op jit(solution)/shard_map/ppermute | solution.py:170
  16.9 15.1 %collective-permute-start.4 = (bf16[3,2,144,128]{3,2,1,0:T(8,128)(2,1)S(1)}, bf16[3,2,144,128]{3,2,1,0:T(8,128)(2,1)S(1)}, u32[]{:S(2)}, u32[]{:S(2)}) collective-permute-start(bf16[3,2,144,128]{3,2,1,0:T(8,128)(2,1)S(1)} %pad_maximum_fusion.refs_3_), channel_id=1, source_target_pairs={{0,8},{8,16},{16,24},{24,0},{1,9},{9,17},{17,25},{25,1},{2,10},{10... | collective-permute-start | bytes 663560 | tf_op jit(solution)/shard_map/ppermute | solution.py:170
  18.4 15.9 %collective-permute-start.3 = (bf16[3,2,144,128]{3,2,1,0:T(8,128)(2,1)S(1)}, bf16[3,2,144,128]{3,2,1,0:T(8,128)(2,1)S(1)}, u32[]{:S(2)}, u32[]{:S(2)}) collective-permute-start(bf16[3,2,144,128]{3,2,1,0:T(8,128)(2,1)S(1)} %pad_maximum_fusion.refs_3_), channel_id=1, source_target_pairs={{0,24},{8,0},{16,8},{24,16},{1,25},{9,1},{17,9},{25,17},{2,26},{10... | collective-permute-start | bytes 663560 | tf_op jit(solution)/shard_map/ppermute | solution.py:170
  19.9 3.4 %copy-start.1 = (bf16[768,128]{1,0:T(8,128)(2,1)S(1)}, bf16[768,128]{1,0:T(8,128)(2,1)}, u32[]{:S(2)}) copy-start(bf16[768,128]{1,0:T(8,128)(2,1)} %refs_4_.5) | copy-start | bytes 589828
  20.0 5.7 %collective-permute-start.10 = (bf16[256,128]{1,0:T(8,128)(2,1)S(1)}, bf16[256,128]{1,0:T(8,128)(2,1)S(1)}, u32[]{:S(2)}, u32[]{:S(2)}) collective-permute-start(bf16[256,128]{1,0:T(8,128)(2,1)S(1)} %shard_map.119.refs_5_.refs_2_), channel_id=1, source_target_pairs={{0,6},{2,0},{4,2},{6,4},{1,7},{3,1},{5,3},{7,5},{8,14},{10,8},{12,... | collective-permute-start | bytes 196616 | tf_op jit(solution)/shard_map/ppermute | solution.py:170
  22.6 6.1 %collective-permute-start.8 = (bf16[256,128]{1,0:T(8,128)(2,1)S(1)}, bf16[256,128]{1,0:T(8,128)(2,1)S(1)}, u32[]{:S(2)}, u32[]{:S(2)}) collective-permute-start(bf16[256,128]{1,0:T(8,128)(2,1)S(1)} %shard_map.119.refs_5_.refs_2_), channel_id=1, source_target_pairs={{0,2},{2,4},{4,6},{6,0},{1,3},{3,5},{5,7},{7,1},{8,10},{10,12},{12... | collective-permute-start | bytes 196616 | tf_op jit(solution)/shard_map/ppermute | solution.py:170
  22.6 6.1 %collective-permute-start.9 = (bf16[256,128]{1,0:T(8,128)(2,1)S(1)}, bf16[256,128]{1,0:T(8,128)(2,1)S(1)}, u32[]{:S(2)}, u32[]{:S(2)}) collective-permute-start(bf16[256,128]{1,0:T(8,128)(2,1)S(1)} %shard_map.119.refs_5_.refs_2_), channel_id=1, source_target_pairs={{0,4},{2,6},{4,0},{6,2},{1,5},{3,7},{5,1},{7,3},{8,12},{10,14},{12... | collective-permute-start | bytes 196616 | tf_op jit(solution)/shard_map/ppermute | solution.py:170
  23.3 5.4 %copy-start.5 = (f32[128,128]{1,0:T(8,128)S(1)}, f32[128,128]{1,0:T(8,128)}, u32[]{:S(2)}) copy-start(f32[128,128]{1,0:T(8,128)} %refs_1_.1) | copy-start | bytes 196612
  29.0 7.7 %collective-permute-start.11 = (bf16[256,128]{1,0:T(8,128)(2,1)S(1)}, bf16[256,128]{1,0:T(8,128)(2,1)S(1)}, u32[]{:S(2)}, u32[]{:S(2)}) collective-permute-start(bf16[256,128]{1,0:T(8,128)(2,1)S(1)} %shard_map.121.refs_6_.refs_2_), channel_id=1, source_target_pairs={{0,24},{8,0},{16,8},{24,16},{1,25},{9,1},{17,9},{25,17},{2,26},{10... | collective-permute-start | bytes 196616 | tf_op jit(solution)/shard_map/ppermute | solution.py:170
  31.4 5.3 %collective-permute-start.12 = (bf16[256,128]{1,0:T(8,128)(2,1)S(1)}, bf16[256,128]{1,0:T(8,128)(2,1)S(1)}, u32[]{:S(2)}, u32[]{:S(2)}) collective-permute-start(bf16[256,128]{1,0:T(8,128)(2,1)S(1)} %shard_map.121.refs_6_.refs_2_), channel_id=1, source_target_pairs={{0,16},{8,24},{16,0},{24,8},{1,17},{9,25},{17,1},{25,9},{2,18},{10... | collective-permute-start | bytes 196616 | tf_op jit(solution)/shard_map/ppermute | solution.py:170
  31.9 5.2 %collective-permute-start.13 = (bf16[256,128]{1,0:T(8,128)(2,1)S(1)}, bf16[256,128]{1,0:T(8,128)(2,1)S(1)}, u32[]{:S(2)}, u32[]{:S(2)}) collective-permute-start(bf16[256,128]{1,0:T(8,128)(2,1)S(1)} %shard_map.121.refs_6_.refs_2_), channel_id=1, source_target_pairs={{0,8},{8,16},{16,24},{24,0},{1,9},{9,17},{17,25},{25,1},{2,10},{10... | collective-permute-start | bytes 196616 | tf_op jit(solution)/shard_map/ppermute | solution.py:170
  37.0 1.9 %copy-start.2 = (bf16[1,1,2,128,128]{4,3,2,1,0:T(8,128)(2,1)S(1)}, bf16[1,1,2,128,128]{4,3,2,1,0:T(8,128)(2,1)}, u32[]{:S(2)}) copy-start(bf16[1,1,2,128,128]{4,3,2,1,0:T(8,128)(2,1)} %param.12) | copy-start | bytes 196612
  37.0 1.9 %copy-start.3 = (bf16[128,256]{1,0:T(8,128)(2,1)S(1)}, bf16[128,256]{1,0:T(8,128)(2,1)}, u32[]{:S(2)}) copy-start(bf16[128,256]{1,0:T(8,128)(2,1)} %refs_2_.3) | copy-start | bytes 196612
  37.0 1.9 %copy-start.4 = (bf16[256,128]{1,0:T(8,128)(2,1)S(1)}, bf16[256,128]{1,0:T(8,128)(2,1)}, u32[]{:S(2)}) copy-start(bf16[256,128]{1,0:T(8,128)(2,1)} %refs_3_.1) | copy-start | bytes 196612
  37.5 1.4 %collective-permute-start.14 = (f32[256,128]{1,0:T(8,128)S(1)}, f32[256,128]{1,0:T(8,128)S(1)}, u32[]{:S(2)}, u32[]{:S(2)}) collective-permute-start(f32[256,128]{1,0:T(8,128)S(1)} %get-tuple-element.20), channel_id=1, source_target_pairs={{0,1},{1,0},{2,3},{3,2},{4,5},{5,4},{6,7},{7,6},{8,9},{9,8},{10,11... | collective-permute-start | bytes 393224 | tf_op jit(solution)/shard_map/ppermute | solution.py:170
  38.9 0.7 %copy-start.7 = (f32[128]{0:T(128)S(1)}, f32[128]{0:T(128)}, u32[]{:S(2)}) copy-start(f32[128]{0:T(128)} %param.19) | copy-start | bytes 1540

commit v5 on v4

--- a/solution.py
+++ b/solution.py
@@ -193,9 +193,27 @@
     return turns - ((turns + ROUND) - ROUND)
 
 
-def table_kernel(n_blocks, z_tiles, place_ref, waves_ref, charge_ref, *refs):
-    z_size = len(refs) - 2 - n_blocks
-    columns, copy_ref, table_ref, parts = refs[:z_size], *refs[z_size : z_size + 2], refs[z_size + 2 :]
+def payload_kernel(features_ref, positions_ref, out_ref, held_ref, sems):
+    z_tiles, tile, width = features_ref.shape
+    move = pltpu.make_async_copy(features_ref, out_ref.at[:, pl.ds(0, tile), :], sems.at[0])
+    fetch = pltpu.make_async_copy(positions_ref, held_ref, sems.at[1])
+    fetch.start()
+    move.start()
+    fetch.wait()
+    row = lax.broadcasted_iota(jnp.int32, (POS_ROWS, width), 0)
+    for t in range(z_tiles):
+        rows = jnp.zeros((POS_ROWS, width), jnp.float32)
+        for c in range(3):
+            pos = held_ref[c, t : t + 1, :].astype(jnp.float32)
+            rows = jnp.where(row == c, pos, rows)
+        out_ref[t, tile:, :] = rows.astype(jnp.bfloat16)
+    move.wait()
+
+
+def table_kernel(n_blocks, z_tiles, place_ref, waves_ref, charge_ref, gain_ref, *refs):
+    z_size = len(refs) - 3 - n_blocks
+    refs[-1][...] = gain_ref[...]
+    columns, copy_ref, table_ref, parts = refs[:z_size], *refs[z_size : z_size + 2], refs[z_size + 2 : -1]
     copy_ref[...] = columns[0][...]
     tile = columns[0].shape[2]
     block = waves_ref.shape[1] // n_blocks
@@ -400,11 +418,12 @@
     refs[-1][...] = updated.astype(jnp.bfloat16)
 
 
-def call(kernel, out_shape, *args, scalars=0, after=(), scratch=(), keep=True):
+def call(kernel, out_shape, *args, scalars=0, after=(), scratch=(), keep=True, hold=True):
     in_vmem = pl.BlockSpec(memory_space=pltpu.VMEM)
     anywhere = pl.BlockSpec(memory_space=pl.ANY)
     single = not isinstance(out_shape, (list, tuple))
-    held = [pltpu.with_memory_space_constraint(a, pltpu.VMEM) for a in args[scalars:]]
+    space = pltpu.VMEM if hold else pltpu.HBM
+    held = [pltpu.with_memory_space_constraint(a, space) for a in args[scalars:]]
     n_args, n_after = len(args), len(after)
     if keep:
         out_shape = jax.tree.map(lambda o: pltpu.VMEM(o.shape, o.dtype), out_shape)
@@ -416,7 +435,7 @@
         body,
         out_shape=out_shape,
         in_specs=[pl.BlockSpec(memory_space=pltpu.SMEM)] * scalars
-        + [in_vmem] * len(held)
+        + [in_vmem if hold else pl.BlockSpec(memory_space=pltpu.HBM)] * len(held)
         + [anywhere] * n_after,
         out_specs=in_vmem if single else [in_vmem] * len(out_shape),
         scratch_shapes=list(scratch),
@@ -445,13 +464,13 @@
     atoms = z_tiles * tile
     shape = jax.ShapeDtypeStruct
 
-    pos = jnp.moveaxis(positions.reshape(3, z_tiles, tile), 0, 1).astype(jnp.bfloat16)
-    payload = jnp.concatenate(
-        [
-            features.reshape(z_tiles, tile, width),
-            jnp.pad(pos, ((0, 0), (0, POS_ROWS - 3), (0, 0))),
-        ],
-        axis=1,
+    payload = call(
+        payload_kernel,
+        shape((z_tiles, tile + POS_ROWS, width), jnp.bfloat16),
+        features.reshape(z_tiles, tile, width),
+        positions.reshape(3, z_tiles, tile),
+        hold=False,
+        scratch=[pltpu.VMEM((3, z_tiles, tile), jnp.int32), pltpu.SemaphoreType.DMA((2,))],
     )
     column = [payload] + [shift(payload, "gz", -step) for step in range(1, sizes[2])]
     mine = lax.dynamic_slice_in_dim(wavevectors, place[2] * waves, waves, axis=1)
@@ -462,13 +481,15 @@
     mine = jnp.concatenate([mine * fine, mine * coarse], axis=0)
     mine = jnp.pad(mine, ((0, POS_ROWS - 6), (0, 0))).astype(jnp.bfloat16)
 
-    later, table, *parts = call(
+    later, table, *parts, gain = call(
         functools.partial(table_kernel, n_blocks, z_tiles),
         [shape(payload.shape, payload.dtype), shape((2 * waves, sizes[2] * atoms), jnp.bfloat16)]
-        + [shape((2 * block, width), jnp.bfloat16)] * n_blocks,
+        + [shape((2 * block, width), jnp.bfloat16)] * n_blocks
+        + [shape((1, width), jnp.float32)],
         place,
         mine,
         charge_weight,
+        norm_gain.reshape(1, width),
         *column,
         scalars=1,
     )
@@ -529,7 +550,7 @@
         node_kernel,
         shape((atoms, width), jnp.bfloat16),
         features.reshape(atoms, width),
-        norm_gain.reshape(1, width),
+        gain,
         up_weight,
         down_weight,
         *sums,

time: 40.9 us -> 37.6 us (0.919)
  other arithmetic: 1.73 us -> 0.14 us
  waiting for transfers between devices: 7.1 us -> 6.17 us
  Pallas kernels: 11.2 us -> 12.1 us
  starting transfers between devices: 19.4 us -> 18.6 us
  local copies, waits for them, and re-layouts: 0.97 us -> 0.22 us
    ppermute x15, waiting for transfers between devices: 7.1 us -> 6.17 us  [shift(): lax.ppermute(array, axis, [(i, (i + step) % size) for i in range(size)])]
    pallas_call x8 -> x9, Pallas kernels: 11.2 us -> 12.1 us  [call(): pl.pallas_call(body, out_shape=out_shape, in_specs=[pl.BlockSpec(memory_s...]
    concatenate x1 -> x0, other arithmetic: 0.84 us -> none  [fast_device(): jnp.concatenate([features.reshape(z_tiles, tile, width), jnp.pad(pos, ((0...]
    ppermute x15, starting transfers between devices: 19.4 us -> 18.6 us  [shift(): lax.ppermute(array, axis, [(i, (i + step) % size) for i in range(size)])]
    unnamed x18, local copies, waits for them, and re-layouts: 0.96 us -> 0.21 us
    convert_element_type x1 -> x0, other arithmetic: 0.75 us -> none  [fast_device(): jnp.moveaxis(positions.reshape(3, z_tiles, tile), 0, 1).astype(jnp.bfloat16)]
  transfers between devices with their start and end apart: 15 -> 15, of which waited for: 6 -> 7; matrix products, arithmetic and copies ran while one was open for 0% -> 0% of each run, Pallas kernels for 18% -> 19%
where the time goes in v5:
time: 37.6 us; the launch traced here: 37.4 us
  starting transfers between devices  18.6 us (49%)
  Pallas kernels  12.1 us (32%)
  waiting for transfers between devices  6.17 us (16%)
    ppermute x15, starting transfers between devices, shift(): lax.ppermute(array, axis, [(i, (i + step) % size) for i in range(size)])  18.6 us
    pallas_call x9, Pallas kernels, call(): pl.pallas_call(body, out_shape=out_shape, in_specs=[pl.BlockSpec(memory_s...  12.1 us
    ppermute x15, waiting for transfers between devices, shift(): lax.ppermute(array, axis, [(i, (i + step) % size) for i in range(size)])  6.17 us
  transfers between devices with their start and end apart: 15, of which 7 were waited for; matrix products, arithmetic and copies ran while one was open for 0% of the time, Pallas kernels for 19%

profile of v5, /device:TPU:0, one launch (start us, length us, event | category | flops | bytes accessed | tf_op | source)
XLA Modules:
  0.0 37.4 jit_solution(2557790771489566017)
XLA Ops:
  0.0 0.9 %shard_map.118.refs_4_.refs_0_ = bf16[2,144,128]{2,1,0:T(8,128)(2,1)S(1)} custom-call(bf16[2,128,128]{2,1,0:T(8,128)(2,1)} %bitcast.11, s32[3,2,128]{2,1,0:T(2,128)} %bitcast.17), custom_call_target="tpu_custom_call" | custom-call | tf_op jit(solution)/shard_map/pallas_call | solution.py:434
  1.0 0.6 %collective-permute-start = (bf16[2,144,128]{2,1,0:T(8,128)(2,1)S(1)}, bf16[2,144,128]{2,1,0:T(8,128)(2,1)S(1)}, u32[]{:S(2)}, u32[]{:S(2)}) collective-permute-start(bf16[2,144,128]{2,1,0:T(8,128)(2,1)S(1)} %shard_map.118.refs_4_.refs_0_), channel_id=1, source_target_pairs={{0,1},{1,0},{2,3},{3,2},{4,5},{5,4},{6,7},{7,6},{8,9},{9,8},{10,11... | collective-permute-start | bytes 221192 | tf_op jit(solution)/shard_map/ppermute | solution.py:170
  1.5 0.1 copy-done.8
  1.7 0.1 pad_add_fusion.refs_0_
  1.8 0.6 %collective-permute-done.refs_5_.refs_1_.refs_2_ = bf16[2,144,128]{2,1,0:T(8,128)(2,1)S(1)} collective-permute-done((bf16[2,144,128]{2,1,0:T(8,128)(2,1)S(1)}, bf16[2,144,128]{2,1,0:T(8,128)(2,1)S(1)}, u32[]{:S(2)}, u32[]{:S(2)}) %collective-permute-start) | collective-permute-done | bytes 73760 | tf_op jit(solution)/shard_map/ppermute | solution.py:170
  2.5 2.5 %shard_map.119 = (bf16[2,144,128]{2,1,0:T(8,128)(2,1)S(1)}, bf16[1024,512]{1,0:T(8,128)(2,1)S(1)}, bf16[256,128]{1,0:T(8,128)(2,1)S(1)}, bf16[256,128]{1,0:T(8,1...) custom-call(s32[3]{0:T(128)S(1)} %pad_add_fusion.refs_0_, ...), custom_call_target="tpu_custom_call" | custom-call | tf_op jit(solution)/shard_map/pallas_call | solution.py:434
  5.0 3.1 %collective-permute-start.1 = (bf16[2,144,128]{2,1,0:T(8,128)(2,1)S(1)}, bf16[2,144,128]{2,1,0:T(8,128)(2,1)S(1)}, u32[]{:S(2)}, u32[]{:S(2)}) collective-permute-start(bf16[2,144,128]{2,1,0:T(8,128)(2,1)S(1)} %get-tuple-element.16), channel_id=1, source_target_pairs={{0,2},{2,4},{4,6},{6,0},{1,3},{3,5},{5,7},{7,1},{8,10},{10,12},{12... | collective-permute-start | bytes 221192 | tf_op jit(solution)/shard_map/ppermute | solution.py:170
  8.1 2.1 %collective-permute-start.2 = (bf16[2,144,128]{2,1,0:T(8,128)(2,1)S(1)}, bf16[2,144,128]{2,1,0:T(8,128)(2,1)S(1)}, u32[]{:S(2)}, u32[]{:S(2)}) collective-permute-start(bf16[2,144,128]{2,1,0:T(8,128)(2,1)S(1)} %get-tuple-element.16), channel_id=1, source_target_pairs={{0,6},{2,0},{4,2},{6,4},{1,7},{3,1},{5,3},{7,5},{8,14},{10,8},{12,... | collective-permute-start | bytes 221192 | tf_op jit(solution)/shard_map/ppermute | solution.py:170
  10.2 1.6 %collective-permute-start.5 = (bf16[256,128]{1,0:T(8,128)(2,1)S(1)}, bf16[256,128]{1,0:T(8,128)(2,1)S(1)}, u32[]{:S(2)}, u32[]{:S(2)}) collective-permute-start(bf16[256,128]{1,0:T(8,128)(2,1)S(1)} %get-tuple-element.18), channel_id=1, source_target_pairs={{0,8},{8,16},{16,24},{24,0},{1,9},{9,17},{17,25},{25,1},{2,10},{10... | collective-permute-start | bytes 196616 | tf_op jit(solution)/shard_map/ppermute | solution.py:170
  11.8 1.5 %collective-permute-start.6 = (bf16[256,128]{1,0:T(8,128)(2,1)S(1)}, bf16[256,128]{1,0:T(8,128)(2,1)S(1)}, u32[]{:S(2)}, u32[]{:S(2)}) collective-permute-start(bf16[256,128]{1,0:T(8,128)(2,1)S(1)} %get-tuple-element.19), channel_id=1, source_target_pairs={{0,16},{8,24},{16,0},{24,8},{1,17},{9,25},{17,1},{25,9},{2,18},{10... | collective-permute-start | bytes 196616 | tf_op jit(solution)/shard_map/ppermute | solution.py:170
  13.3 1.4 %collective-permute-start.7 = (bf16[256,128]{1,0:T(8,128)(2,1)S(1)}, bf16[256,128]{1,0:T(8,128)(2,1)S(1)}, u32[]{:S(2)}, u32[]{:S(2)}) collective-permute-start(bf16[256,128]{1,0:T(8,128)(2,1)S(1)} %get-tuple-element.20), channel_id=1, source_target_pairs={{0,24},{8,0},{16,8},{24,16},{1,25},{9,1},{17,9},{25,17},{2,26},{10... | collective-permute-start | bytes 196616 | tf_op jit(solution)/shard_map/ppermute | solution.py:170
  14.8 0.6 %collective-permute-start.4 = (bf16[3,2,144,128]{3,2,1,0:T(8,128)(2,1)S(1)}, bf16[3,2,144,128]{3,2,1,0:T(8,128)(2,1)S(1)}, u32[]{:S(2)}, u32[]{:S(2)}) collective-permute-start(bf16[3,2,144,128]{3,2,1,0:T(8,128)(2,1)S(1)} %pad_maximum_fusion.refs_3_), channel_id=1, source_target_pairs={{0,8},{8,16},{16,24},{24,0},{1,9},{9,17},{17,25},{25,1},{2,10},{10... | collective-permute-start | bytes 663560 | tf_op jit(solution)/shard_map/ppermute | solution.py:170
  15.5 2.3 %collective-permute-start.3 = (bf16[3,2,144,128]{3,2,1,0:T(8,128)(2,1)S(1)}, bf16[3,2,144,128]{3,2,1,0:T(8,128)(2,1)S(1)}, u32[]{:S(2)}, u32[]{:S(2)}) collective-permute-start(bf16[3,2,144,128]{3,2,1,0:T(8,128)(2,1)S(1)} %pad_maximum_fusion.refs_3_), channel_id=1, source_target_pairs={{0,24},{8,0},{16,8},{24,16},{1,25},{9,1},{17,9},{25,17},{2,26},{10... | collective-permute-start | bytes 663560 | tf_op jit(solution)/shard_map/ppermute | solution.py:170
  17.8 0.5 %collective-permute-done.7.refs_3_ = bf16[256,128]{1,0:T(8,128)(2,1)S(1)} collective-permute-done((bf16[256,128]{1,0:T(8,128)(2,1)S(1)}, bf16[256,128]{1,0:T(8,128)(2,1)S(1)}, u32[]{:S(2)}, u32[]{:S(2)}) %collective-permute-start.7) | collective-permute-done | bytes 65568 | tf_op jit(solution)/shard_map/ppermute | solution.py:170
  18.3 1.8 %collective-permute-start.10 = (bf16[256,128]{1,0:T(8,128)(2,1)S(1)}, bf16[256,128]{1,0:T(8,128)(2,1)S(1)}, u32[]{:S(2)}, u32[]{:S(2)}) collective-permute-start(bf16[256,128]{1,0:T(8,128)(2,1)S(1)} %shard_map.120.refs_5_.refs_2_), channel_id=1, source_target_pairs={{0,6},{2,0},{4,2},{6,4},{1,7},{3,1},{5,3},{7,5},{8,14},{10,8},{12,... | collective-permute-start | bytes 196616 | tf_op jit(solution)/shard_map/ppermute | solution.py:170
  20.1 0.3 collective-permute-start.8
  20.4 0.8 %collective-permute-start.9 = (bf16[256,128]{1,0:T(8,128)(2,1)S(1)}, bf16[256,128]{1,0:T(8,128)(2,1)S(1)}, u32[]{:S(2)}, u32[]{:S(2)}) collective-permute-start(bf16[256,128]{1,0:T(8,128)(2,1)S(1)} %shard_map.120.refs_5_.refs_2_), channel_id=1, source_target_pairs={{0,4},{2,6},{4,0},{6,2},{1,5},{3,7},{5,1},{7,3},{8,12},{10,14},{12... | collective-permute-start | bytes 196616 | tf_op jit(solution)/shard_map/ppermute | solution.py:170
  21.3 2.3 %shard_map.121.refs_6_.refs_5_ = f32[4,128,128]{2,1,0:T(8,128)S(1)} custom-call(bf16[2,144,128]{2,1,0:T(8,128)(2,1)S(1)} %shard_map.118.refs_4_.refs_0_, bf16[2,144,128]{2,1,0:T(8,128)(2,1)S(1)} %collective-permute-done.refs_5_.refs_1_.refs_2_, bf16[2,144,128]{2,1,0:T(8,128)(2,1)S(1)} %collective-permute-done.refs_5_.refs_1_.refs_2_, ...), custom_call_target="tpu_custom_call" | custom-call | tf_op jit(solution)/shard_map/pallas_call | solution.py:434
  23.5 0.1 collective-permute-done.10.refs_5_
  23.6 2.7 %collective-permute-done.8.refs_3_ = bf16[256,128]{1,0:T(8,128)(2,1)S(1)} collective-permute-done((bf16[256,128]{1,0:T(8,128)(2,1)S(1)}, bf16[256,128]{1,0:T(8,128)(2,1)S(1)}, u32[]{:S(2)}, u32[]{:S(2)}) %collective-permute-start.8) | collective-permute-done | bytes 65568 | tf_op jit(solution)/shard_map/ppermute | solution.py:170
  26.3 0.7 %collective-permute-done.9.refs_4_ = bf16[256,128]{1,0:T(8,128)(2,1)S(1)} collective-permute-done((bf16[256,128]{1,0:T(8,128)(2,1)S(1)}, bf16[256,128]{1,0:T(8,128)(2,1)S(1)}, u32[]{:S(2)}, u32[]{:S(2)}) %collective-permute-start.9) | collective-permute-done | bytes 65568 | tf_op jit(solution)/shard_map/ppermute | solution.py:170
  27.0 0.3 shard_map.122.refs_6_.refs_2_
  27.3 1.7 %collective-permute-start.11 = (bf16[256,128]{1,0:T(8,128)(2,1)S(1)}, bf16[256,128]{1,0:T(8,128)(2,1)S(1)}, u32[]{:S(2)}, u32[]{:S(2)}) collective-permute-start(bf16[256,128]{1,0:T(8,128)(2,1)S(1)} %shard_map.122.refs_6_.refs_2_), channel_id=1, source_target_pairs={{0,24},{8,0},{16,8},{24,16},{1,25},{9,1},{17,9},{25,17},{2,26},{10... | collective-permute-start | bytes 196616 | tf_op jit(solution)/shard_map/ppermute | solution.py:170
  29.0 0.4 collective-permute-start.12
  29.3 0.3 collective-permute-start.13
  29.6 2.3 %shard_map.123.refs_5_ = f32[4,128,128]{2,1,0:T(8,128)S(1)} custom-call(bf16[2,144,128]{2,1,0:T(8,128)(2,1)S(1)} %shard_map.118.refs_4_.refs_0_, bf16[2,144,128]{2,1,0:T(8,128)(2,1)S(1)} %collective-permute-done.refs_5_.refs_1_.refs_2_, bf16[2,144,128]{2,1,0:T(8,128)(2,1)S(1)} %collective-permute-done.refs_5_.refs_1_.refs_2_, ...), custom_call_target="tpu_custom_call" | custom-call | tf_op jit(solution)/shard_map/pallas_call | solution.py:434
  31.9 2.3 %shard_map.124.refs_1_ = f32[4,128,128]{2,1,0:T(8,128)S(1)} custom-call(bf16[2,144,128]{2,1,0:T(8,128)(2,1)S(1)} %shard_map.118.refs_4_.refs_0_, bf16[2,144,128]{2,1,0:T(8,128)(2,1)S(1)} %collective-permute-done.refs_5_.refs_1_.refs_2_, bf16[2,144,128]{2,1,0:T(8,128)(2,1)S(1)} %collective-permute-done.refs_5_.refs_1_.refs_2_, ...), custom_call_target="tpu_custom_call" | custom-call | tf_op jit(solution)/shard_map/pallas_call | solution.py:434
  34.3 0.2 collective-permute-done.13.refs_5_
  34.5 0.4 %shard_map.125 = (f32[256,128]{1,0:T(8,128)S(1)}, f32[256,128]{1,0:T(8,128)S(1)}) custom-call(bf16[1024,512]{1,0:T(8,128)(2,1)S(1)} %get-tuple-element.15.refs_0_, f32[4,128,128]{2,1,0:T(8,128)S(1)} %shard_map.124.refs_1_, bf16[256,128]{1,0:T(8,128)(2,1)S(1)} %shard_map.122.refs_6_.refs_2_, bf16[256,128]{1,0:T(8,128)(2,1)S(1)} %collective-permute-done.11.refs_3_, ...), custom_call_target="tpu_custom_call" | custom-call | tf_op jit(solution)/shard_map/pallas_call | solution.py:434
  34.9 0.1 collective-permute-start.14
  35.0 1.3 %collective-permute-done.14.refs_5_ = f32[256,128]{1,0:T(8,128)S(1)} collective-permute-done((f32[256,128]{1,0:T(8,128)S(1)}, f32[256,128]{1,0:T(8,128)S(1)}, u32[]{:S(2)}, u32[]{:S(2)}) %collective-permute-start.14) | collective-permute-done | bytes 131104 | tf_op jit(solution)/shard_map/ppermute | solution.py:170
  36.4 1.0 %shard_map.126 = bf16[256,128]{1,0:T(8,128)(2,1)} custom-call(bf16[256,128]{1,0:T(8,128)(2,1)S(1)} %bitcast.12, f32[1,128]{1,0:T(1,128)S(1)} %get-tuple-element.14.refs_1_, bf16[128,256]{1,0:T(8,128)(2,1)S(1)} %copy-done.3, bf16[256,128]{1,0:T(8,128)(2,1)S(1)} %copy-done.4, f32[256,128]{1,0:T(8,128)S(1)} %get-tuple-element.21.refs_4_, ...), custom_call_target="tpu_custom_call" | custom-call | tf_op jit(solution)/shard_map/pallas_call | solution.py:434
  (31 shorter events, 0.2 us)
Async XLA Ops:
  0.0 21.2 %copy-start = (f32[1024,128]{1,0:T(8,128)S(1)}, f32[1024,128]{1,0:T(8,128)}, u32[]{:S(2)}) copy-start(f32[1024,128]{1,0:T(8,128)} %param.17) | copy-start | bytes 1572868
  0.9 0.7 %copy-start.8 = (s32[3,1024]{1,0:T(4,128)S(1)}, s32[3,1024]{1,0:T(4,128)}, u32[]{:S(2)}) copy-start(s32[3,1024]{1,0:T(4,128)} %param.14) | copy-start | bytes 36868
  1.0 1.5 %collective-permute-start = (bf16[2,144,128]{2,1,0:T(8,128)(2,1)S(1)}, bf16[2,144,128]{2,1,0:T(8,128)(2,1)S(1)}, u32[]{:S(2)}, u32[]{:S(2)}) collective-permute-start(bf16[2,144,128]{2,1,0:T(8,128)(2,1)S(1)} %shard_map.118.refs_4_.refs_0_), channel_id=1, source_target_pairs={{0,1},{1,0},{2,3},{3,2},{4,5},{5,4},{6,7},{7,6},{8,9},{9,8},{10,11... | collective-permute-start | bytes 221192 | tf_op jit(solution)/shard_map/ppermute | solution.py:170
  1.7 0.8 %copy-start.6 = (bf16[128,128]{1,0:T(8,128)(2,1)S(1)}, bf16[128,128]{1,0:T(8,128)(2,1)}, u32[]{:S(2)}) copy-start(bf16[128,128]{1,0:T(8,128)(2,1)} %refs_2_.2) | copy-start | bytes 98308
  1.8 0.7 %copy-start.7 = (f32[128]{0:T(128)S(1)}, f32[128]{0:T(128)}, u32[]{:S(2)}) copy-start(f32[128]{0:T(128)} %param.19) | copy-start | bytes 1540
  5.0 9.8 %collective-permute-start.1 = (bf16[2,144,128]{2,1,0:T(8,128)(2,1)S(1)}, bf16[2,144,128]{2,1,0:T(8,128)(2,1)S(1)}, u32[]{:S(2)}, u32[]{:S(2)}) collective-permute-start(bf16[2,144,128]{2,1,0:T(8,128)(2,1)S(1)} %get-tuple-element.16), channel_id=1, source_target_pairs={{0,2},{2,4},{4,6},{6,0},{1,3},{3,5},{5,7},{7,1},{8,10},{10,12},{12... | collective-permute-start | bytes 221192 | tf_op jit(solution)/shard_map/ppermute | solution.py:170
  8.1 6.7 %collective-permute-start.2 = (bf16[2,144,128]{2,1,0:T(8,128)(2,1)S(1)}, bf16[2,144,128]{2,1,0:T(8,128)(2,1)S(1)}, u32[]{:S(2)}, u32[]{:S(2)}) collective-permute-start(bf16[2,144,128]{2,1,0:T(8,128)(2,1)S(1)} %get-tuple-element.16), channel_id=1, source_target_pairs={{0,6},{2,0},{4,2},{6,4},{1,7},{3,1},{5,3},{7,5},{8,14},{10,8},{12,... | collective-permute-start | bytes 221192 | tf_op jit(solution)/shard_map/ppermute | solution.py:170
  10.2 7.6 %collective-permute-start.5 = (bf16[256,128]{1,0:T(8,128)(2,1)S(1)}, bf16[256,128]{1,0:T(8,128)(2,1)S(1)}, u32[]{:S(2)}, u32[]{:S(2)}) collective-permute-start(bf16[256,128]{1,0:T(8,128)(2,1)S(1)} %get-tuple-element.18), channel_id=1, source_target_pairs={{0,8},{8,16},{16,24},{24,0},{1,9},{9,17},{17,25},{25,1},{2,10},{10... | collective-permute-start | bytes 196616 | tf_op jit(solution)/shard_map/ppermute | solution.py:170
  11.8 6.0 %collective-permute-start.6 = (bf16[256,128]{1,0:T(8,128)(2,1)S(1)}, bf16[256,128]{1,0:T(8,128)(2,1)S(1)}, u32[]{:S(2)}, u32[]{:S(2)}) collective-permute-start(bf16[256,128]{1,0:T(8,128)(2,1)S(1)} %get-tuple-element.19), channel_id=1, source_target_pairs={{0,16},{8,24},{16,0},{24,8},{1,17},{9,25},{17,1},{25,9},{2,18},{10... | collective-permute-start | bytes 196616 | tf_op jit(solution)/shard_map/ppermute | solution.py:170
  13.3 5.0 %collective-permute-start.7 = (bf16[256,128]{1,0:T(8,128)(2,1)S(1)}, bf16[256,128]{1,0:T(8,128)(2,1)S(1)}, u32[]{:S(2)}, u32[]{:S(2)}) collective-permute-start(bf16[256,128]{1,0:T(8,128)(2,1)S(1)} %get-tuple-element.20), channel_id=1, source_target_pairs={{0,24},{8,0},{16,8},{24,16},{1,25},{9,1},{17,9},{25,17},{2,26},{10... | collective-permute-start | bytes 196616 | tf_op jit(solution)/shard_map/ppermute | solution.py:170
  14.8 14.8 %collective-permute-start.4 = (bf16[3,2,144,128]{3,2,1,0:T(8,128)(2,1)S(1)}, bf16[3,2,144,128]{3,2,1,0:T(8,128)(2,1)S(1)}, u32[]{:S(2)}, u32[]{:S(2)}) collective-permute-start(bf16[3,2,144,128]{3,2,1,0:T(8,128)(2,1)S(1)} %pad_maximum_fusion.refs_3_), channel_id=1, source_target_pairs={{0,8},{8,16},{16,24},{24,0},{1,9},{9,17},{17,25},{25,1},{2,10},{10... | collective-permute-start | bytes 663560 | tf_op jit(solution)/shard_map/ppermute | solution.py:170
  15.5 16.5 %collective-permute-start.3 = (bf16[3,2,144,128]{3,2,1,0:T(8,128)(2,1)S(1)}, bf16[3,2,144,128]{3,2,1,0:T(8,128)(2,1)S(1)}, u32[]{:S(2)}, u32[]{:S(2)}) collective-permute-start(bf16[3,2,144,128]{3,2,1,0:T(8,128)(2,1)S(1)} %pad_maximum_fusion.refs_3_), channel_id=1, source_target_pairs={{0,24},{8,0},{16,8},{24,16},{1,25},{9,1},{17,9},{25,17},{2,26},{10... | collective-permute-start | bytes 663560 | tf_op jit(solution)/shard_map/ppermute | solution.py:170
  18.3 2.9 %copy-start.1 = (bf16[768,128]{1,0:T(8,128)(2,1)S(1)}, bf16[768,128]{1,0:T(8,128)(2,1)}, u32[]{:S(2)}) copy-start(bf16[768,128]{1,0:T(8,128)(2,1)} %refs_4_.5) | copy-start | bytes 589828
  18.3 5.3 %collective-permute-start.10 = (bf16[256,128]{1,0:T(8,128)(2,1)S(1)}, bf16[256,128]{1,0:T(8,128)(2,1)S(1)}, u32[]{:S(2)}, u32[]{:S(2)}) collective-permute-start(bf16[256,128]{1,0:T(8,128)(2,1)S(1)} %shard_map.120.refs_5_.refs_2_), channel_id=1, source_target_pairs={{0,6},{2,0},{4,2},{6,4},{1,7},{3,1},{5,3},{7,5},{8,14},{10,8},{12,... | collective-permute-start | bytes 196616 | tf_op jit(solution)/shard_map/ppermute | solution.py:170
  20.1 6.2 %collective-permute-start.8 = (bf16[256,128]{1,0:T(8,128)(2,1)S(1)}, bf16[256,128]{1,0:T(8,128)(2,1)S(1)}, u32[]{:S(2)}, u32[]{:S(2)}) collective-permute-start(bf16[256,128]{1,0:T(8,128)(2,1)S(1)} %shard_map.120.refs_5_.refs_2_), channel_id=1, source_target_pairs={{0,2},{2,4},{4,6},{6,0},{1,3},{3,5},{5,7},{7,1},{8,10},{10,12},{12... | collective-permute-start | bytes 196616 | tf_op jit(solution)/shard_map/ppermute | solution.py:170
  20.4 6.6 %collective-permute-start.9 = (bf16[256,128]{1,0:T(8,128)(2,1)S(1)}, bf16[256,128]{1,0:T(8,128)(2,1)S(1)}, u32[]{:S(2)}, u32[]{:S(2)}) collective-permute-start(bf16[256,128]{1,0:T(8,128)(2,1)S(1)} %shard_map.120.refs_5_.refs_2_), channel_id=1, source_target_pairs={{0,4},{2,6},{4,0},{6,2},{1,5},{3,7},{5,1},{7,3},{8,12},{10,14},{12... | collective-permute-start | bytes 196616 | tf_op jit(solution)/shard_map/ppermute | solution.py:170
  21.2 5.8 %copy-start.5 = (f32[128,128]{1,0:T(8,128)S(1)}, f32[128,128]{1,0:T(8,128)}, u32[]{:S(2)}) copy-start(f32[128,128]{1,0:T(8,128)} %refs_1_.1) | copy-start | bytes 196612
  27.3 7.0 %collective-permute-start.11 = (bf16[256,128]{1,0:T(8,128)(2,1)S(1)}, bf16[256,128]{1,0:T(8,128)(2,1)S(1)}, u32[]{:S(2)}, u32[]{:S(2)}) collective-permute-start(bf16[256,128]{1,0:T(8,128)(2,1)S(1)} %shard_map.122.refs_6_.refs_2_), channel_id=1, source_target_pairs={{0,24},{8,0},{16,8},{24,16},{1,25},{9,1},{17,9},{25,17},{2,26},{10... | collective-permute-start | bytes 196616 | tf_op jit(solution)/shard_map/ppermute | solution.py:170
  29.0 5.3 %collective-permute-start.12 = (bf16[256,128]{1,0:T(8,128)(2,1)S(1)}, bf16[256,128]{1,0:T(8,128)(2,1)S(1)}, u32[]{:S(2)}, u32[]{:S(2)}) collective-permute-start(bf16[256,128]{1,0:T(8,128)(2,1)S(1)} %shard_map.122.refs_6_.refs_2_), channel_id=1, source_target_pairs={{0,16},{8,24},{16,0},{24,8},{1,17},{9,25},{17,1},{25,9},{2,18},{10... | collective-permute-start | bytes 196616 | tf_op jit(solution)/shard_map/ppermute | solution.py:170
  29.3 5.2 %collective-permute-start.13 = (bf16[256,128]{1,0:T(8,128)(2,1)S(1)}, bf16[256,128]{1,0:T(8,128)(2,1)S(1)}, u32[]{:S(2)}, u32[]{:S(2)}) collective-permute-start(bf16[256,128]{1,0:T(8,128)(2,1)S(1)} %shard_map.122.refs_6_.refs_2_), channel_id=1, source_target_pairs={{0,8},{8,16},{16,24},{24,0},{1,9},{9,17},{17,25},{25,1},{2,10},{10... | collective-permute-start | bytes 196616 | tf_op jit(solution)/shard_map/ppermute | solution.py:170
  34.5 1.9 %copy-start.2 = (bf16[1,1,2,128,128]{4,3,2,1,0:T(8,128)(2,1)S(1)}, bf16[1,1,2,128,128]{4,3,2,1,0:T(8,128)(2,1)}, u32[]{:S(2)}) copy-start(bf16[1,1,2,128,128]{4,3,2,1,0:T(8,128)(2,1)} %param.12) | copy-start | bytes 196612
  34.5 1.9 %copy-start.3 = (bf16[128,256]{1,0:T(8,128)(2,1)S(1)}, bf16[128,256]{1,0:T(8,128)(2,1)}, u32[]{:S(2)}) copy-start(bf16[128,256]{1,0:T(8,128)(2,1)} %refs_2_.3) | copy-start | bytes 196612
  34.5 1.9 %copy-start.4 = (bf16[256,128]{1,0:T(8,128)(2,1)S(1)}, bf16[256,128]{1,0:T(8,128)(2,1)}, u32[]{:S(2)}) copy-start(bf16[256,128]{1,0:T(8,128)(2,1)} %refs_3_.1) | copy-start | bytes 196612
  34.9 1.4 %collective-permute-start.14 = (f32[256,128]{1,0:T(8,128)S(1)}, f32[256,128]{1,0:T(8,128)S(1)}, u32[]{:S(2)}, u32[]{:S(2)}) collective-permute-start(f32[256,128]{1,0:T(8,128)S(1)} %get-tuple-element.22), channel_id=1, source_target_pairs={{0,1},{1,0},{2,3},{3,2},{4,5},{5,4},{6,7},{7,6},{8,9},{9,8},{10,11... | collective-permute-start | bytes 393224 | tf_op jit(solution)/shard_map/ppermute | solution.py:170
